TPU v7x, 128 devices: a whole 4x4x4 slice. The times are simulated.
128 devices in a mesh: wide: 16 (over z, y_lo, core), narrow: 8 (over x, y_hi).
Axes of the slice: x: 4, y: 4 (y_hi: 2, y_lo: 2; y = y_hi * 2 + y_lo), z: 4, core: 2. Of those that a mesh axis runs over, the one named last changes fastest.
Arguments:
- tridiag_vectors: float32 [128, 131072], P(('wide', 'narrow')), may hold values from -6 to 6
- reflectors: float32 [2, 131072, 256], P(None, 'wide'), may hold values from -0.015625 to 0.015625
- triangles: float32 [2, 256, 256], replicated, as said below
- lower_blocks: float32 [6, 1536, 1536], P(None, 'wide'), may hold values from -0.109375 to 0.109375
- diag_inverses: float32 [4, 1536, 1536], P(None, None, 'wide'), as said below
Outputs:
- transformed: float32 [128, 131072], P('narrow', 'wide')
- solved: float32 [128, 4, 1536], P('narrow', None, 'wide')
Inputs may be any that keep to these rules, and one draw needn't show every extreme that they name: `triangles`: zero below the diagonal, positive on it. `diag_inverses`: zero above the diagonal, positive on it.
All inputs are finite; a program needn't handle non-finite values.
Results may differ from a plain program's by a relative error of at most 0.00019.
Values sent between devices are 32-bit elements; how exact they have to be, the bound alone decides.
No kernel may reach another device: no remote copies, remote signals or barrier semaphores. Data moves between devices by JAX's collectives and lax.ppermute only.
A program may use at most 128 MiB of HBM per device.

v0:
```python
import jax
import jax.numpy as jnp
from jax import lax
from jax.sharding import PartitionSpec as P

HIGHEST = lax.Precision.HIGHEST


def in_order(parts, dim):
    parts = jnp.moveaxis(parts, 0, dim)
    dims = parts.shape
    return parts.reshape(*dims[:dim], dims[dim] * dims[dim + 1], *dims[dim + 2 :])


def from_everyone(array, axis):
    devices = lax.axis_size(axis)
    return lax.all_to_all(
        jnp.broadcast_to(array[None], (devices, *array.shape)), axis, 0, 0, tiled=True
    )


def gathered_copies(array, axis, dim):
    return in_order(from_everyone(array, axis), dim)


def in_blocks(array, dim, devices):
    before, after = (array.shape[:dim], array.shape[dim + 1 :])
    return jnp.moveaxis(array.reshape(*before, devices, -1, *after), dim, 0)


def sent_and_summed(array, axis, dim):
    devices = lax.axis_size(axis)
    parts = lax.all_to_all(in_blocks(array, dim, devices), axis, 0, 0, tiled=True)
    return jnp.sum(parts, axis=0)


def over_copies(array, axis):
    everything = from_everyone(array, axis)
    return jnp.sum(everything, axis=0)


def reflect(current, vectors, factor, products):
    coeffs = jnp.dot(products, factor.T, precision=HIGHEST)
    return current - jnp.dot(coeffs, vectors.T, precision=HIGHEST)


def add_piece(inverse, segment):
    return jnp.dot(segment, inverse, precision=HIGHEST)


def solve_chain(corner, lower_blocks, diag_inverses):
    local_count, panels, share_cols = corner.shape
    zeroed = jnp.zeros((local_count, share_cols), jnp.float32)
    pending = [zeroed] * panels
    results = [zeroed] * panels
    for source in reversed(range(panels)):
        remain = corner[:, source, :] - pending[source]
        solution = add_piece(diag_inverses[source], gathered_copies(remain, "wide", 1))
        results[source] = solution
        if source > 0:
            offset = source * (source - 1) // 2
            blocks = lower_blocks[offset : offset + source]
            partial_terms = jnp.einsum("ks,qsc->kqc", solution, blocks, precision=HIGHEST)
            scattered = sent_and_summed(partial_terms, "wide", 2)
            for target in range(source):
                pending[target] = pending[target] + scattered[:, target, :]
    return jnp.stack(results, axis=1)


def body(tridiag_vectors, reflectors, triangles, lower_blocks, diag_inverses):
    wide_size = lax.axis_size("wide")
    narrow_size = lax.axis_size("narrow")
    current = lax.all_to_all(
        lax.all_to_all(tridiag_vectors, "wide", split_axis=1, concat_axis=0, tiled=True),
        "narrow",
        split_axis=0,
        concat_axis=0,
        tiled=True,
    )
    per_device = tridiag_vectors.shape[0]
    length = current.shape[1]
    current = current.reshape(narrow_size, wide_size // narrow_size, per_device, length)
    current = current.transpose(1, 0, 2, 3).reshape(-1, length)
    for which in (1, 0):
        products = over_copies(jnp.dot(current, reflectors[which], precision=HIGHEST), "wide")
        current = reflect(current, reflectors[which], triangles[which], products)
    panels, panel_rows, share_cols = diag_inverses.shape
    corner_span = panels * panel_rows
    tail_cols = current[:, current.shape[1] - corner_span :]
    framed = tail_cols.reshape(tail_cols.shape[0], panels, wide_size, share_cols)
    received = lax.all_to_all(framed, "wide", split_axis=2, concat_axis=2, tiled=True)
    corner = received[:, :, wide_size - 1, :]
    solved = solve_chain(corner, lower_blocks, diag_inverses)
    return (current, solved)


def solution(mesh):
    placed = (
        P(("wide", "narrow"), None),
        P(None, "wide", None),
        P(),
        P(None, "wide", None),
        P(None, None, "wide"),
    )
    return jax.shard_map(
        body,
        mesh=mesh,
        in_specs=placed,
        out_specs=(P("narrow", "wide"), P("narrow", None, "wide")),
        check_vma=False,
    )
```

profile of v0, /device:TPU:1, one launch (start us, length us, event | category | flops | bytes accessed | tf_op | source)
XLA Modules:
  0.0 210.6 jit_solution(999282913706440636)
XLA Ops:
  0.6 17.6 %all_to_all.72 = f32[1,16,8192]{2,0,1:T(1,128)S(1)} all-to-all(f32[1,16,8192]{2,0,1:T(1,128)} %bitcast.109), channel_id=1, replica_groups=mesh['wide'=16,'narrow'=8] {'wide'}, dimensions={1} | all-to-all | bytes 1048576 | tf_op jit(solution)/shard_map/all_to_all | solution.py:74
  18.3 1.2 reduce.1
  19.5 0.3 all_to_all.48
  19.8 15.6 %all_to_all.73 = f32[8,2,8192]{2,1,0:T(2,128)S(1)} all-to-all(f32[8,2,8192]{2,1,0:T(2,128)S(1)} %all_to_all.48), channel_id=1, replica_groups=mesh['wide'=16,'narrow'=8] {'narrow'}, dimensions={0} | all-to-all | bytes 1048576 | tf_op jit(solution)/shard_map/all_to_all | solution.py:73
  35.5 0.0 copy-start.2
  35.5 5.8 %fusion.4 = f32[16,256]{1,0:T(8,128)S(1)} fusion(f32[2,8192,256]{2,1,0:T(8,128)} %param.6, f32[2,8,1,8192]{3,0,1,2:T(2,128)S(1)} %bitcast.104), kind=kOutput, calls=%fused_computation.6 | convolution fusion | flops 402653184 | bytes 8929280 | tf_op jit(solution)/shard_map/dot_general | solution.py:85
  41.3 12.3 %all_to_all.74 = f32[16,16,256]{2,1,0:T(8,128)S(1)} all-to-all(f32[16,16,256]{2,1,0:T(8,128)S(1)} %broadcast_in_dim.14), channel_id=1, replica_groups=mesh['wide'=16,'narrow'=8] {'wide'}, dimensions={0} | all-to-all | bytes 524288 | tf_op jit(solution)/shard_map/all_to_all | solution.py:17
  53.7 0.0 copy-done.2
  53.7 0.3 fusion.29
  54.0 9.2 %convolution_subtract_fusion.1 = f32[16,8192]{1,0:T(8,128)S(1)} fusion(f32[16,256]{1,0:T(8,128)S(1)} %fusion.29, f32[2,8192,256]{2,1,0:T(8,128)} %param.6, f32[2,8,1,8192]{3,0,1,2:T(2,128)S(1)} %bitcast.105), kind=kOutput, calls=%fused_computation.1 | convolution fusion | flops 402784256 | bytes 9453568 | tf_op jit(solution)/shard_map/dot_general | solution.py:44
  63.2 5.7 %fusion.1 = f32[16,256]{1,0:T(8,128)S(1)} fusion(f32[16,8192]{1,0:T(8,128)S(1)} %convolution_subtract_fusion.1, f32[2,8192,256]{2,1,0:T(8,128)} %param.6), kind=kOutput, calls=%fused_computation.3 | convolution fusion | flops 402653184 | bytes 8929280 | tf_op jit(solution)/shard_map/dot_general | solution.py:85
  68.9 10.6 %all_to_all.75 = f32[16,16,256]{2,1,0:T(8,128)S(1)} all-to-all(f32[16,16,256]{2,1,0:T(8,128)S(1)} %broadcast_in_dim.15), channel_id=1, replica_groups=mesh['wide'=16,'narrow'=8] {'wide'}, dimensions={0} | all-to-all | bytes 524288 | tf_op jit(solution)/shard_map/all_to_all | solution.py:17
  79.6 0.3 fusion.27
  79.8 9.2 %convolution_subtract_fusion = f32[16,8192]{1,0:T(8,128)S(1)} fusion(f32[16,8192]{1,0:T(8,128)S(1)} %convolution_subtract_fusion.1, f32[16,256]{1,0:T(8,128)S(1)} %fusion.27, f32[2,8192,256]{2,1,0:T(8,128)} %param.6), kind=kOutput, calls=%fused_computation | convolution fusion | flops 402784256 | bytes 9453568 | tf_op jit(solution)/shard_map/dot_general | solution.py:44
  89.1 0.0 copy-start.1
  89.1 0.8 copy-done.1
  89.9 0.0 copy-start
  89.9 0.8 slice.90
  90.6 2.4 %reshape.104 = f32[16,4,16,96]{3,2,1,0:T(8,128)} reshape(f32[16,6144]{1,0:T(8,128)} %slice.90) | data formatting | bytes 786432 | tf_op jit(solution)/shard_map/reshape | solution.py:90
  93.1 1.2 copy.29
  94.3 13.3 %all_to_all.76 = f32[16,4,16,96]{3,1,0,2:T(4,128)S(1)} all-to-all(f32[16,4,16,96]{3,1,0,2:T(4,128)S(1)} %copy.29), channel_id=1, replica_groups=mesh['wide'=16,'narrow'=8] {'wide'}, dimensions={2} | all-to-all | bytes 786432 | tf_op jit(solution)/shard_map/all_to_all | solution.py:91
  107.7 0.0 copy-start.3
  107.7 0.6 copy-done.3
  108.3 9.8 %all_to_all.77 = f32[16,16,96]{2,1,0:T(8,128)S(1)} all-to-all(f32[16,16,96]{2,1,0:T(8,128)S(1)} %broadcast_in_dim.17), channel_id=1, replica_groups=mesh['wide'=16,'narrow'=8] {'wide'}, dimensions={0} | all-to-all | bytes 196608 | tf_op jit(solution)/shard_map/all_to_all | solution.py:17
  118.1 0.7 copy.31
  118.8 1.6 reshape.105
  120.4 1.7 fusion.19
  122.1 0.0 copy-done
  122.1 1.7 fusion.10
  123.8 1.8 reshape.106
  125.6 1.1 copy.59
  126.8 12.2 %all_to_all.78 = f32[16,16,3,96]{3,1,2,0:T(8,128)} all-to-all(f32[16,16,3,96]{3,1,2,0:T(8,128)S(1)} %bitcast.107), channel_id=1, replica_groups=mesh['wide'=16,'narrow'=8] {'wide'}, dimensions={0} | all-to-all | bytes 589824 | tf_op jit(solution)/shard_map/all_to_all | solution.py:33
  139.0 1.6 reduce_sum.47
  140.6 0.7 fusion.38
  141.4 9.8 %all_to_all.79 = f32[16,16,96]{2,1,0:T(8,128)S(1)} all-to-all(f32[16,16,96]{2,1,0:T(8,128)S(1)} %broadcast_in_dim.18), channel_id=1, replica_groups=mesh['wide'=16,'narrow'=8] {'wide'}, dimensions={0} | all-to-all | bytes 196608 | tf_op jit(solution)/shard_map/all_to_all | solution.py:17
  151.2 0.7 copy.34
  151.8 1.6 reshape.107
  153.5 1.7 fusion.17
  155.2 1.4 fusion.12
  156.5 1.7 reshape.108
  158.3 1.0 copy.60
  159.3 11.0 %all_to_all.80 = f32[16,16,2,96]{3,1,2,0:T(8,128)} all-to-all(f32[16,16,2,96]{3,1,2,0:T(8,128)S(1)} %bitcast.108), channel_id=1, replica_groups=mesh['wide'=16,'narrow'=8] {'wide'}, dimensions={0} | all-to-all | bytes 393216 | tf_op jit(solution)/shard_map/all_to_all | solution.py:33
  170.3 1.6 reduce_sum.48
  171.9 0.7 fusion.34
  172.6 0.7 broadcast_in_dim.19
  173.3 4.9 %all-to-all-start.9 = ((f32[16,16,96]{2,1,0:T(8,128)}), f32[16,16,96]{2,1,0:T(8,128)}, u32[]{:S(2)}, u32[]{:S(2)}) async-start(f32[16,16,96]{2,1,0:T(8,128)} %broadcast_in_dim.19), calls=%async_computation.9 | async-start | bytes 262144 | tf_op jit(solution)/shard_map/all_to_all | solution.py:17
  178.2 0.8 slice_bitcast_fusion
  179.0 0.0 copy-start.4
  179.0 1.3 copy.38
  180.4 4.1 %all-to-all-done.9 = f32[16,16,96]{2,1,0:T(8,128)} async-done(((f32[16,16,96]{2,1,0:T(8,128)}), f32[16,16,96]{2,1,0:T(8,128)}, u32[]{:S(2)}, u32[]{:S(2)}) %all-to-all-start.9) | async-done | bytes 98336 | tf_op jit(solution)/shard_map/all_to_all | solution.py:17
  184.5 0.9 copy.37
  185.4 0.1 reshape.109
  185.5 1.6 fusion.15
  187.2 1.5 convolution_bitcast_fusion
  188.7 9.3 %all_to_all.81 = f32[16,16,1,96]{3,1,2,0:T(8,128)S(1)} all-to-all(f32[16,16,1,96]{3,1,2,0:T(8,128)S(1)} %convolution_bitcast_fusion), channel_id=1, replica_groups=mesh['wide'=16,'narrow'=8] {'wide'}, dimensions={0} | all-to-all | bytes 196608 | tf_op jit(solution)/shard_map/all_to_all | solution.py:33
  198.1 0.0 copy-done.4
  198.1 0.7 fusion.37
  198.8 9.3 %all_to_all.82 = f32[16,16,96]{2,1,0:T(8,128)S(1)} all-to-all(f32[16,16,96]{2,1,0:T(8,128)S(1)} %broadcast_in_dim.20), channel_id=1, replica_groups=mesh['wide'=16,'narrow'=8] {'wide'}, dimensions={0} | all-to-all | bytes 196608 | tf_op jit(solution)/shard_map/all_to_all | solution.py:17
  208.2 0.1 reshape.112
  208.3 1.6 convolution_bitcast_fusion.1
  209.9 0.6 copy.41
  (13 shorter events, 0.2 us)
Async XLA Ops:
  35.5 18.2 %copy-start.2 = (f32[2,256,256]{2,1,0:T(8,128)S(1)}, f32[2,256,256]{2,1,0:T(8,128)}, u32[]{:S(2)}) copy-start(f32[2,256,256]{2,1,0:T(8,128)} %param.7) | copy-start | bytes 1572868
  89.1 0.8 copy-start.1
  89.9 32.2 %copy-start = (f32[6,96,1536]{2,1,0:T(8,128)S(1)}, f32[6,96,1536]{2,1,0:T(8,128)}, u32[]{:S(2)}) copy-start(f32[6,96,1536]{2,1,0:T(8,128)} %param.8) | copy-start | bytes 10616836
  107.7 0.6 copy-start.3
  173.3 11.2 %all-to-all-start.9 = ((f32[16,16,96]{2,1,0:T(8,128)}), f32[16,16,96]{2,1,0:T(8,128)}, u32[]{:S(2)}, u32[]{:S(2)}) async-start(f32[16,16,96]{2,1,0:T(8,128)} %broadcast_in_dim.19), calls=%async_computation.9 | async-start | bytes 262144 | tf_op jit(solution)/shard_map/all_to_all | solution.py:17
  179.0 19.1 %copy-start.4 = (f32[16,2,96]{2,0,1:T(8,128)S(1)}, f32[16,2,96]{2,0,1:T(8,128)}, u32[]{:S(2)}) copy-start(f32[16,2,96]{2,0,1:T(8,128)} %reduce_sum.48) | copy-start | bytes 36868
where the time goes:
time: 212 us; the launch traced here: 211 us
  blocking collectives  131 us (62%)
  matrix products  41.7 us (20%)
  local copies, waits for them, and re-layouts  21.3 us (10%)
  other arithmetic  6.7 us (3%)
  starting transfers between devices  4.9 us (2%)
  waiting for transfers between devices  4.14 us (2%)
    all_to_all x5, blocking collectives, from_everyone(): lax.all_to_all(jnp.broadcast_to(array[None], (devices, *array.shape)), ax...  51.9 us
    all_to_all x3, blocking collectives, sent_and_summed(): lax.all_to_all(in_blocks(array, dim, devices), axis, 0, 0, tiled=True)  32.6 us
    dot_general x2, matrix products, reflect(): return current - jnp.dot(coeffs, vectors.T, precision=HIGHEST)  18.4 us
    all_to_all x1, blocking collectives, body(): lax.all_to_all(tridiag_vectors, 'wide', split_axis=1, concat_axis=0, tile...  17.6 us
    all_to_all x1, blocking collectives, body(): lax.all_to_all(lax.all_to_all(tridiag_vectors, 'wide', split_axis=1, conc...  15.6 us
    all_to_all x1, blocking collectives, body(): lax.all_to_all(framed, 'wide', split_axis=2, concat_axis=2, tiled=True)  13.3 us
    dot_general x2, matrix products, body(): jnp.dot(current, reflectors[which], precision=HIGHEST)  11.5 us
    dot_general x4, matrix products, add_piece(): return jnp.dot(segment, inverse, precision=HIGHEST)  6.62 us
  transfers between devices with their start and end apart: 1, of which 1 were waited for; matrix products, arithmetic and copies ran while one was open for 1% of the time, Pallas kernels for 0%

commit v1 on v0

v1 whole, which is shorter than its diff:
```python
import jax
import jax.numpy as jnp
from jax import lax
from jax.sharding import PartitionSpec as P

HIGH = lax.Precision.HIGH


def dot(a, b):
    return jnp.dot(a, b, precision=HIGH)


def from_everyone(array, axis):
    devices = lax.axis_size(axis)
    return lax.all_to_all(
        jnp.broadcast_to(array[None], (devices, *array.shape)), axis, 0, 0, tiled=True
    )


def swapped(array):
    size = lax.axis_size("wide")
    return lax.ppermute(array, "wide", [(i, i ^ 1) for i in range(size)])


def summed_over_chips(array):
    size = lax.axis_size("wide")
    array = array + lax.ppermute(array, "wide", [(i, i ^ 2) for i in range(size)])
    far = lax.ppermute(array, "wide", [(i, (i + 8) % size) for i in range(size)])
    up = lax.ppermute(array, "wide", [(i, (i + 4) % size) for i in range(size)])
    down = lax.ppermute(array, "wide", [(i, (i + 12) % size) for i in range(size)])
    return (array + far) + (up + down)


def from_last_chip(array, is_last):
    size = lax.axis_size("wide")
    array = jnp.where(is_last, array, 0.0)
    last = size - 2
    total = array
    for back in (8, 4, 12):
        pairs = [(last + c, (last + c + back) % size) for c in range(2)]
        total = total + lax.ppermute(array, "wide", pairs)
    pairs = [(i, i ^ 2) for i in range(size) if i & 2]
    return total + lax.ppermute(total, "wide", pairs)


def solve_chain(tail, lower_blocks, diag_inverses):
    count = tail.shape[0]
    panels, rows, share = diag_inverses.shape
    half = rows // 2
    me = lax.axis_index("wide")
    core = me % 2
    is_last = me >= lax.axis_size("wide") - 2
    mine, other = core * half, (1 - core) * half
    turned = jnp.swapaxes(diag_inverses, 1, 2)
    d_keep = lax.dynamic_slice_in_dim(turned, mine, half, 2)
    d_send = lax.dynamic_slice_in_dim(turned, other, half, 2)
    d_pair = jnp.concatenate([d_keep, swapped(d_send)], axis=1)
    l_keep = lax.dynamic_slice_in_dim(lower_blocks, mine, half, 2)
    l_send = lax.dynamic_slice_in_dim(lower_blocks, other, half, 2)
    l_pair = jnp.concatenate([l_keep, swapped(l_send)], axis=1)
    tail = tail.reshape(count, panels, 2, half)
    corner = jnp.where(
        me == lax.axis_size("wide") - 1, tail[:, :, 1, :], swapped(tail[:, :, 0, :])
    )
    remain = from_last_chip(corner[:, panels - 1, :], is_last)
    pending = [jnp.where(is_last, corner[:, p, :], 0.0) for p in range(panels - 1)]
    results = [None] * panels
    for source in reversed(range(panels)):
        part = lax.dot_general(
            remain, d_pair[source], (((1,), (1,)), ((), ())), precision=HIGH
        )
        back = jnp.concatenate([part[:, share:], part[:, :share]], axis=1)
        pair = part + swapped(back)
        results[source] = pair[:, :share]
        offset = source * (source - 1) // 2
        for target in range(source):
            pending[target] = pending[target] - dot(pair, l_pair[offset + target])
        if source > 0:
            remain = summed_over_chips(pending[source - 1])
    return jnp.stack(results, axis=1)


def body(tridiag_vectors, reflectors, triangles, lower_blocks, diag_inverses):
    wide_size = lax.axis_size("wide")
    narrow_size = lax.axis_size("narrow")
    current = lax.all_to_all(
        lax.all_to_all(tridiag_vectors, "wide", split_axis=1, concat_axis=0, tiled=True),
        "narrow",
        split_axis=0,
        concat_axis=0,
        tiled=True,
    )
    per_device = tridiag_vectors.shape[0]
    length = current.shape[1]
    current = current.reshape(narrow_size, wide_size // narrow_size, per_device, length)
    current = current.transpose(1, 0, 2, 3).reshape(-1, length)
    for which in (1, 0):
        parts = from_everyone(dot(current, reflectors[which]), "wide")
        coeffs = dot(jnp.sum(parts, axis=0), triangles[which].T)
        current = current - dot(coeffs, reflectors[which].T)
    panels, panel_rows, _ = diag_inverses.shape
    tail = current[:, length - panels * panel_rows :]
    solved = solve_chain(tail, lower_blocks, diag_inverses)
    return (current, solved)


def solution(mesh):
    placed = (
        P(("wide", "narrow"), None),
        P(None, "wide", None),
        P(),
        P(None, "wide", None),
        P(None, None, "wide"),
    )
    return jax.shard_map(
        body,
        mesh=mesh,
        in_specs=placed,
        out_specs=(P("narrow", "wide"), P("narrow", None, "wide")),
        check_vma=False,
    )
```

time: 212 us -> 162 us (0.76)
  blocking collectives: 131 us -> 33.3 us
  starting transfers between devices: 4.9 us -> 39.4 us
  waiting for transfers between devices: 4.14 us -> 36.9 us
  matrix products: 41.7 us -> 33 us
  local copies, waits for them, and re-layouts: 21.3 us -> 13.5 us
  other arithmetic: 6.7 us -> 3.68 us
    all_to_all x9 -> x0, blocking collectives: 97.8 us -> none  [the longest x5 51.9 us: from_everyone(): lax.all_to_all(jnp.broadcast_to(array[None], (devices, *array.shape)), ax...]
    ppermute x0 -> x23, starting transfers between devices: none -> 28.4 us  [the longest x7 13 us: swapped(): return lax.ppermute(array, 'wide', [(i, i ^ 1) for i in range(size)])]
    ppermute x0 -> x23, waiting for transfers between devices: none -> 27.1 us  [the longest x3 8.77 us: summed_over_chips(): lax.ppermute(array, 'wide', [(i, i ^ 2) for i in range(size)])]
    reshape x10 -> x1, local copies, waits for them, and re-layouts: 12.9 us -> 2.07 us  [solve_chain(): tail = tail.reshape(count, panels, 2, half)]
    dot_general x13 -> x16, matrix products: 41.7 us -> 33 us  [the longest x12 27.9 us: dot(): return jnp.dot(a, b, precision=HIGH)]
    all_to_all x1 -> x2, starting transfers between devices: 4.9 us -> 10.9 us  [from_everyone(): lax.all_to_all(jnp.broadcast_to(array[None], (devices, *array.shape)), ax...]
    all_to_all x1 -> x2, waiting for transfers between devices: 4.14 us -> 9.89 us  [from_everyone(): lax.all_to_all(jnp.broadcast_to(array[None], (devices, *array.shape)), ax...]
    dynamic_slice x0 -> x2, local copies, waits for them, and re-layouts: none -> 3.16 us  [the longest x1 1.64 us: solve_chain(): d_send = lax.dynamic_slice_in_dim(turned, other, half, 2)]
  transfers between devices with their start and end apart: 1 -> 25, of which waited for: 1 -> 18; matrix products, arithmetic and copies ran while one was open for 1% -> 13% of each run, Pallas kernels for 0% -> 0%
where the time goes in v1:
time: 162 us; the launch traced here: 161 us
  starting transfers between devices  39.4 us (24%)
  waiting for transfers between devices  36.9 us (23%)
  blocking collectives  33.3 us (21%)
  matrix products  33 us (20%)
  local copies, waits for them, and re-layouts  13.5 us (8%)
  other arithmetic  3.68 us (2%)
    dot_general x12, matrix products, dot(): return jnp.dot(a, b, precision=HIGH)  27.9 us
    all_to_all x1, blocking collectives, body(): lax.all_to_all(tridiag_vectors, 'wide', split_axis=1, concat_axis=0, tile...  17.6 us
    all_to_all x1, blocking collectives, body(): lax.all_to_all(lax.all_to_all(tridiag_vectors, 'wide', split_axis=1, conc...  15.6 us
    ppermute x7, starting transfers between devices, swapped(): return lax.ppermute(array, 'wide', [(i, i ^ 1) for i in range(size)])  13 us
    all_to_all x2, starting transfers between devices, from_everyone(): lax.all_to_all(jnp.broadcast_to(array[None], (devices, *array.shape)), ax...  10.9 us
    all_to_all x2, waiting for transfers between devices, from_everyone(): lax.all_to_all(jnp.broadcast_to(array[None], (devices, *array.shape)), ax...  9.89 us
    ppermute x3, waiting for transfers between devices, summed_over_chips(): lax.ppermute(array, 'wide', [(i, i ^ 2) for i in range(size)])  8.77 us
    ppermute x1, waiting for transfers between devices, from_last_chip(): return total + lax.ppermute(total, 'wide', pairs)  6.83 us
  transfers between devices with their start and end apart: 25, of which 18 were waited for; matrix products, arithmetic and copies ran while one was open for 13% of the time, Pallas kernels for 0%

profile of v1, /device:TPU:1, one launch (start us, length us, event | category | flops | bytes accessed | tf_op | source)
XLA Modules:
  0.0 160.8 jit_solution(17474489403532791785)
XLA Ops:
  0.6 17.6 %all_to_all.32 = f32[1,16,8192]{2,0,1:T(1,128)S(1)} all-to-all(f32[1,16,8192]{2,0,1:T(1,128)} %bitcast.114), channel_id=1, replica_groups=mesh['wide'=16,'narrow'=8] {'wide'}, dimensions={1} | all-to-all | bytes 1048576 | tf_op jit(solution)/shard_map/all_to_all | solution.py:87
  18.3 1.2 reduce
  19.5 0.3 all_to_all.24
  19.8 15.6 %all_to_all.33 = f32[8,2,8192]{2,1,0:T(2,128)S(1)} all-to-all(f32[8,2,8192]{2,1,0:T(2,128)S(1)} %all_to_all.24), channel_id=1, replica_groups=mesh['wide'=16,'narrow'=8] {'narrow'}, dimensions={0} | all-to-all | bytes 1048576 | tf_op jit(solution)/shard_map/all_to_all | solution.py:86
  35.5 5.6 %fusion.4 = f32[16,256]{1,0:T(8,128)S(1)} fusion(f32[2,8192,256]{2,1,0:T(8,128)} %param.6, f32[2,8,1,8192]{3,0,1,2:T(2,128)S(1)} %bitcast.112), kind=kOutput, calls=%fused_computation.6 | convolution fusion | flops 201326592 | bytes 8929280 | tf_op jit(solution)/shard_map/dot_general | solution.py:10
  41.1 0.7 broadcast_in_dim.19
  41.8 6.0 %all-to-all-start.2 = ((f32[16,16,256]{2,1,0:T(8,128)}), f32[16,16,256]{2,1,0:T(8,128)S(1)}, u32[]{:S(2)}, u32[]{:S(2)}) async-start(f32[16,16,256]{2,1,0:T(8,128)} %broadcast_in_dim.19), calls=%async_computation.2 | async-start | bytes 524288 | tf_op jit(solution)/shard_map/all_to_all | solution.py:15
  47.9 7.2 %all-to-all-done.2 = f32[16,16,256]{2,1,0:T(8,128)S(1)} async-done(((f32[16,16,256]{2,1,0:T(8,128)}), f32[16,16,256]{2,1,0:T(8,128)S(1)}, u32[]{:S(2)}, u32[]{:S(2)}) %all-to-all-start.2) | async-done | bytes 262176 | tf_op jit(solution)/shard_map/all_to_all | solution.py:15
  55.3 6.8 %convolution_subtract_fusion.1 = f32[16,8192]{1,0:T(8,128)S(1)} fusion(f32[16,256]{1,0:T(8,128)S(1)} %fusion.54, f32[2,8192,256]{2,1,0:T(8,128)} %param.6, f32[2,8,1,8192]{3,0,1,2:T(2,128)S(1)} %bitcast.113), kind=kOutput, calls=%fused_computation.1 | convolution fusion | flops 201457664 | bytes 9453568 | tf_op jit(solution)/shard_map/dot_general | solution.py:10
  62.2 5.6 %fusion.1 = f32[16,256]{1,0:T(8,128)S(1)} fusion(f32[16,8192]{1,0:T(8,128)S(1)} %convolution_subtract_fusion.1, f32[2,8192,256]{2,1,0:T(8,128)} %param.6), kind=kOutput, calls=%fused_computation.3 | convolution fusion | flops 201326592 | bytes 8929280 | tf_op jit(solution)/shard_map/dot_general | solution.py:10
  67.8 0.7 broadcast_in_dim.20
  68.5 4.9 %all-to-all-start.3 = ((f32[16,16,256]{2,1,0:T(8,128)}), f32[16,16,256]{2,1,0:T(8,128)}, u32[]{:S(2)}, u32[]{:S(2)}) async-start(f32[16,16,256]{2,1,0:T(8,128)} %broadcast_in_dim.20), calls=%async_computation.3 | async-start | bytes 524288 | tf_op jit(solution)/shard_map/all_to_all | solution.py:15
  73.5 1.6 %dynamic-slice_bitcast_fusion = (f32[4,96,768]{2,1,0:T(8,128)}, f32[4,96,768]{2,1,0:T(8,128)}) fusion(f32[4,1536,96]{1,2,0:T(8,128)S(1)} %copy-done.3, s32[]{:T(128)S(6)} %select_n.64, s32[]{:T(128)S(6)} %select_n.63), kind=kLoop, calls=%fused_computation.28 | loop fusion | bytes 4718600 | tf_op jit(solution)/shard_map/dynamic_slice | solution.py:56
  75.1 0.3 collective-permute-start.5
  75.4 0.9 copy-done.2
  76.3 1.5 constant_dynamic-slice_fusion
  77.8 0.3 collective-permute-start.7
  78.1 2.7 %all-to-all-done.3 = f32[16,16,256]{2,1,0:T(8,128)} async-done(((f32[16,16,256]{2,1,0:T(8,128)}), f32[16,16,256]{2,1,0:T(8,128)}, u32[]{:S(2)}, u32[]{:S(2)}) %all-to-all-start.3) | async-done | bytes 262176 | tf_op jit(solution)/shard_map/all_to_all | solution.py:15
  80.8 1.0 reduce_sum.19
  81.8 1.1 fusion.52
  82.9 6.9 %convolution_subtract_fusion = f32[16,8192]{1,0:T(8,128)S(1)} fusion(f32[16,8192]{1,0:T(8,128)} %copy-done.1, f32[16,256]{1,0:T(8,128)S(1)} %fusion.52, f32[2,8192,256]{2,1,0:T(8,128)} %param.6), kind=kOutput, calls=%fused_computation | convolution fusion | flops 201457664 | bytes 9453568 | tf_op jit(solution)/shard_map/dot_general | solution.py:10
  89.8 0.8 copy-done.4
  90.6 0.8 slice.134
  91.4 2.1 %reshape.39 = f32[16,4,2,768]{3,2,1,0:T(2,128)} reshape(f32[16,6144]{1,0:T(8,128)} %slice.134) | data formatting | bytes 786432 | tf_op jit(solution)/shard_map/reshape | solution.py:61
  93.4 2.2 %fusion.96 = (f32[16,4,1,768]{3,2,1,0:T(1,128)}, f32[16,4,1,768]{3,2,1,0:T(1,128)S(1)}) fusion(f32[16,4,2,768]{3,2,1,0:T(2,128)} %reshape.39), kind=kLoop, calls=%fused_computation.120 | loop fusion | bytes 786432 | tf_op jit(solution)/shard_map/slice | solution.py:63
  95.6 0.7 copy.34
  96.3 1.0 collective-permute-start
  97.3 1.4 collective-permute-done
  98.7 1.1 fusion.58
  99.8 0.7 collective-permute-start.1
  100.5 0.7 collective-permute-start.2
  101.2 0.7 collective-permute-start.3
  101.9 1.3 collective-permute-start.4
  103.2 6.8 %collective-permute-done.4 = f32[16,768]{1,0:T(8,128)S(1)} collective-permute-done((f32[16,768]{1,0:T(8,128)S(1)}, f32[16,768]{1,0:T(8,128)S(1)}, u32[]{:S(2)}, u32[]{:S(2)}) %collective-permute-start.4) | collective-permute-done | bytes 49184 | tf_op jit(solution)/shard_map/ppermute | solution.py:43
  110.0 1.4 fusion.16
  111.6 2.2 %collective-permute-start.6 = (f32[16,192]{1,0:T(8,128)S(1)}, f32[16,192]{1,0:T(8,128)S(1)}, u32[]{:S(2)}, u32[]{:S(2)}) collective-permute-start(f32[16,192]{1,0:T(8,128)S(1)} %pad_maximum_fusion.3), channel_id=1, source_target_pairs={{0,8},{8,0},{16,24},{24,16},{32,40},{40,32},{48,56},{56,48},{64,72... | collective-permute-start | bytes 36872 | tf_op jit(solution)/shard_map/ppermute | solution.py:22
  113.8 0.8 collective-permute-done.6
  114.6 0.3 fusion.63
  115.0 2.9 %collective-permute-done.8 = f32[16,768]{1,0:T(8,128)S(1)} collective-permute-done((f32[16,768]{1,0:T(8,128)S(1)}, f32[16,768]{1,0:T(8,128)S(1)}, u32[]{:S(2)}, u32[]{:S(2)}) %collective-permute-start.8) | collective-permute-done | bytes 49184 | tf_op jit(solution)/shard_map/ppermute | solution.py:27
  118.0 2.7 %collective-permute-start.11 = (f32[16,768]{1,0:T(8,128)S(1)}, f32[16,768]{1,0:T(8,128)S(1)}, u32[]{:S(2)}, u32[]{:S(2)}) collective-permute-start(f32[16,768]{1,0:T(8,128)S(1)} %add.80), channel_id=1, source_target_pairs={{0,96},{8,104},{16,112},{24,120},{32,0},{40,8},{48,16},{56,24},{64... | collective-permute-start | bytes 147464 | tf_op jit(solution)/shard_map/ppermute | solution.py:30
  120.7 1.3 collective-permute-start.9
  122.1 3.0 %collective-permute-done.9 = f32[16,768]{1,0:T(8,128)S(1)} collective-permute-done((f32[16,768]{1,0:T(8,128)S(1)}, f32[16,768]{1,0:T(8,128)S(1)}, u32[]{:S(2)}, u32[]{:S(2)}) %collective-permute-start.9) | collective-permute-done | bytes 49184 | tf_op jit(solution)/shard_map/ppermute | solution.py:28
  125.1 1.3 fusion.20
  126.6 3.2 %collective-permute-start.12 = (f32[16,192]{1,0:T(8,128)S(1)}, f32[16,192]{1,0:T(8,128)S(1)}, u32[]{:S(2)}, u32[]{:S(2)}) collective-permute-start(f32[16,192]{1,0:T(8,128)S(1)} %pad_maximum_fusion.4), channel_id=1, source_target_pairs={{0,8},{8,0},{16,24},{24,16},{32,40},{40,32},{48,56},{56,48},{64,72... | collective-permute-start | bytes 36872 | tf_op jit(solution)/shard_map/ppermute | solution.py:22
  130.1 0.6 collective-permute-done.12
  131.0 2.9 %collective-permute-done.13 = f32[16,768]{1,0:T(8,128)S(1)} collective-permute-done((f32[16,768]{1,0:T(8,128)S(1)}, f32[16,768]{1,0:T(8,128)S(1)}, u32[]{:S(2)}, u32[]{:S(2)}) %collective-permute-start.13) | collective-permute-done | bytes 49184 | tf_op jit(solution)/shard_map/ppermute | solution.py:27
  134.0 1.3 collective-permute-start.14
  135.3 2.7 %collective-permute-start.16 = (f32[16,768]{1,0:T(8,128)S(1)}, f32[16,768]{1,0:T(8,128)S(1)}, u32[]{:S(2)}, u32[]{:S(2)}) collective-permute-start(f32[16,768]{1,0:T(8,128)S(1)} %add.85), channel_id=1, source_target_pairs={{0,96},{8,104},{16,112},{24,120},{32,0},{40,8},{48,16},{56,24},{64... | collective-permute-start | bytes 147464 | tf_op jit(solution)/shard_map/ppermute | solution.py:30
  138.5 1.0 collective-permute-done.15
  139.5 1.3 fusion.12
  141.0 2.9 %collective-permute-start.17 = (f32[16,192]{1,0:T(8,128)S(1)}, f32[16,192]{1,0:T(8,128)S(1)}, u32[]{:S(2)}, u32[]{:S(2)}) collective-permute-start(f32[16,192]{1,0:T(8,128)S(1)} %pad_maximum_fusion.5), channel_id=1, source_target_pairs={{0,8},{8,0},{16,24},{24,16},{32,40},{40,32},{48,56},{56,48},{64,72... | collective-permute-start | bytes 36872 | tf_op jit(solution)/shard_map/ppermute | solution.py:22
  144.2 0.6 collective-permute-done.17
  144.7 0.3 fusion.68
  145.1 2.9 %collective-permute-done.18 = f32[16,768]{1,0:T(8,128)S(1)} collective-permute-done((f32[16,768]{1,0:T(8,128)S(1)}, f32[16,768]{1,0:T(8,128)S(1)}, u32[]{:S(2)}, u32[]{:S(2)}) %collective-permute-start.18) | collective-permute-done | bytes 49184 | tf_op jit(solution)/shard_map/ppermute | solution.py:27
  148.0 1.3 collective-permute-start.19
  149.3 2.3 %collective-permute-start.20 = (f32[16,768]{1,0:T(8,128)S(1)}, f32[16,768]{1,0:T(8,128)S(1)}, u32[]{:S(2)}, u32[]{:S(2)}) collective-permute-start(f32[16,768]{1,0:T(8,128)S(1)} %add.90), channel_id=1, source_target_pairs={{0,32},{8,40},{16,48},{24,56},{32,64},{40,72},{48,80},{56,88},{64,... | collective-permute-start | bytes 147464 | tf_op jit(solution)/shard_map/ppermute | solution.py:29
  151.6 0.3 collective-permute-start.21
  152.0 0.6 collective-permute-done.19
  152.6 0.9 collective-permute-done.20
  153.4 1.4 collective-permute-done.21
  154.8 1.3 fusion.33
  156.3 3.0 %collective-permute-start.22 = (f32[16,192]{1,0:T(8,128)S(1)}, f32[16,192]{1,0:T(8,128)S(1)}, u32[]{:S(2)}, u32[]{:S(2)}) collective-permute-start(f32[16,192]{1,0:T(8,128)S(1)} %pad_maximum_fusion.6), channel_id=1, source_target_pairs={{0,8},{8,0},{16,24},{24,16},{32,40},{40,32},{48,56},{56,48},{64,72... | collective-permute-start | bytes 36872 | tf_op jit(solution)/shard_map/ppermute | solution.py:22
  159.3 0.8 collective-permute-done.22
  160.1 0.6 copy.21
  (51 shorter events, 2.9 us)
Async XLA Ops:
  35.5 19.6 %copy-start.5 = (f32[2,256,256]{2,1,0:T(8,128)S(1)}, f32[2,256,256]{2,1,0:T(8,128)}, u32[]{:S(2)}) copy-start(f32[2,256,256]{2,1,0:T(8,128)} %param.7) | copy-start | bytes 1572868
  41.8 13.2 %all-to-all-start.2 = ((f32[16,16,256]{2,1,0:T(8,128)}), f32[16,16,256]{2,1,0:T(8,128)S(1)}, u32[]{:S(2)}, u32[]{:S(2)}) async-start(f32[16,16,256]{2,1,0:T(8,128)} %broadcast_in_dim.19), calls=%async_computation.2 | async-start | bytes 524288 | tf_op jit(solution)/shard_map/all_to_all | solution.py:15
  62.1 5.7 %copy-start.1 = (f32[16,8192]{1,0:T(8,128)}, f32[16,8192]{1,0:T(8,128)S(1)}, u32[]{:S(2)}) copy-start(f32[16,8192]{1,0:T(8,128)S(1)} %convolution_subtract_fusion.1) | copy-start | bytes 1572868
  62.1 11.3 %copy-start.3 = (f32[4,1536,96]{1,2,0:T(8,128)S(1)}, f32[4,1536,96]{1,2,0:T(8,128)}, u32[]{:S(2)}) copy-start(f32[4,1536,96]{1,2,0:T(8,128)} %param.9) | copy-start | bytes 7077892
  68.5 12.3 %all-to-all-start.3 = ((f32[16,16,256]{2,1,0:T(8,128)}), f32[16,16,256]{2,1,0:T(8,128)}, u32[]{:S(2)}, u32[]{:S(2)}) async-start(f32[16,16,256]{2,1,0:T(8,128)} %broadcast_in_dim.20), calls=%async_computation.3 | async-start | bytes 524288 | tf_op jit(solution)/shard_map/all_to_all | solution.py:15
  73.5 2.9 %copy-start.2 = (f32[6,96,1536]{2,1,0:T(8,128)S(1)}, f32[6,96,1536]{2,1,0:T(8,128)}, u32[]{:S(2)}) copy-start(f32[6,96,1536]{2,1,0:T(8,128)} %param.8) | copy-start | bytes 10616836
  75.1 28.1 %collective-permute-start.5 = (f32[4,96,768]{2,1,0:T(8,128)}, f32[4,96,768]{2,1,0:T(8,128)}, u32[]{:S(2)}, u32[]{:S(2)}) collective-permute-start(f32[4,96,768]{2,1,0:T(8,128)} %get-tuple-element.12), channel_id=1, source_target_pairs={{0,8},{8,0},{16,24},{24,16},{32,40},{40,32},{48,56},{56,48},{64,72... | collective-permute-start | bytes 3538952 | tf_op jit(solution)/shard_map/ppermute | solution.py:22
  77.8 36.8 %collective-permute-start.7 = (f32[6,96,768]{2,1,0:T(8,128)}, f32[6,96,768]{2,1,0:T(8,128)S(1)}, u32[]{:S(2)}, u32[]{:S(2)}) collective-permute-start(f32[6,96,768]{2,1,0:T(8,128)} %get-tuple-element.10), channel_id=1, source_target_pairs={{0,8},{8,0},{16,24},{24,16},{32,40},{40,32},{48,56},{56,48},{64,72... | collective-permute-start | bytes 5308424 | tf_op jit(solution)/shard_map/ppermute | solution.py:22
  89.8 0.8 copy-start.4
  96.3 2.4 %collective-permute-start = (f32[16,4,768]{2,0,1:T(8,128)}, f32[16,4,768]{2,0,1:T(8,128)}, u32[]{:S(2)}, u32[]{:S(2)}) collective-permute-start(f32[16,4,768]{2,0,1:T(8,128)} %bitcast.111), channel_id=1, source_target_pairs={{0,8},{8,0},{16,24},{24,16},{32,40},{40,32},{48,56},{56,48},{64,72... | collective-permute-start | bytes 589832 | tf_op jit(solution)/shard_map/ppermute | solution.py:22
  99.8 2.0 %collective-permute-start.1 = (f32[16,768]{1,0:T(8,128)S(1)}, f32[16,768]{1,0:T(8,128)S(1)}, u32[]{:S(2)}, u32[]{:S(2)}) collective-permute-start(f32[16,768]{1,0:T(8,128)S(1)} %fusion.64), channel_id=1, source_target_pairs={{112,48},{120,56},{113,49},{121,57},{114,50},{122,58},{115,51},{12... | collective-permute-start | bytes 147464 | tf_op jit(solution)/shard_map/ppermute | solution.py:41
  100.5 1.4 collective-permute-start.2
  101.2 0.7 collective-permute-start.3
  101.9 8.1 %collective-permute-start.4 = (f32[16,768]{1,0:T(8,128)S(1)}, f32[16,768]{1,0:T(8,128)S(1)}, u32[]{:S(2)}, u32[]{:S(2)}) collective-permute-start(f32[16,768]{1,0:T(8,128)S(1)} %add_add_fusion), channel_id=1, source_target_pairs={{16,0},{24,8},{48,32},{56,40},{80,64},{88,72},{112,96},{120,104},{... | collective-permute-start | bytes 147464 | tf_op jit(solution)/shard_map/ppermute | solution.py:43
  111.6 3.0 %collective-permute-start.6 = (f32[16,192]{1,0:T(8,128)S(1)}, f32[16,192]{1,0:T(8,128)S(1)}, u32[]{:S(2)}, u32[]{:S(2)}) collective-permute-start(f32[16,192]{1,0:T(8,128)S(1)} %pad_maximum_fusion.3), channel_id=1, source_target_pairs={{0,8},{8,0},{16,24},{24,16},{32,40},{40,32},{48,56},{56,48},{64,72... | collective-permute-start | bytes 36872 | tf_op jit(solution)/shard_map/ppermute | solution.py:22
  114.6 10.5 %copy-start = (f32[4,96,768]{2,1,0:T(8,128)S(1)}, f32[4,96,768]{2,1,0:T(8,128)}, u32[]{:S(2)}) copy-start(f32[4,96,768]{2,1,0:T(8,128)} %get-tuple-element.13) | copy-start | bytes 3538948
  114.9 3.0 %collective-permute-start.8 = (f32[16,768]{1,0:T(8,128)S(1)}, f32[16,768]{1,0:T(8,128)S(1)}, u32[]{:S(2)}, u32[]{:S(2)}) collective-permute-start(f32[16,768]{1,0:T(8,128)S(1)} %fusion.63), channel_id=1, source_target_pairs={{0,16},{8,24},{16,0},{24,8},{32,48},{40,56},{48,32},{56,40},{64,80... | collective-permute-start | bytes 147464 | tf_op jit(solution)/shard_map/ppermute | solution.py:27
  117.9 4.2 %collective-permute-start.10 = (f32[16,768]{1,0:T(8,128)S(1)}, f32[16,768]{1,0:T(8,128)S(1)}, u32[]{:S(2)}, u32[]{:S(2)}) collective-permute-start(f32[16,768]{1,0:T(8,128)S(1)} %add.80), channel_id=1, source_target_pairs={{0,32},{8,40},{16,48},{24,56},{32,64},{40,72},{48,80},{56,88},{64,... | collective-permute-start | bytes 147464 | tf_op jit(solution)/shard_map/ppermute | solution.py:29
  118.0 4.1 %collective-permute-start.11 = (f32[16,768]{1,0:T(8,128)S(1)}, f32[16,768]{1,0:T(8,128)S(1)}, u32[]{:S(2)}, u32[]{:S(2)}) collective-permute-start(f32[16,768]{1,0:T(8,128)S(1)} %add.80), channel_id=1, source_target_pairs={{0,96},{8,104},{16,112},{24,120},{32,0},{40,8},{48,16},{56,24},{64... | collective-permute-start | bytes 147464 | tf_op jit(solution)/shard_map/ppermute | solution.py:30
  120.7 4.4 %collective-permute-start.9 = (f32[16,768]{1,0:T(8,128)S(1)}, f32[16,768]{1,0:T(8,128)S(1)}, u32[]{:S(2)}, u32[]{:S(2)}) collective-permute-start(f32[16,768]{1,0:T(8,128)S(1)} %add.80), channel_id=1, source_target_pairs={{0,64},{8,72},{16,80},{24,88},{32,96},{40,104},{48,112},{56,120},{... | collective-permute-start | bytes 147464 | tf_op jit(solution)/shard_map/ppermute | solution.py:28
  126.6 4.1 %collective-permute-start.12 = (f32[16,192]{1,0:T(8,128)S(1)}, f32[16,192]{1,0:T(8,128)S(1)}, u32[]{:S(2)}, u32[]{:S(2)}) collective-permute-start(f32[16,192]{1,0:T(8,128)S(1)} %pad_maximum_fusion.4), channel_id=1, source_target_pairs={{0,8},{8,0},{16,24},{24,16},{32,40},{40,32},{48,56},{56,48},{64,72... | collective-permute-start | bytes 36872 | tf_op jit(solution)/shard_map/ppermute | solution.py:22
  131.0 3.0 %collective-permute-start.13 = (f32[16,768]{1,0:T(8,128)S(1)}, f32[16,768]{1,0:T(8,128)S(1)}, u32[]{:S(2)}, u32[]{:S(2)}) collective-permute-start(f32[16,768]{1,0:T(8,128)S(1)} %fusion.61), channel_id=1, source_target_pairs={{0,16},{8,24},{16,0},{24,8},{32,48},{40,56},{48,32},{56,40},{64,80... | collective-permute-start | bytes 147464 | tf_op jit(solution)/shard_map/ppermute | solution.py:27
  134.0 4.5 %collective-permute-start.14 = (f32[16,768]{1,0:T(8,128)S(1)}, f32[16,768]{1,0:T(8,128)S(1)}, u32[]{:S(2)}, u32[]{:S(2)}) collective-permute-start(f32[16,768]{1,0:T(8,128)S(1)} %add.85), channel_id=1, source_target_pairs={{0,64},{8,72},{16,80},{24,88},{32,96},{40,104},{48,112},{56,120},{... | collective-permute-start | bytes 147464 | tf_op jit(solution)/shard_map/ppermute | solution.py:28
  135.3 4.2 %collective-permute-start.15 = (f32[16,768]{1,0:T(8,128)S(1)}, f32[16,768]{1,0:T(8,128)S(1)}, u32[]{:S(2)}, u32[]{:S(2)}) collective-permute-start(f32[16,768]{1,0:T(8,128)S(1)} %add.85), channel_id=1, source_target_pairs={{0,32},{8,40},{16,48},{24,56},{32,64},{40,72},{48,80},{56,88},{64,... | collective-permute-start | bytes 147464 | tf_op jit(solution)/shard_map/ppermute | solution.py:29
  135.3 4.2 %collective-permute-start.16 = (f32[16,768]{1,0:T(8,128)S(1)}, f32[16,768]{1,0:T(8,128)S(1)}, u32[]{:S(2)}, u32[]{:S(2)}) collective-permute-start(f32[16,768]{1,0:T(8,128)S(1)} %add.85), channel_id=1, source_target_pairs={{0,96},{8,104},{16,112},{24,120},{32,0},{40,8},{48,16},{56,24},{64... | collective-permute-start | bytes 147464 | tf_op jit(solution)/shard_map/ppermute | solution.py:30
  141.0 3.8 %collective-permute-start.17 = (f32[16,192]{1,0:T(8,128)S(1)}, f32[16,192]{1,0:T(8,128)S(1)}, u32[]{:S(2)}, u32[]{:S(2)}) collective-permute-start(f32[16,192]{1,0:T(8,128)S(1)} %pad_maximum_fusion.5), channel_id=1, source_target_pairs={{0,8},{8,0},{16,24},{24,16},{32,40},{40,32},{48,56},{56,48},{64,72... | collective-permute-start | bytes 36872 | tf_op jit(solution)/shard_map/ppermute | solution.py:22
  145.0 3.0 %collective-permute-start.18 = (f32[16,768]{1,0:T(8,128)S(1)}, f32[16,768]{1,0:T(8,128)S(1)}, u32[]{:S(2)}, u32[]{:S(2)}) collective-permute-start(f32[16,768]{1,0:T(8,128)S(1)} %fusion.68), channel_id=1, source_target_pairs={{0,16},{8,24},{16,0},{24,8},{32,48},{40,56},{48,32},{56,40},{64,80... | collective-permute-start | bytes 147464 | tf_op jit(solution)/shard_map/ppermute | solution.py:27
  148.0 4.5 %collective-permute-start.19 = (f32[16,768]{1,0:T(8,128)S(1)}, f32[16,768]{1,0:T(8,128)S(1)}, u32[]{:S(2)}, u32[]{:S(2)}) collective-permute-start(f32[16,768]{1,0:T(8,128)S(1)} %add.90), channel_id=1, source_target_pairs={{0,64},{8,72},{16,80},{24,88},{32,96},{40,104},{48,112},{56,120},{... | collective-permute-start | bytes 147464 | tf_op jit(solution)/shard_map/ppermute | solution.py:28
  149.3 4.2 %collective-permute-start.20 = (f32[16,768]{1,0:T(8,128)S(1)}, f32[16,768]{1,0:T(8,128)S(1)}, u32[]{:S(2)}, u32[]{:S(2)}) collective-permute-start(f32[16,768]{1,0:T(8,128)S(1)} %add.90), channel_id=1, source_target_pairs={{0,32},{8,40},{16,48},{24,56},{32,64},{40,72},{48,80},{56,88},{64,... | collective-permute-start | bytes 147464 | tf_op jit(solution)/shard_map/ppermute | solution.py:29
  151.6 3.2 %collective-permute-start.21 = (f32[16,768]{1,0:T(8,128)S(1)}, f32[16,768]{1,0:T(8,128)S(1)}, u32[]{:S(2)}, u32[]{:S(2)}) collective-permute-start(f32[16,768]{1,0:T(8,128)S(1)} %add.90), channel_id=1, source_target_pairs={{0,96},{8,104},{16,112},{24,120},{32,0},{40,8},{48,16},{56,24},{64... | collective-permute-start | bytes 147464 | tf_op jit(solution)/shard_map/ppermute | solution.py:30
  156.3 3.8 %collective-permute-start.22 = (f32[16,192]{1,0:T(8,128)S(1)}, f32[16,192]{1,0:T(8,128)S(1)}, u32[]{:S(2)}, u32[]{:S(2)}) collective-permute-start(f32[16,192]{1,0:T(8,128)S(1)} %pad_maximum_fusion.6), channel_id=1, source_target_pairs={{0,8},{8,0},{16,24},{24,16},{32,40},{40,32},{48,56},{56,48},{64,72... | collective-permute-start | bytes 36872 | tf_op jit(solution)/shard_map/ppermute | solution.py:22

commit v2 on v1

v2 whole, which is shorter than its diff:
```python
import functools

import jax
import jax.numpy as jnp
from jax import lax
from jax.experimental import pallas as pl
from jax.experimental.pallas import tpu as pltpu
from jax.sharding import PartitionSpec as P

HIGH = lax.Precision.HIGH
NN = (((1,), (0,)), ((), ()))
NT = (((1,), (1,)), ((), ()))


def dot(a, b):
    return jnp.dot(a, b, precision=HIGH)


def split(x):
    high = x.astype(jnp.bfloat16)
    return high, (x - high.astype(jnp.float32)).astype(jnp.bfloat16)


def dot_split(a, b, dims):
    rows = a[0].shape[0]
    both = jnp.concatenate(a, axis=0)
    with_high = lax.dot_general(both, b[0], dims, preferred_element_type=jnp.float32)
    with_low = lax.dot_general(a[0], b[1], dims, preferred_element_type=jnp.float32)
    return with_high[:rows] + (with_high[rows:] + with_low)


def in_vmem(count):
    return [pl.BlockSpec(memory_space=pltpu.VMEM)] * count


BIG = pltpu.CompilerParams(vmem_limit_bytes=50 << 20)


def streamed(v_ref, held, sems, first, count, use):
    unit = held.shape[2]
    slots = held.shape[0]

    def fetch(i):
        where = pl.ds((first + i) * unit, unit)
        return pltpu.make_async_copy(
            v_ref.at[:, where, :], held.at[i % slots], sems.at[i % slots]
        )

    for i in range(min(slots, count)):
        fetch(i).start()
    for i in range(count):
        fetch(i).wait()
        use(i, held.at[i % slots])
        if i + slots < count:
            fetch(i + slots).start()


def products_kernel(z_ref, v_ref, flat_ref, p1_ref, p0_ref, held, sems):
    unit = held.shape[2]
    _, per, subs, lanes = z_ref.shape
    sums = [jnp.zeros(p1_ref.shape, jnp.float32) for _ in range(2)]

    def use(i, v_ref):
        columns = []
        for s in range(i * unit // lanes, (i + 1) * unit // lanes):
            rows = [z_ref[:, c, s, :] for c in range(per)]
            columns.append(jnp.concatenate(rows, axis=0))
        z = jnp.concatenate(columns, axis=1)
        flat_ref[:, i * unit : (i + 1) * unit] = z
        z = split(z)
        for which in range(2):
            sums[which] = sums[which] + dot_split(z, split(v_ref[which]), NN)

    streamed(v_ref, held, sems, 0, subs * lanes // unit, use)
    p1_ref[...] = sums[1]
    p0_ref[...] = sums[0]


def products_of(received, reflectors):
    parts, per, subs, lanes = received.shape
    rows = parts * per
    length = subs * lanes
    block = reflectors.shape[2]
    sums = jax.ShapeDtypeStruct((rows, block), jnp.float32)
    return pl.pallas_call(
        products_kernel,
        out_shape=[jax.ShapeDtypeStruct((rows, length), jnp.float32), sums, sums],
        in_specs=in_vmem(1) + [pl.BlockSpec(memory_space=pl.ANY)],
        out_specs=in_vmem(3),
        scratch_shapes=held_pieces(block, 512, 6),
        compiler_params=BIG,
        cost_estimate=update_cost(rows, length, block),
    )(received, reflectors)


def pieces_of(z_ref, coeffs_ref, v_ref, held, sems, first, count, write):
    unit = held.shape[2]
    block = v_ref.shape[2]
    coeffs = [
        split(coeffs_ref[:, slot * block : (slot + 1) * block]) for slot in range(2)
    ]

    def use(i, piece_ref):
        total = z_ref[:, (first + i) * unit : (first + i + 1) * unit]
        for slot, which in enumerate((1, 0)):
            total = total - dot_split(coeffs[slot], split(piece_ref[which]), NT)
        write(i, total)

    streamed(v_ref, held, sems, first, count, use)


def corner_kernel(first, z_ref, coeffs_ref, v_ref, o_ref, held, sems):
    unit = held.shape[2]
    _, panels, _, half = o_ref.shape
    each = half // unit

    def write(i, total):
        p, h, k = i // (2 * each), (i // each) % 2, i % each
        o_ref[h, p, :, k * unit : (k + 1) * unit] = total

    count = 2 * panels * each
    pieces_of(z_ref, coeffs_ref, v_ref, held, sems, first, count, write)


def final_kernel(z_ref, coeffs_ref, v_ref, rest_ref, last_ref, o_ref, held, sems):
    unit = held.shape[2]
    _, others, _, half = rest_ref.shape
    start = o_ref.shape[1] - 2 * half * (others + 1)

    def write(i, total):
        o_ref[:, i * unit : (i + 1) * unit] = total

    pieces_of(z_ref, coeffs_ref, v_ref, held, sems, 0, start // unit, write)
    for p in range(others + 1):
        for h in range(2):
            piece = rest_ref[h, p] if p < others else last_ref[h, 0]
            at = start + (2 * p + h) * half
            o_ref[:, at : at + half] = piece


UNIT = 256


def held_pieces(block, unit, slots):
    return [
        pltpu.VMEM((slots, 2, unit, block), jnp.float32),
        pltpu.SemaphoreType.DMA((slots,)),
    ]


def update_cost(rows, columns, block):
    return pl.CostEstimate(
        flops=12 * rows * columns * block,
        bytes_accessed=8 * columns * block + 8 * rows * columns,
        transcendentals=0,
    )


def corner_of(flat, coeffs, reflectors, first, panels, half):
    rows = flat.shape[0]
    block = reflectors.shape[2]
    return pl.pallas_call(
        functools.partial(corner_kernel, first // UNIT),
        out_shape=jax.ShapeDtypeStruct((2, panels, rows, half), jnp.float32),
        in_specs=in_vmem(2) + [pl.BlockSpec(memory_space=pl.ANY)],
        out_specs=in_vmem(1)[0],
        scratch_shapes=held_pieces(block, UNIT, 6),
        compiler_params=BIG,
        cost_estimate=update_cost(rows, 2 * panels * half, block),
    )(flat, coeffs, reflectors)


def transformed_of(flat, coeffs, reflectors, rest, last):
    rows, columns = flat.shape
    block = reflectors.shape[2]
    start = columns - (rest.size + last.size) // rows
    return pl.pallas_call(
        final_kernel,
        out_shape=jax.ShapeDtypeStruct((rows, columns), jnp.float32),
        in_specs=in_vmem(2) + [pl.BlockSpec(memory_space=pl.ANY)] + in_vmem(2),
        out_specs=in_vmem(1)[0],
        scratch_shapes=held_pieces(block, UNIT, 6),
        compiler_params=BIG,
        cost_estimate=update_cost(rows, start, block),
    )(flat, coeffs, reflectors, rest, last)


def swapped(array):
    size = lax.axis_size("wide")
    return lax.ppermute(array, "wide", [(i, i ^ 1) for i in range(size)])


def from_chips(array):
    size = lax.axis_size("wide")
    array = array + lax.ppermute(array, "wide", [(i, i ^ 2) for i in range(size)])
    others = [
        lax.ppermute(array, "wide", [(i, (i + by) % size) for i in range(size)])
        for by in (8, 4, 12)
    ]
    return array, *others


def summed_over_wide(array):
    own, far, up, down = from_chips(array + swapped(array))
    return (own + far) + (up + down)


def from_last_chip(array, is_last, beside):
    size = lax.axis_size("wide")
    array = jnp.where(is_last, array, 0.0)
    last = size - 2
    total = array
    for back in (8, 4, 12):
        pairs = [(last + c, (last + c + back) % size) for c in range(2)]
        total = total + lax.ppermute(array, "wide", pairs)
    pairs = [(i, i ^ 2) for i in range(size) if i & 2]
    total, beside = lax.optimization_barrier((total, beside))
    return total + lax.ppermute(total, "wide", pairs), beside


def half_pairs(arrays, others, half):
    mine = (lax.axis_index("wide") % 2) * half
    return [
        jnp.concatenate(
            [lax.dynamic_slice_in_dim(x, mine, half, 2) for x in (array, other)], axis=1
        )
        for array, other in zip(arrays, others)
    ]


def own_half(halves):
    is_owner = lax.axis_index("wide") == lax.axis_size("wide") - 1
    return jnp.where(is_owner, halves[1], swapped(halves[0]))


def solve_chain(remain, rest, d_pair, l_pair, is_last):
    panels, pair_cols, half = d_pair.shape
    share = pair_cols // 2
    rest = own_half(rest)
    pending = [jnp.where(is_last, rest[p], 0.0) for p in range(panels - 1)]
    results = [None] * panels
    for source in reversed(range(panels)):
        part = lax.dot_general(remain, d_pair[source], NT, precision=HIGH)
        back = jnp.concatenate([part[:, share:], part[:, :share]], axis=1)
        pair = part + swapped(back)
        results[source] = pair[:, :share]
        offset = source * (source - 1) // 2
        for target in range(source):
            pending[target] = pending[target] - dot(pair, l_pair[offset + target])
        if source > 0:
            own, far, up, down = from_chips(pending[source - 1])
            remain = (own + far) + (up + down)
    return jnp.stack(results, axis=1)


def gram_of(reflectors, lo, hi):
    return lax.dot_general(
        reflectors[1, lo:hi],
        reflectors[0, lo:hi],
        (((0,), (0,)), ((), ())),
        precision=HIGH,
    )


def body(tridiag_vectors, reflectors, triangles, lower_blocks, diag_inverses):
    wide_size = lax.axis_size("wide")
    narrow_size = lax.axis_size("narrow")
    _, length, block = reflectors.shape
    panels, panel_rows, _ = diag_inverses.shape
    half = panel_rows // 2
    subs = length // 128
    weights = (jnp.swapaxes(diag_inverses, 1, 2), lower_blocks)
    traded = [swapped(array) for array in weights]

    received = tridiag_vectors.reshape(wide_size, subs, 128)
    received = lax.all_to_all(received, "wide", 0, 0, tiled=True)
    gram = gram_of(reflectors, 0, length // 2)
    received, gram = lax.optimization_barrier((received, gram))
    received, later = lax.optimization_barrier((received, reflectors))
    received = lax.all_to_all(received, "narrow", 0, 0, tiled=True)
    gram = gram + gram_of(later, length // 2, length)
    received, gram, weights = lax.optimization_barrier((received, gram, weights))
    per = wide_size // narrow_size
    received = received.reshape(narrow_size, per, subs, 128)
    flat, first, second = products_of(received, reflectors)
    coeffs1 = dot(summed_over_wide(first), triangles[1].T)
    second = second - dot(coeffs1, gram)
    second = summed_over_wide(second)
    d_pair, l_pair = half_pairs(weights, traded, half)
    second, d_pair, l_pair = lax.optimization_barrier((second, d_pair, l_pair))
    coeffs0 = dot(second, triangles[0].T)
    coeffs = jnp.concatenate([coeffs1, coeffs0], axis=1)

    is_last = lax.axis_index("wide") >= wide_size - 2
    start = length - panels * panel_rows
    last = corner_of(flat, coeffs, reflectors, length - panel_rows, 1, half)
    corner = own_half(last)[0]
    corner, late = lax.optimization_barrier((corner, coeffs))
    rest = corner_of(flat, late, reflectors, start, panels - 1, half)
    remain, rest = from_last_chip(corner, is_last, rest)
    remain, late = lax.optimization_barrier((remain, late))
    transformed = transformed_of(flat, late, reflectors, rest, last)
    solved = solve_chain(remain, rest, d_pair, l_pair, is_last)
    return (transformed, solved)


def solution(mesh):
    placed = (
        P(("wide", "narrow"), None),
        P(None, "wide", None),
        P(),
        P(None, "wide", None),
        P(None, None, "wide"),
    )
    return jax.shard_map(
        body,
        mesh=mesh,
        in_specs=placed,
        out_specs=(P("narrow", "wide"), P("narrow", None, "wide")),
        check_vma=False,
    )
```

time: 162 us -> 135 us (0.83)
  blocking collectives: 33.3 us -> 0 us
  Pallas kernels: 0 us -> 19 us
  starting transfers between devices: 39.4 us -> 57.6 us
  matrix products: 33 us -> 17.2 us
  local copies, waits for them, and re-layouts: 13.5 us -> 5.98 us
  waiting for transfers between devices: 36.9 us -> 31.5 us
    all_to_all x2 -> x0, blocking collectives: 33.3 us -> none  [the longest x1 17.6 us: body(): lax.all_to_all(tridiag_vectors, 'wide', split_axis=1, concat_axis=0, tile...]
    dot_general x12 -> x9, matrix products: 27.9 us -> 2.19 us  [dot(): return jnp.dot(a, b, precision=HIGH)]
    pallas_call x0 -> x4, Pallas kernels: none -> 19 us  [the longest x2 8.55 us: corner_of(): pl.pallas_call(functools.partial(corner_kernel, first // UNIT), out_shape...]
    dot_general x4 -> x6, matrix products: 5.16 us -> 15 us  [the longest x2 13.8 us: gram_of(): lax.dot_general(reflectors[1, lo:hi], reflectors[0, lo:hi], (((0,), (0,))...]
    ppermute x13 -> x21, starting transfers between devices: 13.5 us -> 22.6 us  [the longest x15 18.6 us: from_chips(): lax.ppermute(array, 'wide', [(i, (i + by) % size) for i in range(size)])]
    ppermute x7 -> x10, starting transfers between devices: 13 us -> 19.5 us  [swapped(): return lax.ppermute(array, 'wide', [(i, i ^ 1) for i in range(size)])]
    all_to_all x2, waiting for transfers between devices: 9.89 us -> 4.75 us  [the longest x1 3.01 us: body(): received = lax.all_to_all(received, 'wide', 0, 0, tiled=True)]
    slice x2 -> x0, local copies, waits for them, and re-layouts: 2.95 us -> none  [the longest x1 2.16 us: solve_chain(): tail[:, :, 1, :]]
  transfers between devices with their start and end apart: 25 -> 36, of which waited for: 18 -> 26; matrix products, arithmetic and copies ran while one was open for 13% -> 14% of each run, Pallas kernels for 0% -> 12%
where the time goes in v2:
time: 135 us
  starting transfers between devices  57.6 us (43%)
  waiting for transfers between devices  31.5 us (23%)
  Pallas kernels  19 us (14%)
  matrix products  17.2 us (13%)
  local copies, waits for them, and re-layouts  5.98 us (4%)
  other arithmetic  2.75 us (2%)
    ppermute x10, starting transfers between devices, swapped(): return lax.ppermute(array, 'wide', [(i, i ^ 1) for i in range(size)])  19.5 us
    ppermute x15, starting transfers between devices, from_chips(): lax.ppermute(array, 'wide', [(i, (i + by) % size) for i in range(size)])  18.6 us
    dot_general x2, matrix products, gram_of(): lax.dot_general(reflectors[1, lo:hi], reflectors[0, lo:hi], (((0,), (0,))...  13.8 us
    ppermute x15, waiting for transfers between devices, from_chips(): lax.ppermute(array, 'wide', [(i, (i + by) % size) for i in range(size)])  11.1 us
    pallas_call x2, Pallas kernels, corner_of(): pl.pallas_call(functools.partial(corner_kernel, first // UNIT), out_shape...  8.55 us
    ppermute x5, waiting for transfers between devices, from_chips(): lax.ppermute(array, 'wide', [(i, i ^ 2) for i in range(size)])  7.08 us
    all_to_all x1, starting transfers between devices, body(): received = lax.all_to_all(received, 'wide', 0, 0, tiled=True)  6.84 us
    pallas_call x1, Pallas kernels, products_of(): pl.pallas_call(products_kernel, out_shape=[jax.ShapeDtypeStruct((rows, le...  6.43 us
  transfers between devices with their start and end apart: 36, of which 26 were waited for; matrix products, arithmetic and copies ran while one was open for 14% of the time, Pallas kernels for 12%

profile of v2, /device:TPU:1, one launch (start us, length us, event | category | flops | bytes accessed | tf_op | source)
XLA Modules:
  0.0 135.0 jit_solution(16461808372235216400)
XLA Ops:
  0.6 1.5 %collective-permute-start.11 = (f32[6,96,1536]{2,1,0:T(8,128)}, f32[6,96,1536]{2,1,0:T(8,128)}, u32[]{:S(2)}, u32[]{:S(2)}) collective-permute-start(f32[6,96,1536]{2,1,0:T(8,128)} %param.8), channel_id=1, source_target_pairs={{0,8},{8,0},{16,24},{24,16},{32,40},{40,32},{48,56},{56,48},{64,72... | collective-permute-start | bytes 10616840 | tf_op jit(solution)/shard_map/ppermute | solution.py:190
  2.2 6.8 %all-to-all-start = ((f32[16,64,128]{2,1,0:T(8,128)}), f32[16,64,128]{2,1,0:T(8,128)}, u32[]{:S(2)}, u32[]{:S(2)}) async-start(f32[16,64,128]{2,1,0:T(8,128)} %bitcast.114), calls=%async_computation | async-start | bytes 1048576 | tf_op jit(solution)/shard_map/all_to_all | solution.py:276
  9.1 6.9 %fusion.3 = f32[256,256]{1,0:T(8,128)S(1)} fusion(f32[2,8192,256]{2,1,0:T(8,128)} %v_ref.7), kind=kOutput, calls=%fused_computation.3 | convolution fusion | flops 1610612736 | bytes 8650752 | tf_op jit(solution)/shard_map/dot_general | solution.py:257
  16.0 3.0 %all-to-all-done = f32[16,64,128]{2,1,0:T(8,128)} async-done(((f32[16,64,128]{2,1,0:T(8,128)}), f32[16,64,128]{2,1,0:T(8,128)}, u32[]{:S(2)}, u32[]{:S(2)}) %all-to-all-start) | async-done | bytes 524320 | tf_op jit(solution)/shard_map/all_to_all | solution.py:276
  19.0 6.4 %all-to-all-start.1 = ((f32[16,64,128]{2,1,0:T(8,128)}), f32[16,64,128]{2,1,0:T(8,128)S(1)}, u32[]{:S(2)}, u32[]{:S(2)}) async-start(f32[16,64,128]{2,1,0:T(8,128)} %all-to-all-done), calls=%async_computation.1 | async-start | bytes 1048576 | tf_op jit(solution)/shard_map/all_to_all | solution.py:280
  25.3 6.9 %fusion.10 = f32[256,256]{1,0:T(8,128)S(1)} fusion(f32[256,256]{1,0:T(8,128)S(1)} %fusion.3, f32[2,8192,256]{2,1,0:T(8,128)} %v_ref.7), kind=kOutput, calls=%fused_computation.12 | convolution fusion | flops 1610678272 | bytes 8912896 | tf_op jit(solution)/shard_map/dot_general | solution.py:257
  32.2 1.7 %all-to-all-done.1 = f32[16,64,128]{2,1,0:T(8,128)S(1)} async-done(((f32[16,64,128]{2,1,0:T(8,128)}), f32[16,64,128]{2,1,0:T(8,128)S(1)}, u32[]{:S(2)}, u32[]{:S(2)}) %all-to-all-start.1) | async-done | bytes 524320 | tf_op jit(solution)/shard_map/all_to_all | solution.py:280
  34.0 6.4 %shard_map.68 = (f32[16,8192]{1,0:T(8,128)S(1)}, f32[16,256]{1,0:T(8,128)S(1)}, f32[16,256]{1,0:T(8,128)S(1)}) custom-call(f32[8,2,64,128]{3,2,1,0:T(8,128)S(1)} %bitcast.111, f32[2,8192,256]{2,1,0:T(8,128)} %v_ref.7), custom_call_target="tpu_custom_call" | custom-call | flops 402653184 | bytes 17825792 | tf_op jit(solution)/shard_map/pallas_call | solution.py:85
  40.4 3.3 %collective-permute-start = (f32[16,256]{1,0:T(8,128)S(1)}, f32[16,256]{1,0:T(8,128)S(1)}, u32[]{:S(2)}, u32[]{:S(2)}) collective-permute-start(f32[16,256]{1,0:T(8,128)S(1)} %get-tuple-element.28), channel_id=1, source_target_pairs={{0,8},{8,0},{16,24},{24,16},{32,40},{40,32},{48,56},{56,48},{64,72... | collective-permute-start | bytes 49160 | tf_op jit(solution)/shard_map/ppermute | solution.py:190
  43.7 0.8 collective-permute-done
  44.5 0.7 collective-permute-start.1
  45.2 1.9 %collective-permute-done.1 = f32[16,256]{1,0:T(8,128)S(1)} collective-permute-done((f32[16,256]{1,0:T(8,128)S(1)}, f32[16,256]{1,0:T(8,128)S(1)}, u32[]{:S(2)}, u32[]{:S(2)}) %collective-permute-start.1) | collective-permute-done | bytes 16416 | tf_op jit(solution)/shard_map/ppermute | solution.py:195
  47.1 1.1 collective-permute-start.2
  48.3 2.6 %collective-permute-start.4 = (f32[16,256]{1,0:T(8,128)S(1)}, f32[16,256]{1,0:T(8,128)S(1)}, u32[]{:S(2)}, u32[]{:S(2)}) collective-permute-start(f32[16,256]{1,0:T(8,128)S(1)} %add.105), channel_id=1, source_target_pairs={{0,96},{8,104},{16,112},{24,120},{32,0},{40,8},{48,16},{56,24},{64... | collective-permute-start | bytes 49160 | tf_op jit(solution)/shard_map/ppermute | solution.py:197
  51.2 0.8 collective-permute-done.3
  52.4 3.0 %collective-permute-start.5 = (f32[16,256]{1,0:T(8,128)S(1)}, f32[16,256]{1,0:T(8,128)S(1)}, u32[]{:S(2)}, u32[]{:S(2)}) collective-permute-start(f32[16,256]{1,0:T(8,128)S(1)} %convolution_subtract_fusion), channel_id=1, source_target_pairs={{0,8},{8,0},{16,24},{24,16},{32,40},{40,32},{48,56},{56,48},{64,72... | collective-permute-start | bytes 49160 | tf_op jit(solution)/shard_map/ppermute | solution.py:190
  55.4 0.8 collective-permute-done.5
  56.4 1.6 %constant_dynamic-slice_fusion.1 = f32[6,96,768]{2,1,0:T(8,128)S(1)} fusion(f32[6,96,1536]{2,1,0:T(8,128)} %param.8, s32[]{:T(128)S(6)} %select_n.63), kind=kLoop, calls=%fused_computation.95 | loop fusion | bytes 3538948 | tf_op jit(solution)/shard_map/dynamic_slice | solution.py:225
  58.1 0.8 collective-permute-done.6
  58.8 1.4 %collective-permute-start.7 = (f32[16,256]{1,0:T(8,128)S(1)}, f32[16,256]{1,0:T(8,128)S(1)}, u32[]{:S(2)}, u32[]{:S(2)}) collective-permute-start(f32[16,256]{1,0:T(8,128)S(1)} %add.110), channel_id=1, source_target_pairs={{0,64},{8,72},{16,80},{24,88},{32,96},{40,104},{48,112},{56,120},{... | collective-permute-start | bytes 49160 | tf_op jit(solution)/shard_map/ppermute | solution.py:197
  60.2 2.1 %collective-permute-start.8 = (f32[16,256]{1,0:T(8,128)S(1)}, f32[16,256]{1,0:T(8,128)S(1)}, u32[]{:S(2)}, u32[]{:S(2)}) collective-permute-start(f32[16,256]{1,0:T(8,128)S(1)} %add.110), channel_id=1, source_target_pairs={{0,32},{8,40},{16,48},{24,56},{32,64},{40,72},{48,80},{56,88},{64,... | collective-permute-start | bytes 49160 | tf_op jit(solution)/shard_map/ppermute | solution.py:197
  62.4 0.5 collective-permute-start.9
  63.0 1.0 collective-permute-done.8
  64.0 1.1 collective-permute-done.9
  65.2 1.4 %constant_dynamic-slice_fusion.2 = f32[4,96,768]{2,1,0:T(8,128)S(1)} fusion(f32[4,96,1536]{2,1,0:T(8,128)} %collective-permute-done.10, s32[]{:T(128)S(6)} %select_n.63), kind=kLoop, calls=%fused_computation.96 | loop fusion | bytes 2359300 | tf_op jit(solution)/shard_map/dynamic_slice | solution.py:225
  66.7 1.6 %constant_dynamic-slice_fusion = f32[6,96,768]{2,1,0:T(8,128)S(1)} fusion(f32[6,96,1536]{2,1,0:T(8,128)} %collective-permute-done.11, s32[]{:T(128)S(6)} %select_n.63), kind=kLoop, calls=%fused_computation.94 | loop fusion | bytes 3538948 | tf_op jit(solution)/shard_map/dynamic_slice | solution.py:225
  68.4 2.2 %pad_maximum_fusion = f32[6,192,768]{2,1,0:T(8,128)} fusion(f32[6,96,768]{2,1,0:T(8,128)S(1)} %constant_dynamic-slice_fusion, f32[6,96,768]{2,1,0:T(8,128)S(1)} %constant_dynamic-slice_fusion.1), kind=kLoop, calls=%fused_computation.10 | loop fusion | flops 884736 | bytes 7077888 | tf_op jit(solution)/shard_map/concatenate | solution.py:224
  70.8 2.7 %shard_map.69.last_ref = f32[2,1,16,768]{3,2,1,0:T(8,128)S(1)} custom-call(f32[16,8192]{1,0:T(8,128)S(1)} %get-tuple-element.27.z_ref, f32[16,512]{1,0:T(8,128)S(1)} %pad_maximum_fusion.2.coeffs_ref, f32[2,8192,256]{2,1,0:T(8,128)} %v_ref.7), custom_call_target="tpu_custom_call" | custom-call | flops 75497472 | bytes 3342336 | tf_op jit(solution)/shard_map/pallas_call | solution.py:162
  73.5 3.1 %collective-permute-start.12 = (f32[1,16,768]{2,1,0:T(8,128)S(1)}, f32[1,16,768]{2,1,0:T(8,128)S(1)}, u32[]{:S(2)}, u32[]{:S(2)}) collective-permute-start(f32[1,16,768]{2,1,0:T(8,128)S(1)} %slice_bitcast_fusion.1), channel_id=1, source_target_pairs={{0,8},{8,0},{16,24},{24,16},{32,40},{40,32},{48,56},{56,48},{64,72... | collective-permute-start | bytes 147464 | tf_op jit(solution)/shard_map/ppermute | solution.py:190
  76.6 0.9 collective-permute-done.12
  77.5 0.8 collective-permute-start.13
  78.3 0.8 collective-permute-start.14
  79.1 0.7 collective-permute-start.15
  79.8 5.9 %shard_map.70.rest_ref = f32[2,3,16,768]{3,2,1,0:T(8,128)S(1)} custom-call(f32[16,8192]{1,0:T(8,128)S(1)} %get-tuple-element.27.z_ref, f32[16,512]{1,0:T(8,128)S(1)} %pad_maximum_fusion.2.coeffs_ref, f32[2,8192,256]{2,1,0:T(8,128)} %v_ref.7), custom_call_target="tpu_custom_call" | custom-call | flops 226492416 | bytes 10027008 | tf_op jit(solution)/shard_map/pallas_call | solution.py:162
  85.7 1.3 collective-permute-start.16
  87.4 3.1 %collective-permute-done.16 = f32[16,768]{1,0:T(8,128)S(1)} collective-permute-done((f32[16,768]{1,0:T(8,128)S(1)}, f32[16,768]{1,0:T(8,128)S(1)}, u32[]{:S(2)}, u32[]{:S(2)}) %collective-permute-start.16) | collective-permute-done | bytes 49184 | tf_op jit(solution)/shard_map/ppermute | solution.py:218
  91.1 1.5 %collective-permute-start.18 = (f32[16,192]{1,0:T(8,128)S(1)}, f32[16,192]{1,0:T(8,128)S(1)}, u32[]{:S(2)}, u32[]{:S(2)}) collective-permute-start(f32[16,192]{1,0:T(8,128)S(1)} %pad_maximum_fusion.4), channel_id=1, source_target_pairs={{0,8},{8,0},{16,24},{24,16},{32,40},{40,32},{48,56},{56,48},{64,72... | collective-permute-start | bytes 36872 | tf_op jit(solution)/shard_map/ppermute | solution.py:190
  92.6 0.8 collective-permute-done.18
  93.8 2.9 %collective-permute-done.19 = f32[16,768]{1,0:T(8,128)S(1)} collective-permute-done((f32[16,768]{1,0:T(8,128)S(1)}, f32[16,768]{1,0:T(8,128)S(1)}, u32[]{:S(2)}, u32[]{:S(2)}) %collective-permute-start.19) | collective-permute-done | bytes 49184 | tf_op jit(solution)/shard_map/ppermute | solution.py:195
  96.7 0.8 collective-permute-start.20
  97.5 2.6 %collective-permute-start.21 = (f32[16,768]{1,0:T(8,128)S(1)}, f32[16,768]{1,0:T(8,128)S(1)}, u32[]{:S(2)}, u32[]{:S(2)}) collective-permute-start(f32[16,768]{1,0:T(8,128)S(1)} %add.121), channel_id=1, source_target_pairs={{0,32},{8,40},{16,48},{24,56},{32,64},{40,72},{48,80},{56,88},{64,... | collective-permute-start | bytes 147464 | tf_op jit(solution)/shard_map/ppermute | solution.py:197
  100.2 1.1 collective-permute-done.20
  101.3 0.5 collective-permute-done.21
  101.8 1.7 %collective-permute-done.22 = f32[16,768]{1,0:T(8,128)S(1)} collective-permute-done((f32[16,768]{1,0:T(8,128)S(1)}, f32[16,768]{1,0:T(8,128)S(1)}, u32[]{:S(2)}, u32[]{:S(2)}) %collective-permute-start.22) | collective-permute-done | bytes 49184 | tf_op jit(solution)/shard_map/ppermute | solution.py:197
  104.0 2.8 %collective-permute-start.23 = (f32[16,192]{1,0:T(8,128)S(1)}, f32[16,192]{1,0:T(8,128)S(1)}, u32[]{:S(2)}, u32[]{:S(2)}) collective-permute-start(f32[16,192]{1,0:T(8,128)S(1)} %pad_maximum_fusion.5), channel_id=1, source_target_pairs={{0,8},{8,0},{16,24},{24,16},{32,40},{40,32},{48,56},{56,48},{64,72... | collective-permute-start | bytes 36872 | tf_op jit(solution)/shard_map/ppermute | solution.py:190
  107.1 0.6 collective-permute-done.23
  108.0 4.0 %shard_map.71 = f32[16,8192]{1,0:T(8,128)} custom-call(f32[16,8192]{1,0:T(8,128)S(1)} %get-tuple-element.27.z_ref, f32[16,512]{1,0:T(8,128)S(1)} %pad_maximum_fusion.2.coeffs_ref, f32[2,8192,256]{2,1,0:T(8,128)} %v_ref.7, f32[2,3,16,768]{3,2,1,0:T(8,128)S(1)} %shard_map.70.rest_ref, f32[2,1,16,768]{3,2,1,0:T(8,128)S(1)} %shard_map.69.last_ref), custom_call_target="tpu_custom_call" | custom-call | flops 100663296 | bytes 4456448 | tf_op jit(solution)/shard_map/pallas_call | solution.py:177
  112.0 0.5 collective-permute-start.25
  112.5 1.5 %collective-permute-start.26 = (f32[16,768]{1,0:T(8,128)S(1)}, f32[16,768]{1,0:T(8,128)S(1)}, u32[]{:S(2)}, u32[]{:S(2)}) collective-permute-start(f32[16,768]{1,0:T(8,128)S(1)} %add.126), channel_id=1, source_target_pairs={{0,32},{8,40},{16,48},{24,56},{32,64},{40,72},{48,80},{56,88},{64,... | collective-permute-start | bytes 147464 | tf_op jit(solution)/shard_map/ppermute | solution.py:197
  114.0 1.2 collective-permute-start.27
  115.5 1.1 collective-permute-done.25
  116.6 1.1 collective-permute-done.26
  118.2 1.4 %collective-permute-start.28 = (f32[16,192]{1,0:T(8,128)S(1)}, f32[16,192]{1,0:T(8,128)S(1)}, u32[]{:S(2)}, u32[]{:S(2)}) collective-permute-start(f32[16,192]{1,0:T(8,128)S(1)} %pad_maximum_fusion.6), channel_id=1, source_target_pairs={{0,8},{8,0},{16,24},{24,16},{32,40},{40,32},{48,56},{56,48},{64,72... | collective-permute-start | bytes 36872 | tf_op jit(solution)/shard_map/ppermute | solution.py:190
  119.9 0.6 collective-permute-done.28
  120.7 1.8 %collective-permute-start.29 = (f32[16,768]{1,0:T(8,128)S(1)}, f32[16,768]{1,0:T(8,128)S(1)}, u32[]{:S(2)}, u32[]{:S(2)}) collective-permute-start(f32[16,768]{1,0:T(8,128)S(1)} %fusion.59), channel_id=1, source_target_pairs={{0,16},{8,24},{16,0},{24,8},{32,48},{40,56},{48,32},{56,40},{64,80... | collective-permute-start | bytes 147464 | tf_op jit(solution)/shard_map/ppermute | solution.py:195
  122.5 1.5 %collective-permute-done.29 = f32[16,768]{1,0:T(8,128)S(1)} collective-permute-done((f32[16,768]{1,0:T(8,128)S(1)}, f32[16,768]{1,0:T(8,128)S(1)}, u32[]{:S(2)}, u32[]{:S(2)}) %collective-permute-start.29) | collective-permute-done | bytes 49184 | tf_op jit(solution)/shard_map/ppermute | solution.py:195
  124.0 1.5 %collective-permute-start.30 = (f32[16,768]{1,0:T(8,128)S(1)}, f32[16,768]{1,0:T(8,128)S(1)}, u32[]{:S(2)}, u32[]{:S(2)}) collective-permute-start(f32[16,768]{1,0:T(8,128)S(1)} %add.131), channel_id=1, source_target_pairs={{0,64},{8,72},{16,80},{24,88},{32,96},{40,104},{48,112},{56,120},{... | collective-permute-start | bytes 147464 | tf_op jit(solution)/shard_map/ppermute | solution.py:197
  125.4 1.6 %collective-permute-start.31 = (f32[16,768]{1,0:T(8,128)S(1)}, f32[16,768]{1,0:T(8,128)S(1)}, u32[]{:S(2)}, u32[]{:S(2)}) collective-permute-start(f32[16,768]{1,0:T(8,128)S(1)} %add.131), channel_id=1, source_target_pairs={{0,32},{8,40},{16,48},{24,56},{32,64},{40,72},{48,80},{56,88},{64,... | collective-permute-start | bytes 147464 | tf_op jit(solution)/shard_map/ppermute | solution.py:197
  127.0 1.1 collective-permute-start.32
  128.5 1.1 collective-permute-done.31
  129.6 0.9 collective-permute-done.32
  131.0 2.4 %collective-permute-start.33 = (f32[16,192]{1,0:T(8,128)S(1)}, f32[16,192]{1,0:T(8,128)S(1)}, u32[]{:S(2)}, u32[]{:S(2)}) collective-permute-start(f32[16,192]{1,0:T(8,128)S(1)} %pad_maximum_fusion.7), channel_id=1, source_target_pairs={{0,8},{8,0},{16,24},{24,16},{32,40},{40,32},{48,56},{56,48},{64,72... | collective-permute-start | bytes 36872 | tf_op jit(solution)/shard_map/ppermute | solution.py:190
  133.5 0.8 collective-permute-done.33
  134.3 0.6 copy.7
  (74 shorter events, 6.5 us)
Async XLA Ops:
  0.6 66.1 %collective-permute-start.11 = (f32[6,96,1536]{2,1,0:T(8,128)}, f32[6,96,1536]{2,1,0:T(8,128)}, u32[]{:S(2)}, u32[]{:S(2)}) collective-permute-start(f32[6,96,1536]{2,1,0:T(8,128)} %param.8), channel_id=1, source_target_pairs={{0,8},{8,0},{16,24},{24,16},{32,40},{40,32},{48,56},{56,48},{64,72... | collective-permute-start | bytes 10616840 | tf_op jit(solution)/shard_map/ppermute | solution.py:190
  2.1 63.1 %collective-permute-start.10 = (f32[4,96,1536]{2,1,0:T(8,128)}, f32[4,96,1536]{2,1,0:T(8,128)}, u32[]{:S(2)}, u32[]{:S(2)}) collective-permute-start(f32[4,96,1536]{2,1,0:T(8,128)} %bitcast.112), channel_id=1, source_target_pairs={{0,8},{8,0},{16,24},{24,16},{32,40},{40,32},{48,56},{56,48},{64,72... | collective-permute-start | bytes 7077896 | tf_op jit(solution)/shard_map/ppermute | solution.py:190
  2.2 16.7 %all-to-all-start = ((f32[16,64,128]{2,1,0:T(8,128)}), f32[16,64,128]{2,1,0:T(8,128)}, u32[]{:S(2)}, u32[]{:S(2)}) async-start(f32[16,64,128]{2,1,0:T(8,128)} %bitcast.114), calls=%async_computation | async-start | bytes 1048576 | tf_op jit(solution)/shard_map/all_to_all | solution.py:276
  19.0 15.0 %all-to-all-start.1 = ((f32[16,64,128]{2,1,0:T(8,128)}), f32[16,64,128]{2,1,0:T(8,128)S(1)}, u32[]{:S(2)}, u32[]{:S(2)}) async-start(f32[16,64,128]{2,1,0:T(8,128)} %all-to-all-done), calls=%async_computation.1 | async-start | bytes 1048576 | tf_op jit(solution)/shard_map/all_to_all | solution.py:280
  34.0 18.0 %copy-start.2 = (f32[2,256,256]{2,1,0:T(8,128)S(1)}, f32[2,256,256]{2,1,0:T(8,128)}, u32[]{:S(2)}) copy-start(f32[2,256,256]{2,1,0:T(8,128)} %param.7) | copy-start | bytes 1572868
  40.4 22.5 %copy-start.1 = (f32[4,1536,96]{1,2,0:T(8,128)S(1)}, f32[4,1536,96]{1,2,0:T(8,128)}, u32[]{:S(2)}) copy-start(f32[4,1536,96]{1,2,0:T(8,128)} %param.9) | copy-start | bytes 7077892
  40.4 4.1 %collective-permute-start = (f32[16,256]{1,0:T(8,128)S(1)}, f32[16,256]{1,0:T(8,128)S(1)}, u32[]{:S(2)}, u32[]{:S(2)}) collective-permute-start(f32[16,256]{1,0:T(8,128)S(1)} %get-tuple-element.28), channel_id=1, source_target_pairs={{0,8},{8,0},{16,24},{24,16},{32,40},{40,32},{48,56},{56,48},{64,72... | collective-permute-start | bytes 49160 | tf_op jit(solution)/shard_map/ppermute | solution.py:190
  44.5 2.6 %collective-permute-start.1 = (f32[16,256]{1,0:T(8,128)S(1)}, f32[16,256]{1,0:T(8,128)S(1)}, u32[]{:S(2)}, u32[]{:S(2)}) collective-permute-start(f32[16,256]{1,0:T(8,128)S(1)} %add.104), channel_id=1, source_target_pairs={{0,16},{8,24},{16,0},{24,8},{32,48},{40,56},{48,32},{56,40},{64,80... | collective-permute-start | bytes 49160 | tf_op jit(solution)/shard_map/ppermute | solution.py:195
  47.1 4.1 %collective-permute-start.2 = (f32[16,256]{1,0:T(8,128)S(1)}, f32[16,256]{1,0:T(8,128)S(1)}, u32[]{:S(2)}, u32[]{:S(2)}) collective-permute-start(f32[16,256]{1,0:T(8,128)S(1)} %add.105), channel_id=1, source_target_pairs={{0,64},{8,72},{16,80},{24,88},{32,96},{40,104},{48,112},{56,120},{... | collective-permute-start | bytes 49160 | tf_op jit(solution)/shard_map/ppermute | solution.py:197
  48.2 3.8 %collective-permute-start.3 = (f32[16,256]{1,0:T(8,128)S(1)}, f32[16,256]{1,0:T(8,128)S(1)}, u32[]{:S(2)}, u32[]{:S(2)}) collective-permute-start(f32[16,256]{1,0:T(8,128)S(1)} %add.105), channel_id=1, source_target_pairs={{0,32},{8,40},{16,48},{24,56},{32,64},{40,72},{48,80},{56,88},{64,... | collective-permute-start | bytes 49160 | tf_op jit(solution)/shard_map/ppermute | solution.py:197
  48.3 3.7 %collective-permute-start.4 = (f32[16,256]{1,0:T(8,128)S(1)}, f32[16,256]{1,0:T(8,128)S(1)}, u32[]{:S(2)}, u32[]{:S(2)}) collective-permute-start(f32[16,256]{1,0:T(8,128)S(1)} %add.105), channel_id=1, source_target_pairs={{0,96},{8,104},{16,112},{24,120},{32,0},{40,8},{48,16},{56,24},{64... | collective-permute-start | bytes 49160 | tf_op jit(solution)/shard_map/ppermute | solution.py:197
  52.4 3.8 %collective-permute-start.5 = (f32[16,256]{1,0:T(8,128)S(1)}, f32[16,256]{1,0:T(8,128)S(1)}, u32[]{:S(2)}, u32[]{:S(2)}) collective-permute-start(f32[16,256]{1,0:T(8,128)S(1)} %convolution_subtract_fusion), channel_id=1, source_target_pairs={{0,8},{8,0},{16,24},{24,16},{32,40},{40,32},{48,56},{56,48},{64,72... | collective-permute-start | bytes 49160 | tf_op jit(solution)/shard_map/ppermute | solution.py:190
  56.2 2.6 %collective-permute-start.6 = (f32[16,256]{1,0:T(8,128)S(1)}, f32[16,256]{1,0:T(8,128)S(1)}, u32[]{:S(2)}, u32[]{:S(2)}) collective-permute-start(f32[16,256]{1,0:T(8,128)S(1)} %add.109), channel_id=1, source_target_pairs={{0,16},{8,24},{16,0},{24,8},{32,48},{40,56},{48,32},{56,40},{64,80... | collective-permute-start | bytes 49160 | tf_op jit(solution)/shard_map/ppermute | solution.py:195
  58.8 4.2 %collective-permute-start.7 = (f32[16,256]{1,0:T(8,128)S(1)}, f32[16,256]{1,0:T(8,128)S(1)}, u32[]{:S(2)}, u32[]{:S(2)}) collective-permute-start(f32[16,256]{1,0:T(8,128)S(1)} %add.110), channel_id=1, source_target_pairs={{0,64},{8,72},{16,80},{24,88},{32,96},{40,104},{48,112},{56,120},{... | collective-permute-start | bytes 49160 | tf_op jit(solution)/shard_map/ppermute | solution.py:197
  60.2 3.8 %collective-permute-start.8 = (f32[16,256]{1,0:T(8,128)S(1)}, f32[16,256]{1,0:T(8,128)S(1)}, u32[]{:S(2)}, u32[]{:S(2)}) collective-permute-start(f32[16,256]{1,0:T(8,128)S(1)} %add.110), channel_id=1, source_target_pairs={{0,32},{8,40},{16,48},{24,56},{32,64},{40,72},{48,80},{56,88},{64,... | collective-permute-start | bytes 49160 | tf_op jit(solution)/shard_map/ppermute | solution.py:197
  62.4 2.8 %collective-permute-start.9 = (f32[16,256]{1,0:T(8,128)S(1)}, f32[16,256]{1,0:T(8,128)S(1)}, u32[]{:S(2)}, u32[]{:S(2)}) collective-permute-start(f32[16,256]{1,0:T(8,128)S(1)} %add.110), channel_id=1, source_target_pairs={{0,96},{8,104},{16,112},{24,120},{32,0},{40,8},{48,16},{56,24},{64... | collective-permute-start | bytes 49160 | tf_op jit(solution)/shard_map/ppermute | solution.py:197
  68.4 2.2 %copy-start.3 = (f32[2,256,256]{2,1,0:T(8,128)S(1)}, f32[2,256,256]{2,1,0:T(8,128)}, u32[]{:S(2)}) copy-start(f32[2,256,256]{2,1,0:T(8,128)} %param.7) | copy-start | bytes 1572868
  73.5 3.9 %collective-permute-start.12 = (f32[1,16,768]{2,1,0:T(8,128)S(1)}, f32[1,16,768]{2,1,0:T(8,128)S(1)}, u32[]{:S(2)}, u32[]{:S(2)}) collective-permute-start(f32[1,16,768]{2,1,0:T(8,128)S(1)} %slice_bitcast_fusion.1), channel_id=1, source_target_pairs={{0,8},{8,0},{16,24},{24,16},{32,40},{40,32},{48,56},{56,48},{64,72... | collective-permute-start | bytes 147464 | tf_op jit(solution)/shard_map/ppermute | solution.py:190
  77.5 16.0 %copy-start = (f32[6,192,768]{2,1,0:T(8,128)S(1)}, f32[6,192,768]{2,1,0:T(8,128)}, u32[]{:S(2)}) copy-start(f32[6,192,768]{2,1,0:T(8,128)} %pad_maximum_fusion) | copy-start | bytes 10616836
  77.5 8.1 %collective-permute-start.13 = (f32[16,768]{1,0:T(8,128)S(1)}, f32[16,768]{1,0:T(8,128)S(1)}, u32[]{:S(2)}, u32[]{:S(2)}) collective-permute-start(f32[16,768]{1,0:T(8,128)S(1)} %broadcast_select_fusion), channel_id=1, source_target_pairs={{112,48},{120,56},{113,49},{121,57},{114,50},{122,58},{115,51},{12... | collective-permute-start | bytes 147464 | tf_op jit(solution)/shard_map/ppermute | solution.py:215
  78.3 7.4 %collective-permute-start.14 = (f32[16,768]{1,0:T(8,128)S(1)}, f32[16,768]{1,0:T(8,128)S(1)}, u32[]{:S(2)}, u32[]{:S(2)}) collective-permute-start(f32[16,768]{1,0:T(8,128)S(1)} %broadcast_select_fusion), channel_id=1, source_target_pairs={{112,16},{120,24},{113,17},{121,25},{114,18},{122,26},{115,19},{12... | collective-permute-start | bytes 147464 | tf_op jit(solution)/shard_map/ppermute | solution.py:215
  79.1 6.6 %collective-permute-start.15 = (f32[16,768]{1,0:T(8,128)S(1)}, f32[16,768]{1,0:T(8,128)S(1)}, u32[]{:S(2)}, u32[]{:S(2)}) collective-permute-start(f32[16,768]{1,0:T(8,128)S(1)} %broadcast_select_fusion), channel_id=1, source_target_pairs={{112,80},{120,88},{113,81},{121,89},{114,82},{122,90},{115,83},{12... | collective-permute-start | bytes 147464 | tf_op jit(solution)/shard_map/ppermute | solution.py:215
  85.7 4.8 %collective-permute-start.16 = (f32[16,768]{1,0:T(8,128)S(1)}, f32[16,768]{1,0:T(8,128)S(1)}, u32[]{:S(2)}, u32[]{:S(2)}) collective-permute-start(f32[16,768]{1,0:T(8,128)S(1)} %add_add_fusion), channel_id=1, source_target_pairs={{16,0},{24,8},{48,32},{56,40},{80,64},{88,72},{112,96},{120,104},{... | collective-permute-start | bytes 147464 | tf_op jit(solution)/shard_map/ppermute | solution.py:218
  87.0 6.4 %collective-permute-start.17 = (f32[3,16,768]{2,1,0:T(8,128)S(1)}, f32[3,16,768]{2,1,0:T(8,128)S(1)}, u32[]{:S(2)}, u32[]{:S(2)}) collective-permute-start(f32[3,16,768]{2,1,0:T(8,128)S(1)} %slice_bitcast_fusion), channel_id=1, source_target_pairs={{0,8},{8,0},{16,24},{24,16},{32,40},{40,32},{48,56},{56,48},{64,72... | collective-permute-start | bytes 442376 | tf_op jit(solution)/shard_map/ppermute | solution.py:190
  91.1 2.4 %collective-permute-start.18 = (f32[16,192]{1,0:T(8,128)S(1)}, f32[16,192]{1,0:T(8,128)S(1)}, u32[]{:S(2)}, u32[]{:S(2)}) collective-permute-start(f32[16,192]{1,0:T(8,128)S(1)} %pad_maximum_fusion.4), channel_id=1, source_target_pairs={{0,8},{8,0},{16,24},{24,16},{32,40},{40,32},{48,56},{56,48},{64,72... | collective-permute-start | bytes 36872 | tf_op jit(solution)/shard_map/ppermute | solution.py:190
  93.7 3.0 %collective-permute-start.19 = (f32[16,768]{1,0:T(8,128)S(1)}, f32[16,768]{1,0:T(8,128)S(1)}, u32[]{:S(2)}, u32[]{:S(2)}) collective-permute-start(f32[16,768]{1,0:T(8,128)S(1)} %fusion.55), channel_id=1, source_target_pairs={{0,16},{8,24},{16,0},{24,8},{32,48},{40,56},{48,32},{56,40},{64,80... | collective-permute-start | bytes 147464 | tf_op jit(solution)/shard_map/ppermute | solution.py:195
  96.7 4.5 %collective-permute-start.20 = (f32[16,768]{1,0:T(8,128)S(1)}, f32[16,768]{1,0:T(8,128)S(1)}, u32[]{:S(2)}, u32[]{:S(2)}) collective-permute-start(f32[16,768]{1,0:T(8,128)S(1)} %add.121), channel_id=1, source_target_pairs={{0,64},{8,72},{16,80},{24,88},{32,96},{40,104},{48,112},{56,120},{... | collective-permute-start | bytes 147464 | tf_op jit(solution)/shard_map/ppermute | solution.py:197
  97.5 4.3 %collective-permute-start.21 = (f32[16,768]{1,0:T(8,128)S(1)}, f32[16,768]{1,0:T(8,128)S(1)}, u32[]{:S(2)}, u32[]{:S(2)}) collective-permute-start(f32[16,768]{1,0:T(8,128)S(1)} %add.121), channel_id=1, source_target_pairs={{0,32},{8,40},{16,48},{24,56},{32,64},{40,72},{48,80},{56,88},{64,... | collective-permute-start | bytes 147464 | tf_op jit(solution)/shard_map/ppermute | solution.py:197
  100.1 3.3 %collective-permute-start.22 = (f32[16,768]{1,0:T(8,128)S(1)}, f32[16,768]{1,0:T(8,128)S(1)}, u32[]{:S(2)}, u32[]{:S(2)}) collective-permute-start(f32[16,768]{1,0:T(8,128)S(1)} %add.121), channel_id=1, source_target_pairs={{0,96},{8,104},{16,112},{24,120},{32,0},{40,8},{48,16},{56,24},{64... | collective-permute-start | bytes 147464 | tf_op jit(solution)/shard_map/ppermute | solution.py:197
  104.0 3.7 %collective-permute-start.23 = (f32[16,192]{1,0:T(8,128)S(1)}, f32[16,192]{1,0:T(8,128)S(1)}, u32[]{:S(2)}, u32[]{:S(2)}) collective-permute-start(f32[16,192]{1,0:T(8,128)S(1)} %pad_maximum_fusion.5), channel_id=1, source_target_pairs={{0,8},{8,0},{16,24},{24,16},{32,40},{40,32},{48,56},{56,48},{64,72... | collective-permute-start | bytes 36872 | tf_op jit(solution)/shard_map/ppermute | solution.py:190
  107.9 4.1 %collective-permute-start.24 = (f32[16,768]{1,0:T(8,128)S(1)}, f32[16,768]{1,0:T(8,128)S(1)}, u32[]{:S(2)}, u32[]{:S(2)}) collective-permute-start(f32[16,768]{1,0:T(8,128)S(1)} %fusion.53), channel_id=1, source_target_pairs={{0,16},{8,24},{16,0},{24,8},{32,48},{40,56},{48,32},{56,40},{64,80... | collective-permute-start | bytes 147464 | tf_op jit(solution)/shard_map/ppermute | solution.py:195
  112.0 4.6 %collective-permute-start.25 = (f32[16,768]{1,0:T(8,128)S(1)}, f32[16,768]{1,0:T(8,128)S(1)}, u32[]{:S(2)}, u32[]{:S(2)}) collective-permute-start(f32[16,768]{1,0:T(8,128)S(1)} %add.126), channel_id=1, source_target_pairs={{0,64},{8,72},{16,80},{24,88},{32,96},{40,104},{48,112},{56,120},{... | collective-permute-start | bytes 147464 | tf_op jit(solution)/shard_map/ppermute | solution.py:197
  112.5 5.1 %collective-permute-start.26 = (f32[16,768]{1,0:T(8,128)S(1)}, f32[16,768]{1,0:T(8,128)S(1)}, u32[]{:S(2)}, u32[]{:S(2)}) collective-permute-start(f32[16,768]{1,0:T(8,128)S(1)} %add.126), channel_id=1, source_target_pairs={{0,32},{8,40},{16,48},{24,56},{32,64},{40,72},{48,80},{56,88},{64,... | collective-permute-start | bytes 147464 | tf_op jit(solution)/shard_map/ppermute | solution.py:197
  114.0 3.7 %collective-permute-start.27 = (f32[16,768]{1,0:T(8,128)S(1)}, f32[16,768]{1,0:T(8,128)S(1)}, u32[]{:S(2)}, u32[]{:S(2)}) collective-permute-start(f32[16,768]{1,0:T(8,128)S(1)} %add.126), channel_id=1, source_target_pairs={{0,96},{8,104},{16,112},{24,120},{32,0},{40,8},{48,16},{56,24},{64... | collective-permute-start | bytes 147464 | tf_op jit(solution)/shard_map/ppermute | solution.py:197
  118.2 2.2 %collective-permute-start.28 = (f32[16,192]{1,0:T(8,128)S(1)}, f32[16,192]{1,0:T(8,128)S(1)}, u32[]{:S(2)}, u32[]{:S(2)}) collective-permute-start(f32[16,192]{1,0:T(8,128)S(1)} %pad_maximum_fusion.6), channel_id=1, source_target_pairs={{0,8},{8,0},{16,24},{24,16},{32,40},{40,32},{48,56},{56,48},{64,72... | collective-permute-start | bytes 36872 | tf_op jit(solution)/shard_map/ppermute | solution.py:190
  120.7 3.2 %collective-permute-start.29 = (f32[16,768]{1,0:T(8,128)S(1)}, f32[16,768]{1,0:T(8,128)S(1)}, u32[]{:S(2)}, u32[]{:S(2)}) collective-permute-start(f32[16,768]{1,0:T(8,128)S(1)} %fusion.59), channel_id=1, source_target_pairs={{0,16},{8,24},{16,0},{24,8},{32,48},{40,56},{48,32},{56,40},{64,80... | collective-permute-start | bytes 147464 | tf_op jit(solution)/shard_map/ppermute | solution.py:195
  124.0 4.5 %collective-permute-start.30 = (f32[16,768]{1,0:T(8,128)S(1)}, f32[16,768]{1,0:T(8,128)S(1)}, u32[]{:S(2)}, u32[]{:S(2)}) collective-permute-start(f32[16,768]{1,0:T(8,128)S(1)} %add.131), channel_id=1, source_target_pairs={{0,64},{8,72},{16,80},{24,88},{32,96},{40,104},{48,112},{56,120},{... | collective-permute-start | bytes 147464 | tf_op jit(solution)/shard_map/ppermute | solution.py:197
  125.4 4.2 %collective-permute-start.31 = (f32[16,768]{1,0:T(8,128)S(1)}, f32[16,768]{1,0:T(8,128)S(1)}, u32[]{:S(2)}, u32[]{:S(2)}) collective-permute-start(f32[16,768]{1,0:T(8,128)S(1)} %add.131), channel_id=1, source_target_pairs={{0,32},{8,40},{16,48},{24,56},{32,64},{40,72},{48,80},{56,88},{64,... | collective-permute-start | bytes 147464 | tf_op jit(solution)/shard_map/ppermute | solution.py:197
  127.0 3.5 %collective-permute-start.32 = (f32[16,768]{1,0:T(8,128)S(1)}, f32[16,768]{1,0:T(8,128)S(1)}, u32[]{:S(2)}, u32[]{:S(2)}) collective-permute-start(f32[16,768]{1,0:T(8,128)S(1)} %add.131), channel_id=1, source_target_pairs={{0,96},{8,104},{16,112},{24,120},{32,0},{40,8},{48,16},{56,24},{64... | collective-permute-start | bytes 147464 | tf_op jit(solution)/shard_map/ppermute | solution.py:197
  131.0 3.3 %collective-permute-start.33 = (f32[16,192]{1,0:T(8,128)S(1)}, f32[16,192]{1,0:T(8,128)S(1)}, u32[]{:S(2)}, u32[]{:S(2)}) collective-permute-start(f32[16,192]{1,0:T(8,128)S(1)} %pad_maximum_fusion.7), channel_id=1, source_target_pairs={{0,8},{8,0},{16,24},{24,16},{32,40},{40,32},{48,56},{56,48},{64,72... | collective-permute-start | bytes 36872 | tf_op jit(solution)/shard_map/ppermute | solution.py:190

commit v3 on v2

v3 whole, which is shorter than its diff:
```python
import functools

import jax
import jax.numpy as jnp
from jax import lax
from jax.experimental import pallas as pl
from jax.experimental.pallas import tpu as pltpu
from jax.sharding import PartitionSpec as P

HIGH = lax.Precision.HIGH
NN = (((1,), (0,)), ((), ()))
NT = (((1,), (1,)), ((), ()))


def dot(a, b):
    return jnp.dot(a, b, precision=HIGH)


def dot_nt(a, b):
    return lax.dot_general(a, b, NT, precision=HIGH)


def split(x):
    high = x.astype(jnp.bfloat16)
    return high, (x - high.astype(jnp.float32)).astype(jnp.bfloat16)


def dot_split(a, b, dims):
    rows = a[0].shape[0]
    both = jnp.concatenate(a, axis=0)
    with_high = lax.dot_general(both, b[0], dims, preferred_element_type=jnp.float32)
    with_low = lax.dot_general(a[0], b[1], dims, preferred_element_type=jnp.float32)
    return with_high[:rows] + (with_high[rows:] + with_low)


def in_vmem(count):
    return [pl.BlockSpec(memory_space=pltpu.VMEM)] * count


BIG = pltpu.CompilerParams(vmem_limit_bytes=50 << 20)


def held_pieces(block, which, unit, slots):
    return [
        pltpu.VMEM((slots, which, unit, block), jnp.float32),
        pltpu.SemaphoreType.DMA((slots, which)),
    ]


def dot_cost(rows, inner, outer):
    return pl.CostEstimate(
        flops=6 * rows * inner * outer,
        bytes_accessed=4 * (inner * outer + rows * inner + rows * outer),
        transcendentals=0,
    )


def pair_kernel(core_ref, own_ref, other_ref, o_ref, held, sems):
    _, pair, half = o_ref.shape
    share = pair // 2
    core = core_ref[0]
    where = pl.ds(pl.multiple_of(core * half, 128), half)
    moves = []
    for slot, (source, at) in enumerate(((own_ref, core), (other_ref, 1 - core))):
        to = o_ref.at[:, pl.ds(pl.multiple_of(at * share, 8), share), :]
        step = held.at[slot]
        moves.append(
            (
                pltpu.make_async_copy(source.at[:, :, where], step, sems.at[slot]),
                pltpu.make_async_copy(step, to, sems.at[2 + slot]),
            )
        )
    for fetch, _ in moves:
        fetch.start()
    for fetch, store in moves:
        fetch.wait()
        store.start()
    for _, store in moves:
        store.wait()


def half_pair(own, other, half):
    core = (lax.axis_index("wide") % 2)[None]
    count, share, _ = own.shape
    out = jax.ShapeDtypeStruct((count, 2 * share, half), own.dtype)
    return pl.pallas_call(
        pair_kernel,
        out_shape=out,
        in_specs=[pl.BlockSpec(memory_space=pltpu.SMEM)]
        + [pl.BlockSpec(memory_space=pl.ANY)] * 2,
        out_specs=pl.BlockSpec(memory_space=pl.ANY),
        scratch_shapes=[
            pltpu.VMEM((2, count, share, half), own.dtype),
            pltpu.SemaphoreType.DMA((4,)),
        ],
        compiler_params=pltpu.CompilerParams(vmem_limit_bytes=60 << 20),
        cost_estimate=pl.CostEstimate(
            flops=0, bytes_accessed=out.size, transcendentals=0
        ),
    )(core, own, other)


def streamed(v_ref, held, sems, which, first, count, use):
    unit = held.shape[2]
    slots = held.shape[0]

    def fetches(i):
        where = pl.ds(first + i * unit, unit)
        slot = i % slots
        return [
            pltpu.make_async_copy(
                v_ref.at[w, where, :], held.at[slot, j], sems.at[slot, j]
            )
            for j, w in enumerate(which)
        ]

    def start(i):
        for copy in fetches(i):
            copy.start()

    for i in range(min(slots, count)):
        start(i)
    for i in range(count):
        for copy in fetches(i):
            copy.wait()
        use(i, held.at[i % slots])
        if i + slots < count:
            start(i + slots)


def products_kernel(z_ref, v_ref, flat_ref, p1_ref, p0_ref, held, sems):
    unit = held.shape[2]
    _, per, subs, lanes = z_ref.shape
    sums = [jnp.zeros(p1_ref.shape, jnp.float32) for _ in range(2)]

    def use(i, v_ref):
        columns = []
        for s in range(i * unit // lanes, (i + 1) * unit // lanes):
            rows = [z_ref[:, c, s, :] for c in range(per)]
            columns.append(jnp.concatenate(rows, axis=0))
        z = jnp.concatenate(columns, axis=1)
        flat_ref[:, i * unit : (i + 1) * unit] = z
        z = split(z)
        for which in range(2):
            sums[which] = sums[which] + dot_split(z, split(v_ref[which]), NN)

    streamed(v_ref, held, sems, (0, 1), 0, subs * lanes // unit, use)
    p1_ref[...] = sums[1]
    p0_ref[...] = sums[0]


def products_of(received, reflectors):
    parts, per, subs, lanes = received.shape
    rows = parts * per
    length = subs * lanes
    block = reflectors.shape[2]
    sums = jax.ShapeDtypeStruct((rows, block), jnp.float32)
    return pl.pallas_call(
        products_kernel,
        out_shape=[jax.ShapeDtypeStruct((rows, length), jnp.float32), sums, sums],
        in_specs=in_vmem(1) + [pl.BlockSpec(memory_space=pl.ANY)],
        out_specs=in_vmem(3),
        scratch_shapes=held_pieces(block, 2, 1024, 4),
        compiler_params=BIG,
        cost_estimate=dot_cost(rows, length, 2 * block),
    )(received, reflectors)


def pieces_of(z_ref, z_first, coeffs, v_ref, held, sems, which, first, count, write):
    unit = held.shape[2]
    coeffs = [split(ref[...]) for ref in coeffs]

    def use(i, piece_ref):
        at = z_first + i * unit
        total = z_ref[:, at : at + unit]
        for j, part in enumerate(coeffs):
            total = total - dot_split(part, split(piece_ref[j]), NT)
        write(i, total)

    streamed(v_ref, held, sems, which, first, count, use)


def update_kernel(z_first, first, which, z_ref, v_ref, *refs):
    *coeffs, o_ref, held, sems = refs
    unit = held.shape[2]
    if len(o_ref.shape) == 2:
        count = o_ref.shape[1] // unit

        def write(i, total):
            o_ref[:, i * unit : (i + 1) * unit] = total

    else:
        _, panels, _, half = o_ref.shape
        each = half // unit
        count = 2 * panels * each

        def write(i, total):
            p, h, k = i // (2 * each), (i // each) % 2, i % each
            o_ref[h, p, :, k * unit : (k + 1) * unit] = total

    pieces_of(z_ref, z_first, coeffs, v_ref, held, sems, which, first, count, write)


def updated(z, z_first, coeffs, reflectors, which, first, out, unit):
    block = reflectors.shape[2]
    rows = z.shape[0]
    columns = out[1] if len(out) == 2 else 2 * out[1] * out[3]
    return pl.pallas_call(
        functools.partial(update_kernel, z_first, first, which),
        out_shape=jax.ShapeDtypeStruct(out, jnp.float32),
        in_specs=in_vmem(1) + [pl.BlockSpec(memory_space=pl.ANY)] + in_vmem(len(which)),
        out_specs=in_vmem(1)[0],
        scratch_shapes=held_pieces(block, len(which), unit, 4),
        compiler_params=BIG,
        cost_estimate=dot_cost(rows, len(which) * block, columns),
    )(z, reflectors, *coeffs)


def joined_kernel(first_ref, *refs):
    *pieces, o_ref = refs
    at = first_ref.shape[1]
    o_ref[:, :at] = first_ref[...]
    for ref in pieces:
        half = ref.shape[3]
        for q in range(ref.shape[1]):
            for h in range(2):
                o_ref[:, at : at + half] = ref[h, q]
                at += half


def joined(first, pieces):
    rows = first.shape[0]
    size = first.size + sum(x.size for x in pieces)
    return pl.pallas_call(
        joined_kernel,
        out_shape=jax.ShapeDtypeStruct((rows, size // rows), jnp.float32),
        in_specs=in_vmem(1 + len(pieces)),
        out_specs=in_vmem(1)[0],
        cost_estimate=pl.CostEstimate(
            flops=0, bytes_accessed=8 * size, transcendentals=0
        ),
    )(first, *pieces)


def swapped(array):
    size = lax.axis_size("wide")
    return lax.ppermute(array, "wide", [(i, i ^ 1) for i in range(size)])


def from_chips(array, beside=()):
    size = lax.axis_size("wide")
    array = array + lax.ppermute(array, "wide", [(i, i ^ 2) for i in range(size)])
    array, beside = lax.optimization_barrier((array, beside))
    others = [
        lax.ppermute(array, "wide", [(i, (i + by) % size) for i in range(size)])
        for by in (4, 8, 12)
    ]
    return (array + others[0]) + (others[1] + others[2]), beside


def summed_over_wide(array, beside):
    return from_chips(array + swapped(array), beside)


def from_last_chip(array, is_last, beside):
    size = lax.axis_size("wide")
    array = jnp.where(is_last, array, 0.0)
    last = size - 2
    total = array
    for back in (12, 4, 8):
        pairs = [(last + c, (last + c + back) % size) for c in range(2)]
        total = total + lax.ppermute(array, "wide", pairs)
    pairs = [(i, i ^ 2) for i in range(size) if i & 2]
    total, beside = lax.optimization_barrier((total, beside))
    return total, total + lax.ppermute(total, "wide", pairs), beside


def own_half(halves):
    is_owner = lax.axis_index("wide") == lax.axis_size("wide") - 1
    return jnp.where(is_owner, halves[1], swapped(halves[0]))


def solve_chain(remain, rest, d_pair, l_pair, is_last, late, fillers):
    panels, pair_cols, _ = d_pair.shape
    share = pair_cols // 2
    pending = []
    for piece in rest:
        owned = own_half(piece)
        pending += [jnp.where(is_last, x, 0.0) for x in owned]
    first_core = lax.axis_index("wide") % 2 == 0
    results = [None] * panels
    for source in reversed(range(panels)):
        part = dot_nt(remain, d_pair[source])
        pair = part + swapped(part)
        results[source] = jnp.where(first_core, pair[:, :share], pair[:, share:])
        offset = source * (source - 1) // 2
        for target in reversed(range(source)):
            pending[target] = pending[target] - dot(pair, l_pair[offset + target])
        if source > 0:
            urgent, late = lax.optimization_barrier((pending[source - 1], late))
            late = fillers[panels - 1 - source](late)
            remain, late = from_chips(urgent, late)
    return late, jnp.stack(results, axis=1)


def gram_of(reflectors, lo, hi):
    return lax.dot_general(
        reflectors[1, lo:hi],
        reflectors[0, lo:hi],
        (((0,), (0,)), ((), ())),
        precision=HIGH,
    )


def body(tridiag_vectors, reflectors, triangles, lower_blocks, diag_inverses):
    wide_size = lax.axis_size("wide")
    narrow_size = lax.axis_size("narrow")
    _, length, block = reflectors.shape
    panels, panel_rows, _ = diag_inverses.shape
    half = panel_rows // 2
    subs = length // 128
    last = length - panel_rows
    is_owner = lax.axis_index("wide") == wide_size - 1
    weights = (jnp.swapaxes(diag_inverses, 1, 2), lower_blocks)
    traded = [swapped(array) for array in weights]

    received = tridiag_vectors.reshape(wide_size, subs, 128)
    received = lax.all_to_all(received, "wide", 0, 0, tiled=True)
    gram = gram_of(reflectors, 0, length // 2)
    gram, early = lax.optimization_barrier((gram, reflectors))
    v_low = early[:, last : last + half]
    received, gram, v_low = lax.optimization_barrier((received, gram, v_low))
    v_low = swapped(v_low)
    received, later = lax.optimization_barrier((received, reflectors))
    received = lax.all_to_all(received, "narrow", 0, 0, tiled=True)
    gram = gram + gram_of(later, length // 2, length)
    v_mine = jnp.where(is_owner, reflectors[:, last + half :], v_low)
    received, gram, v_mine = lax.optimization_barrier((received, gram, v_mine))
    per = wide_size // narrow_size
    received = received.reshape(narrow_size, per, subs, 128)
    flat, first, second = products_of(received, reflectors)
    z_mine = jnp.where(is_owner, flat[:, last + half :], swapped(flat[:, last : last + half]))
    first, weights, traded = lax.optimization_barrier((first, weights, traded))
    first, l_pair = summed_over_wide(first, half_pair(weights[1], traded[1], half))
    coeffs1 = dot(first, triangles[1].T)
    second = second - dot(coeffs1, gram)
    second, weights, traded = lax.optimization_barrier((second, weights, traded))
    second, d_pair = summed_over_wide(second, half_pair(weights[0], traded[0], half))
    z_mine = z_mine - dot_nt(coeffs1, v_mine[1])
    second, z_mine = lax.optimization_barrier((second, z_mine))
    coeffs0 = dot(second, triangles[0].T)
    corner = z_mine - dot_nt(coeffs0, v_mine[0])

    is_last = lax.axis_index("wide") >= wide_size - 2
    start = length - panels * panel_rows
    ends = last - panel_rows
    rows = flat.shape[0]

    def update(coeffs, first, out, unit=half):
        return updated(flat, first, coeffs, reflectors, (1, 0), first, out, unit)

    corner, late0 = lax.optimization_barrier((corner, coeffs0))
    piece2 = update([coeffs1, late0], ends, (2, 1, rows, half))
    near, remain, piece2 = from_last_chip(corner, is_last, piece2)
    near, late0 = lax.optimization_barrier((near, late0))
    rest = update([coeffs1, late0], start, (2, panels - 2, rows, half))
    remain, rest, late0 = lax.optimization_barrier((remain, rest, late0))

    def fill_first(late):
        return late, update([coeffs1, late], 0, (rows, start), 512)

    def fill_last(late):
        late, first = late
        return first, update([coeffs1, late], last, (2, 1, rows, half))

    def fill_join(late):
        first, piece3 = late
        return joined(first, [rest, piece2, piece3])

    fillers = [fill_first, fill_last, fill_join]
    transformed, solved = solve_chain(
        remain, [rest, piece2], d_pair, l_pair, is_last, late0, fillers
    )
    return (transformed, solved)


def solution(mesh):
    placed = (
        P(("wide", "narrow"), None),
        P(None, "wide", None),
        P(),
        P(None, "wide", None),
        P(None, None, "wide"),
    )
    return jax.shard_map(
        body,
        mesh=mesh,
        in_specs=placed,
        out_specs=(P("narrow", "wide"), P("narrow", None, "wide")),
        check_vma=False,
    )
```

time: 135 us -> 129 us (0.956)
  waiting for transfers between devices: 31.5 us -> 22.5 us
  Pallas kernels: 19 us -> 26.2 us
  local copies, waits for them, and re-layouts: 5.98 us -> 2.2 us
  starting transfers between devices: 57.6 us -> 55.5 us
    pallas_call x3 -> x7, Pallas kernels: 12.6 us -> 19.7 us  [the longest x4 11.7 us: updated(): pl.pallas_call(functools.partial(update_kernel, z_first, first, which), o...]
    ppermute x5, waiting for transfers between devices: 7.08 us -> 0.23 us  [from_chips(): lax.ppermute(array, 'wide', [(i, i ^ 2) for i in range(size)])]
    ppermute x15, starting transfers between devices: 18.6 us -> 13.8 us  [from_chips(): lax.ppermute(array, 'wide', [(i, (i + by) % size) for i in range(size)])]
    dynamic_slice x4 -> x0, local copies, waits for them, and re-layouts: 4.72 us -> none  [half_pairs(): lax.dynamic_slice_in_dim(x, mine, half, 2)]
    ppermute x15, waiting for transfers between devices: 11.1 us -> 14.8 us  [from_chips(): lax.ppermute(array, 'wide', [(i, (i + by) % size) for i in range(size)])]
    ppermute x1, waiting for transfers between devices: 3.08 us -> 0.01 us  [from_last_chip(): return (total, total + lax.ppermute(total, 'wide', pairs), beside)]
    concatenate x7 -> x0, other arithmetic: 2.62 us -> none  [the longest x2 2.31 us: half_pairs(): jnp.concatenate([lax.dynamic_slice_in_dim(x, mine, half, 2) for x in (arr...]
    select_n x0 -> x1, other arithmetic: none -> 2.09 us  [body(): v_mine = jnp.where(is_owner, reflectors[:, last + half:], v_low)]
  transfers between devices with their start and end apart: 36 -> 38, of which waited for: 26 -> 19; matrix products, arithmetic and copies ran while one was open for 14% -> 16% of each run, Pallas kernels for 12% -> 20%
where the time goes in v3:
time: 129 us; the launch traced here: 128 us
  starting transfers between devices  55.5 us (43%)
  Pallas kernels  26.2 us (20%)
  waiting for transfers between devices  22.5 us (17%)
  matrix products  18.1 us (14%)
  other arithmetic  2.53 us (2%)
  local copies, waits for them, and re-layouts  2.2 us (2%)
    ppermute x12, starting transfers between devices, swapped(): return lax.ppermute(array, 'wide', [(i, i ^ 1) for i in range(size)])  21.1 us
    ppermute x15, waiting for transfers between devices, from_chips(): lax.ppermute(array, 'wide', [(i, (i + by) % size) for i in range(size)])  14.8 us
    ppermute x15, starting transfers between devices, from_chips(): lax.ppermute(array, 'wide', [(i, (i + by) % size) for i in range(size)])  13.8 us
    dot_general x2, matrix products, gram_of(): lax.dot_general(reflectors[1, lo:hi], reflectors[0, lo:hi], (((0,), (0,))...  13.8 us
    pallas_call x4, Pallas kernels, updated(): pl.pallas_call(functools.partial(update_kernel, z_first, first, which), o...  11.7 us
    pallas_call x1, Pallas kernels, products_of(): pl.pallas_call(products_kernel, out_shape=[jax.ShapeDtypeStruct((rows, le...  6.57 us
    all_to_all x1, starting transfers between devices, body(): received = lax.all_to_all(received, 'wide', 0, 0, tiled=True)  6.54 us
    all_to_all x1, starting transfers between devices, body(): received = lax.all_to_all(received, 'narrow', 0, 0, tiled=True)  6.36 us
  transfers between devices with their start and end apart: 38, of which 19 were waited for; matrix products, arithmetic and copies ran while one was open for 16% of the time, Pallas kernels for 20%

profile of v3, /device:TPU:1, one launch (start us, length us, event | category | flops | bytes accessed | tf_op | source)
XLA Modules:
  0.0 128.1 jit_solution(6599186012746865363)
XLA Ops:
  0.6 1.5 %collective-permute-start.2 = (f32[6,96,1536]{2,1,0:T(8,128)}, f32[6,96,1536]{2,1,0:T(8,128)}, u32[]{:S(2)}, u32[]{:S(2)}) collective-permute-start(f32[6,96,1536]{2,1,0:T(8,128)} %own_ref), channel_id=1, source_target_pairs={{0,8},{8,0},{16,24},{24,16},{32,40},{40,32},{48,56},{56,48},{64,72... | collective-permute-start | bytes 10616840 | tf_op jit(solution)/shard_map/ppermute | solution.py:247
  2.1 6.5 %all-to-all-start = ((f32[16,64,128]{2,1,0:T(8,128)}), f32[16,64,128]{2,1,0:T(8,128)}, u32[]{:S(2)}, u32[]{:S(2)}) async-start(f32[16,64,128]{2,1,0:T(8,128)} %bitcast.121), calls=%async_computation | async-start | bytes 1048576 | tf_op jit(solution)/shard_map/all_to_all | solution.py:328
  8.9 6.9 %fusion.3 = f32[256,256]{1,0:T(8,128)S(1)} fusion(f32[2,8192,256]{2,1,0:T(8,128)} %v_ref.9), kind=kOutput, calls=%fused_computation.3 | convolution fusion | flops 1610612736 | bytes 8650752 | tf_op jit(solution)/shard_map/dot_general | solution.py:307
  15.8 1.5 %slice.104 = f32[2,768,256]{2,1,0:T(8,128)S(1)} slice(f32[2,8192,256]{2,1,0:T(8,128)} %v_ref.9), slice={[0:2], [6656:7424], [0:256]} | slice | bytes 3145728 | tf_op jit(solution)/shard_map/slice | solution.py:331
  17.3 1.3 all-to-all-done
  18.6 1.2 collective-permute-start
  19.7 6.4 %all-to-all-start.1 = ((f32[16,64,128]{2,1,0:T(8,128)}), f32[16,64,128]{2,1,0:T(8,128)S(1)}, u32[]{:S(2)}, u32[]{:S(2)}) async-start(f32[16,64,128]{2,1,0:T(8,128)} %all-to-all-done), calls=%async_computation.1 | async-start | bytes 1048576 | tf_op jit(solution)/shard_map/all_to_all | solution.py:335
  26.1 6.9 %fusion.10 = f32[256,256]{1,0:T(8,128)S(1)} fusion(f32[256,256]{1,0:T(8,128)S(1)} %fusion.3, f32[2,8192,256]{2,1,0:T(8,128)} %v_ref.9), kind=kOutput, calls=%fused_computation.11 | convolution fusion | flops 1610678272 | bytes 8912896 | tf_op jit(solution)/shard_map/dot_general | solution.py:307
  33.0 2.1 %slice_select_fusion = f32[2,768,256]{2,1,0:T(8,128)S(1)} fusion(f32[2,768,256]{2,1,0:T(8,128)} %collective-permute-done, f32[2,8192,256]{2,1,0:T(8,128)} %v_ref.9, pred[]{:T(512)S(6)} %eq.12), kind=kLoop, calls=%fused_computation.10 | loop fusion | flops 393216 | bytes 4718593 | tf_op jit(solution)/shard_map/jit(_where)/select_n | solution.py:337
  35.1 1.5 %all-to-all-done.1 = f32[16,64,128]{2,1,0:T(8,128)S(1)} async-done(((f32[16,64,128]{2,1,0:T(8,128)}), f32[16,64,128]{2,1,0:T(8,128)S(1)}, u32[]{:S(2)}, u32[]{:S(2)}) %all-to-all-start.1) | async-done | bytes 524320 | tf_op jit(solution)/shard_map/all_to_all | solution.py:335
  36.6 6.6 %shard_map.68 = (f32[16,8192]{1,0:T(8,128)S(1)}, f32[16,256]{1,0:T(8,128)S(1)}, f32[16,256]{1,0:T(8,128)S(1)}) custom-call(f32[8,2,64,128]{3,2,1,0:T(8,128)S(1)} %bitcast.118, f32[2,8192,256]{2,1,0:T(8,128)} %v_ref.9), custom_call_target="tpu_custom_call" | custom-call | flops 402653184 | bytes 17334272 | tf_op jit(solution)/shard_map/pallas_call | solution.py:158
  43.2 1.1 collective-permute-start.3
  44.3 0.8 collective-permute-done.3
  45.2 3.3 %shard_map.69 = f32[6,192,768]{2,1,0:T(8,128)} custom-call(s32[1]{0:T(128)} %bitcast.7.core_ref, f32[6,96,1536]{2,1,0:T(8,128)} %own_ref, f32[6,96,1536]{2,1,0:T(8,128)} %collective-permute-done.2.other_ref), custom_call_target="tpu_custom_call" | custom-call | bytes 884736 | tf_op jit(solution)/shard_map/pallas_call | solution.py:86
  48.6 1.9 %collective-permute-start.6 = (f32[16,256]{1,0:T(8,128)S(1)}, f32[16,256]{1,0:T(8,128)S(1)}, u32[]{:S(2)}, u32[]{:S(2)}) collective-permute-start(f32[16,256]{1,0:T(8,128)S(1)} %add.101), channel_id=1, source_target_pairs={{0,64},{8,72},{16,80},{24,88},{32,96},{40,104},{48,112},{56,120},{... | collective-permute-start | bytes 49160 | tf_op jit(solution)/shard_map/ppermute | solution.py:255
  50.5 0.9 collective-permute-start.7
  51.4 0.6 collective-permute-start.5
  52.0 1.5 %collective-permute-start.13 = (f32[16,768]{1,0:T(8,128)S(1)}, f32[16,768]{1,0:T(8,128)S(1)}, u32[]{:S(2)}, u32[]{:S(2)}) collective-permute-start(f32[16,768]{1,0:T(8,128)S(1)} %slice.110), channel_id=1, source_target_pairs={{0,8},{8,0},{16,24},{24,16},{32,40},{40,32},{48,56},{56,48},{64,72... | collective-permute-start | bytes 147464 | tf_op jit(solution)/shard_map/ppermute | solution.py:247
  53.5 1.7 %collective-permute-done.5 = f32[16,256]{1,0:T(8,128)S(1)} collective-permute-done((f32[16,256]{1,0:T(8,128)S(1)}, f32[16,256]{1,0:T(8,128)S(1)}, u32[]{:S(2)}, u32[]{:S(2)}) %collective-permute-start.5) | collective-permute-done | bytes 16416 | tf_op jit(solution)/shard_map/ppermute | solution.py:255
  55.6 2.4 %collective-permute-start.8 = (f32[16,256]{1,0:T(8,128)S(1)}, f32[16,256]{1,0:T(8,128)S(1)}, u32[]{:S(2)}, u32[]{:S(2)}) collective-permute-start(f32[16,256]{1,0:T(8,128)S(1)} %convolution_subtract_fusion), channel_id=1, source_target_pairs={{0,8},{8,0},{16,24},{24,16},{32,40},{40,32},{48,56},{56,48},{64,72... | collective-permute-start | bytes 49160 | tf_op jit(solution)/shard_map/ppermute | solution.py:247
  58.0 0.8 collective-permute-done.8
  58.9 0.9 collective-permute-start.9
  59.7 2.7 %shard_map.70 = f32[4,192,768]{2,1,0:T(8,128)} custom-call(s32[1]{0:T(128)} %bitcast.7.core_ref, f32[4,96,1536]{2,1,0:T(8,128)} %bitcast.120, f32[4,96,1536]{2,1,0:T(8,128)} %collective-permute-done.1.other_ref), custom_call_target="tpu_custom_call" | custom-call | bytes 589824 | tf_op jit(solution)/shard_map/pallas_call | solution.py:86
  62.6 1.7 %collective-permute-start.12 = (f32[16,256]{1,0:T(8,128)S(1)}, f32[16,256]{1,0:T(8,128)S(1)}, u32[]{:S(2)}, u32[]{:S(2)}) collective-permute-start(f32[16,256]{1,0:T(8,128)S(1)} %add.107), channel_id=1, source_target_pairs={{0,96},{8,104},{16,112},{24,120},{32,0},{40,8},{48,16},{56,24},{64... | collective-permute-start | bytes 49160 | tf_op jit(solution)/shard_map/ppermute | solution.py:255
  64.4 0.5 select_subtract_fusion
  64.8 1.9 %collective-permute-done.11 = f32[16,256]{1,0:T(8,128)S(1)} collective-permute-done((f32[16,256]{1,0:T(8,128)S(1)}, f32[16,256]{1,0:T(8,128)S(1)}, u32[]{:S(2)}, u32[]{:S(2)}) %collective-permute-start.11) | collective-permute-done | bytes 16416 | tf_op jit(solution)/shard_map/ppermute | solution.py:255
  66.7 1.5 %collective-permute-done.10 = f32[16,256]{1,0:T(8,128)S(1)} collective-permute-done((f32[16,256]{1,0:T(8,128)S(1)}, f32[16,256]{1,0:T(8,128)S(1)}, u32[]{:S(2)}, u32[]{:S(2)}) %collective-permute-start.10) | collective-permute-done | bytes 16416 | tf_op jit(solution)/shard_map/ppermute | solution.py:255
  68.3 0.5 fusion.15
  68.9 0.7 collective-permute-start.16
  69.6 0.7 collective-permute-start.15
  70.2 0.7 collective-permute-start.14
  70.9 2.5 %shard_map.71.refs_1_ = f32[2,1,16,768]{3,2,1,0:T(8,128)S(1)} custom-call(f32[16,8192]{1,0:T(8,128)S(1)} %get-tuple-element.74.z_ref, f32[2,8192,256]{2,1,0:T(8,128)} %v_ref.9, f32[16,256]{1,0:T(8,128)S(1)} %fusion.53.refs_0_, f32[16,256]{1,0:T(8,128)S(1)} %fusion.51.refs_1_), custom_call_target="tpu_custom_call" | custom-call | flops 75497472 | bytes 3276800 | tf_op jit(solution)/shard_map/pallas_call | solution.py:208
  73.5 1.3 %collective-permute-start.17 = (f32[16,768]{1,0:T(8,128)S(1)}, f32[16,768]{1,0:T(8,128)S(1)}, u32[]{:S(2)}, u32[]{:S(2)}) collective-permute-start(f32[16,768]{1,0:T(8,128)S(1)} %add_add_fusion), channel_id=1, source_target_pairs={{16,0},{24,8},{48,32},{56,40},{80,64},{88,72},{112,96},{120,104},{... | collective-permute-start | bytes 147464 | tf_op jit(solution)/shard_map/ppermute | solution.py:275
  74.8 2.4 %collective-permute-start.20 = (f32[1,16,768]{2,1,0:T(8,128)S(1)}, f32[1,16,768]{2,1,0:T(8,128)S(1)}, u32[]{:S(2)}, u32[]{:S(2)}) collective-permute-start(f32[1,16,768]{2,1,0:T(8,128)S(1)} %slice_bitcast_fusion.1), channel_id=1, source_target_pairs={{0,8},{8,0},{16,24},{24,16},{32,40},{40,32},{48,56},{56,48},{64,72... | collective-permute-start | bytes 147464 | tf_op jit(solution)/shard_map/ppermute | solution.py:247
  77.2 3.6 %shard_map.72.refs_0_ = f32[2,2,16,768]{3,2,1,0:T(8,128)S(1)} custom-call(f32[16,8192]{1,0:T(8,128)S(1)} %get-tuple-element.74.z_ref, f32[2,8192,256]{2,1,0:T(8,128)} %v_ref.9, f32[16,256]{1,0:T(8,128)S(1)} %fusion.53.refs_0_, f32[16,256]{1,0:T(8,128)S(1)} %fusion.51.refs_1_), custom_call_target="tpu_custom_call" | custom-call | flops 150994944 | bytes 6520832 | tf_op jit(solution)/shard_map/pallas_call | solution.py:208
  81.2 2.6 %collective-permute-start.19 = (f32[16,192]{1,0:T(8,128)S(1)}, f32[16,192]{1,0:T(8,128)S(1)}, u32[]{:S(2)}, u32[]{:S(2)}) collective-permute-start(f32[16,192]{1,0:T(8,128)S(1)} %fusion.39), channel_id=1, source_target_pairs={{0,8},{8,0},{16,24},{24,16},{32,40},{40,32},{48,56},{56,48},{64,72... | collective-permute-start | bytes 36872 | tf_op jit(solution)/shard_map/ppermute | solution.py:247
  83.8 0.8 collective-permute-done.19
  84.9 1.8 %collective-permute-start.21 = (f32[16,768]{1,0:T(8,128)S(1)}, f32[16,768]{1,0:T(8,128)S(1)}, u32[]{:S(2)}, u32[]{:S(2)}) collective-permute-start(f32[16,768]{1,0:T(8,128)S(1)} %bitcast_subtract_fusion), channel_id=1, source_target_pairs={{0,16},{8,24},{16,0},{24,8},{32,48},{40,56},{48,32},{56,40},{64,80... | collective-permute-start | bytes 147464 | tf_op jit(solution)/shard_map/ppermute | solution.py:252
  86.7 0.5 collective-permute-start.18
  87.3 2.9 %shard_map.73.first_ref = f32[16,2048]{1,0:T(8,128)S(1)} custom-call(f32[16,8192]{1,0:T(8,128)S(1)} %get-tuple-element.74.z_ref, f32[2,8192,256]{2,1,0:T(8,128)} %v_ref.9, f32[16,256]{1,0:T(8,128)S(1)} %fusion.53.refs_0_, f32[16,256]{1,0:T(8,128)S(1)} %fusion.51.refs_1_), custom_call_target="tpu_custom_call" | custom-call | flops 100663296 | bytes 4358144 | tf_op jit(solution)/shard_map/pallas_call | solution.py:208
  90.2 2.6 %collective-permute-start.23 = (f32[16,768]{1,0:T(8,128)S(1)}, f32[16,768]{1,0:T(8,128)S(1)}, u32[]{:S(2)}, u32[]{:S(2)}) collective-permute-start(f32[16,768]{1,0:T(8,128)S(1)} %add.116), channel_id=1, source_target_pairs={{0,64},{8,72},{16,80},{24,88},{32,96},{40,104},{48,112},{56,120},{... | collective-permute-start | bytes 147464 | tf_op jit(solution)/shard_map/ppermute | solution.py:255
  92.8 1.5 %collective-permute-start.22 = (f32[16,768]{1,0:T(8,128)S(1)}, f32[16,768]{1,0:T(8,128)S(1)}, u32[]{:S(2)}, u32[]{:S(2)}) collective-permute-start(f32[16,768]{1,0:T(8,128)S(1)} %add.116), channel_id=1, source_target_pairs={{0,32},{8,40},{16,48},{24,56},{32,64},{40,72},{48,80},{56,88},{64,... | collective-permute-start | bytes 147464 | tf_op jit(solution)/shard_map/ppermute | solution.py:255
  94.5 0.6 collective-permute-done.23
  95.1 0.6 collective-permute-done.24
  95.7 1.2 collective-permute-done.22
  97.2 1.6 %collective-permute-start.25 = (f32[16,192]{1,0:T(8,128)S(1)}, f32[16,192]{1,0:T(8,128)S(1)}, u32[]{:S(2)}, u32[]{:S(2)}) collective-permute-start(f32[16,192]{1,0:T(8,128)S(1)} %fusion.33), channel_id=1, source_target_pairs={{0,8},{8,0},{16,24},{24,16},{32,40},{40,32},{48,56},{56,48},{64,72... | collective-permute-start | bytes 36872 | tf_op jit(solution)/shard_map/ppermute | solution.py:247
  98.8 0.8 collective-permute-done.25
  99.9 0.8 collective-permute-start.26
  100.7 2.7 %shard_map.74.refs_2_ = f32[2,1,16,768]{3,2,1,0:T(8,128)S(1)} custom-call(f32[16,8192]{1,0:T(8,128)S(1)} %get-tuple-element.74.z_ref, f32[2,8192,256]{2,1,0:T(8,128)} %v_ref.9, f32[16,256]{1,0:T(8,128)S(1)} %fusion.53.refs_0_, f32[16,256]{1,0:T(8,128)S(1)} %fusion.51.refs_1_), custom_call_target="tpu_custom_call" | custom-call | flops 75497472 | bytes 3276800 | tf_op jit(solution)/shard_map/pallas_call | solution.py:208
  103.4 0.8 collective-permute-start.28
  104.3 2.2 %collective-permute-start.29 = (f32[16,768]{1,0:T(8,128)S(1)}, f32[16,768]{1,0:T(8,128)S(1)}, u32[]{:S(2)}, u32[]{:S(2)}) collective-permute-start(f32[16,768]{1,0:T(8,128)S(1)} %add.121), channel_id=1, source_target_pairs={{0,96},{8,104},{16,112},{24,120},{32,0},{40,8},{48,16},{56,24},{64... | collective-permute-start | bytes 147464 | tf_op jit(solution)/shard_map/ppermute | solution.py:255
  106.7 1.2 collective-permute-done.28
  108.0 2.6 %collective-permute-done.27 = f32[16,768]{1,0:T(8,128)S(1)} collective-permute-done((f32[16,768]{1,0:T(8,128)S(1)}, f32[16,768]{1,0:T(8,128)S(1)}, u32[]{:S(2)}, u32[]{:S(2)}) %collective-permute-start.27) | collective-permute-done | bytes 49184 | tf_op jit(solution)/shard_map/ppermute | solution.py:255
  110.9 2.8 %collective-permute-start.30 = (f32[16,192]{1,0:T(8,128)S(1)}, f32[16,192]{1,0:T(8,128)S(1)}, u32[]{:S(2)}, u32[]{:S(2)}) collective-permute-start(f32[16,192]{1,0:T(8,128)S(1)} %fusion.25), channel_id=1, source_target_pairs={{0,8},{8,0},{16,24},{24,16},{32,40},{40,32},{48,56},{56,48},{64,72... | collective-permute-start | bytes 36872 | tf_op jit(solution)/shard_map/ppermute | solution.py:247
  114.0 0.6 collective-permute-done.30
  114.8 0.8 collective-permute-start.31
  115.7 1.9 %shard_map.75 = f32[16,8192]{1,0:T(8,128)} custom-call(f32[16,2048]{1,0:T(8,128)} %copy-done.2, f32[2,2,16,768]{3,2,1,0:T(8,128)} %copy-done, f32[2,1,16,768]{3,2,1,0:T(8,128)} %copy-done.1, f32[2,1,16,768]{3,2,1,0:T(8,128)} %copy-done.3), custom_call_target="tpu_custom_call" | custom-call | bytes 1048576 | tf_op jit(solution)/shard_map/pallas_call | solution.py:234
  117.9 0.9 collective-permute-start.34
  118.8 0.6 collective-permute-start.32
  119.5 2.8 %collective-permute-done.33 = f32[16,768]{1,0:T(8,128)S(1)} collective-permute-done((f32[16,768]{1,0:T(8,128)S(1)}, f32[16,768]{1,0:T(8,128)S(1)}, u32[]{:S(2)}, u32[]{:S(2)}) %collective-permute-start.33) | collective-permute-done | bytes 49184 | tf_op jit(solution)/shard_map/ppermute | solution.py:255
  122.3 0.6 collective-permute-done.32
  123.2 3.3 %collective-permute-start.35 = (f32[16,192]{1,0:T(8,128)S(1)}, f32[16,192]{1,0:T(8,128)S(1)}, u32[]{:S(2)}, u32[]{:S(2)}) collective-permute-start(f32[16,192]{1,0:T(8,128)S(1)} %fusion.21), channel_id=1, source_target_pairs={{0,8},{8,0},{16,24},{24,16},{32,40},{40,32},{48,56},{56,48},{64,72... | collective-permute-start | bytes 36872 | tf_op jit(solution)/shard_map/ppermute | solution.py:247
  126.6 0.8 collective-permute-done.35
  127.5 0.6 copy.7
  (81 shorter events, 4.6 us)
Async XLA Ops:
  0.6 42.5 %collective-permute-start.2 = (f32[6,96,1536]{2,1,0:T(8,128)}, f32[6,96,1536]{2,1,0:T(8,128)}, u32[]{:S(2)}, u32[]{:S(2)}) collective-permute-start(f32[6,96,1536]{2,1,0:T(8,128)} %own_ref), channel_id=1, source_target_pairs={{0,8},{8,0},{16,24},{24,16},{32,40},{40,32},{48,56},{56,48},{64,72... | collective-permute-start | bytes 10616840 | tf_op jit(solution)/shard_map/ppermute | solution.py:247
  2.1 16.4 %all-to-all-start = ((f32[16,64,128]{2,1,0:T(8,128)}), f32[16,64,128]{2,1,0:T(8,128)}, u32[]{:S(2)}, u32[]{:S(2)}) async-start(f32[16,64,128]{2,1,0:T(8,128)} %bitcast.121), calls=%async_computation | async-start | bytes 1048576 | tf_op jit(solution)/shard_map/all_to_all | solution.py:328
  8.7 34.5 %collective-permute-start.1 = (f32[4,96,1536]{2,1,0:T(8,128)}, f32[4,96,1536]{2,1,0:T(8,128)}, u32[]{:S(2)}, u32[]{:S(2)}) collective-permute-start(f32[4,96,1536]{2,1,0:T(8,128)} %bitcast.119), channel_id=1, source_target_pairs={{0,8},{8,0},{16,24},{24,16},{32,40},{40,32},{48,56},{56,48},{64,72... | collective-permute-start | bytes 7077896 | tf_op jit(solution)/shard_map/ppermute | solution.py:247
  18.6 14.4 %collective-permute-start = (f32[2,768,256]{2,1,0:T(8,128)S(1)}, f32[2,768,256]{2,1,0:T(8,128)}, u32[]{:S(2)}, u32[]{:S(2)}) collective-permute-start(f32[2,768,256]{2,1,0:T(8,128)S(1)} %slice.104), channel_id=1, source_target_pairs={{0,8},{8,0},{16,24},{24,16},{32,40},{40,32},{48,56},{56,48},{64,72... | collective-permute-start | bytes 4718600 | tf_op jit(solution)/shard_map/ppermute | solution.py:247
  19.7 16.8 %all-to-all-start.1 = ((f32[16,64,128]{2,1,0:T(8,128)}), f32[16,64,128]{2,1,0:T(8,128)S(1)}, u32[]{:S(2)}, u32[]{:S(2)}) async-start(f32[16,64,128]{2,1,0:T(8,128)} %all-to-all-done), calls=%async_computation.1 | async-start | bytes 1048576 | tf_op jit(solution)/shard_map/all_to_all | solution.py:335
  43.2 2.0 %collective-permute-start.3 = (f32[16,256]{1,0:T(8,128)S(1)}, f32[16,256]{1,0:T(8,128)S(1)}, u32[]{:S(2)}, u32[]{:S(2)}) collective-permute-start(f32[16,256]{1,0:T(8,128)S(1)} %get-tuple-element.63), channel_id=1, source_target_pairs={{0,8},{8,0},{16,24},{24,16},{32,40},{40,32},{48,56},{56,48},{64,72... | collective-permute-start | bytes 49160 | tf_op jit(solution)/shard_map/ppermute | solution.py:247
  45.2 3.4 %collective-permute-start.4 = (f32[16,256]{1,0:T(8,128)S(1)}, f32[16,256]{1,0:T(8,128)S(1)}, u32[]{:S(2)}, u32[]{:S(2)}) collective-permute-start(f32[16,256]{1,0:T(8,128)S(1)} %add.100), channel_id=1, source_target_pairs={{0,16},{8,24},{16,0},{24,8},{32,48},{40,56},{48,32},{56,40},{64,80... | collective-permute-start | bytes 49160 | tf_op jit(solution)/shard_map/ppermute | solution.py:252
  45.2 9.9 %copy-start.7 = (f32[2,256,256]{2,1,0:T(8,128)S(1)}, f32[2,256,256]{2,1,0:T(8,128)}, u32[]{:S(2)}) copy-start(f32[2,256,256]{2,1,0:T(8,128)} %param.7) | copy-start | bytes 1572868
  48.6 4.9 %collective-permute-start.6 = (f32[16,256]{1,0:T(8,128)S(1)}, f32[16,256]{1,0:T(8,128)S(1)}, u32[]{:S(2)}, u32[]{:S(2)}) collective-permute-start(f32[16,256]{1,0:T(8,128)S(1)} %add.101), channel_id=1, source_target_pairs={{0,64},{8,72},{16,80},{24,88},{32,96},{40,104},{48,112},{56,120},{... | collective-permute-start | bytes 49160 | tf_op jit(solution)/shard_map/ppermute | solution.py:255
  50.5 3.0 %collective-permute-start.7 = (f32[16,256]{1,0:T(8,128)S(1)}, f32[16,256]{1,0:T(8,128)S(1)}, u32[]{:S(2)}, u32[]{:S(2)}) collective-permute-start(f32[16,256]{1,0:T(8,128)S(1)} %add.101), channel_id=1, source_target_pairs={{0,96},{8,104},{16,112},{24,120},{32,0},{40,8},{48,16},{56,24},{64... | collective-permute-start | bytes 49160 | tf_op jit(solution)/shard_map/ppermute | solution.py:255
  51.4 3.8 %collective-permute-start.5 = (f32[16,256]{1,0:T(8,128)S(1)}, f32[16,256]{1,0:T(8,128)S(1)}, u32[]{:S(2)}, u32[]{:S(2)}) collective-permute-start(f32[16,256]{1,0:T(8,128)S(1)} %add.101), channel_id=1, source_target_pairs={{0,32},{8,40},{16,48},{24,56},{32,64},{40,72},{48,80},{56,88},{64,... | collective-permute-start | bytes 49160 | tf_op jit(solution)/shard_map/ppermute | solution.py:255
  52.0 12.4 %collective-permute-start.13 = (f32[16,768]{1,0:T(8,128)S(1)}, f32[16,768]{1,0:T(8,128)S(1)}, u32[]{:S(2)}, u32[]{:S(2)}) collective-permute-start(f32[16,768]{1,0:T(8,128)S(1)} %slice.110), channel_id=1, source_target_pairs={{0,8},{8,0},{16,24},{24,16},{32,40},{40,32},{48,56},{56,48},{64,72... | collective-permute-start | bytes 147464 | tf_op jit(solution)/shard_map/ppermute | solution.py:247
  55.6 3.3 %collective-permute-start.8 = (f32[16,256]{1,0:T(8,128)S(1)}, f32[16,256]{1,0:T(8,128)S(1)}, u32[]{:S(2)}, u32[]{:S(2)}) collective-permute-start(f32[16,256]{1,0:T(8,128)S(1)} %convolution_subtract_fusion), channel_id=1, source_target_pairs={{0,8},{8,0},{16,24},{24,16},{32,40},{40,32},{48,56},{56,48},{64,72... | collective-permute-start | bytes 49160 | tf_op jit(solution)/shard_map/ppermute | solution.py:247
  58.9 3.6 %collective-permute-start.9 = (f32[16,256]{1,0:T(8,128)S(1)}, f32[16,256]{1,0:T(8,128)S(1)}, u32[]{:S(2)}, u32[]{:S(2)}) collective-permute-start(f32[16,256]{1,0:T(8,128)S(1)} %add.106), channel_id=1, source_target_pairs={{0,16},{8,24},{16,0},{24,8},{32,48},{40,56},{48,32},{56,40},{64,80... | collective-permute-start | bytes 49160 | tf_op jit(solution)/shard_map/ppermute | solution.py:252
  62.5 4.2 %collective-permute-start.11 = (f32[16,256]{1,0:T(8,128)S(1)}, f32[16,256]{1,0:T(8,128)S(1)}, u32[]{:S(2)}, u32[]{:S(2)}) collective-permute-start(f32[16,256]{1,0:T(8,128)S(1)} %add.107), channel_id=1, source_target_pairs={{0,64},{8,72},{16,80},{24,88},{32,96},{40,104},{48,112},{56,120},{... | collective-permute-start | bytes 49160 | tf_op jit(solution)/shard_map/ppermute | solution.py:255
  62.6 4.1 %collective-permute-start.12 = (f32[16,256]{1,0:T(8,128)S(1)}, f32[16,256]{1,0:T(8,128)S(1)}, u32[]{:S(2)}, u32[]{:S(2)}) collective-permute-start(f32[16,256]{1,0:T(8,128)S(1)} %add.107), channel_id=1, source_target_pairs={{0,96},{8,104},{16,112},{24,120},{32,0},{40,8},{48,16},{56,24},{64... | collective-permute-start | bytes 49160 | tf_op jit(solution)/shard_map/ppermute | solution.py:255
  64.3 3.8 %collective-permute-start.10 = (f32[16,256]{1,0:T(8,128)S(1)}, f32[16,256]{1,0:T(8,128)S(1)}, u32[]{:S(2)}, u32[]{:S(2)}) collective-permute-start(f32[16,256]{1,0:T(8,128)S(1)} %add.107), channel_id=1, source_target_pairs={{0,32},{8,40},{16,48},{24,56},{32,64},{40,72},{48,80},{56,88},{64,... | collective-permute-start | bytes 49160 | tf_op jit(solution)/shard_map/ppermute | solution.py:255
  68.9 4.6 %collective-permute-start.16 = (f32[16,768]{1,0:T(8,128)S(1)}, f32[16,768]{1,0:T(8,128)S(1)}, u32[]{:S(2)}, u32[]{:S(2)}) collective-permute-start(f32[16,768]{1,0:T(8,128)S(1)} %broadcast_select_fusion), channel_id=1, source_target_pairs={{112,48},{120,56},{113,49},{121,57},{114,50},{122,58},{115,51},{12... | collective-permute-start | bytes 147464 | tf_op jit(solution)/shard_map/ppermute | solution.py:272
  69.6 3.9 %collective-permute-start.15 = (f32[16,768]{1,0:T(8,128)S(1)}, f32[16,768]{1,0:T(8,128)S(1)}, u32[]{:S(2)}, u32[]{:S(2)}) collective-permute-start(f32[16,768]{1,0:T(8,128)S(1)} %broadcast_select_fusion), channel_id=1, source_target_pairs={{112,16},{120,24},{113,17},{121,25},{114,18},{122,26},{115,19},{12... | collective-permute-start | bytes 147464 | tf_op jit(solution)/shard_map/ppermute | solution.py:272
  70.2 3.2 %collective-permute-start.14 = (f32[16,768]{1,0:T(8,128)S(1)}, f32[16,768]{1,0:T(8,128)S(1)}, u32[]{:S(2)}, u32[]{:S(2)}) collective-permute-start(f32[16,768]{1,0:T(8,128)S(1)} %broadcast_select_fusion), channel_id=1, source_target_pairs={{112,80},{120,88},{113,81},{121,89},{114,82},{122,90},{115,83},{12... | collective-permute-start | bytes 147464 | tf_op jit(solution)/shard_map/ppermute | solution.py:272
  73.4 11.2 %copy-start.1 = (f32[2,1,16,768]{3,2,1,0:T(8,128)}, f32[2,1,16,768]{3,2,1,0:T(8,128)S(1)}, u32[]{:S(2)}) copy-start(f32[2,1,16,768]{3,2,1,0:T(8,128)S(1)} %shard_map.71.refs_1_) | copy-start | bytes 294916
  73.5 7.3 %collective-permute-start.17 = (f32[16,768]{1,0:T(8,128)S(1)}, f32[16,768]{1,0:T(8,128)S(1)}, u32[]{:S(2)}, u32[]{:S(2)}) collective-permute-start(f32[16,768]{1,0:T(8,128)S(1)} %add_add_fusion), channel_id=1, source_target_pairs={{16,0},{24,8},{48,32},{56,40},{80,64},{88,72},{112,96},{120,104},{... | collective-permute-start | bytes 147464 | tf_op jit(solution)/shard_map/ppermute | solution.py:275
  74.8 6.0 %copy-start.6 = (f32[4,192,768]{2,1,0:T(8,128)S(1)}, f32[4,192,768]{2,1,0:T(8,128)}, u32[]{:S(2)}) copy-start(f32[4,192,768]{2,1,0:T(8,128)} %shard_map.70) | copy-start | bytes 7077892
  74.8 9.8 %copy-start.4 = (f32[6,192,768]{2,1,0:T(8,128)S(1)}, f32[6,192,768]{2,1,0:T(8,128)}, u32[]{:S(2)}) copy-start(f32[6,192,768]{2,1,0:T(8,128)} %shard_map.69) | copy-start | bytes 10616836
  74.8 9.8 %collective-permute-start.20 = (f32[1,16,768]{2,1,0:T(8,128)S(1)}, f32[1,16,768]{2,1,0:T(8,128)S(1)}, u32[]{:S(2)}, u32[]{:S(2)}) collective-permute-start(f32[1,16,768]{2,1,0:T(8,128)S(1)} %slice_bitcast_fusion.1), channel_id=1, source_target_pairs={{0,8},{8,0},{16,24},{24,16},{32,40},{40,32},{48,56},{56,48},{64,72... | collective-permute-start | bytes 147464 | tf_op jit(solution)/shard_map/ppermute | solution.py:247
  80.8 18.0 %copy-start = (f32[2,2,16,768]{3,2,1,0:T(8,128)}, f32[2,2,16,768]{3,2,1,0:T(8,128)S(1)}, u32[]{:S(2)}) copy-start(f32[2,2,16,768]{3,2,1,0:T(8,128)S(1)} %shard_map.72.refs_0_) | copy-start | bytes 589828
  81.2 3.5 %collective-permute-start.19 = (f32[16,192]{1,0:T(8,128)S(1)}, f32[16,192]{1,0:T(8,128)S(1)}, u32[]{:S(2)}, u32[]{:S(2)}) collective-permute-start(f32[16,192]{1,0:T(8,128)S(1)} %fusion.39), channel_id=1, source_target_pairs={{0,8},{8,0},{16,24},{24,16},{32,40},{40,32},{48,56},{56,48},{64,72... | collective-permute-start | bytes 36872 | tf_op jit(solution)/shard_map/ppermute | solution.py:247
  84.9 5.3 %collective-permute-start.21 = (f32[16,768]{1,0:T(8,128)S(1)}, f32[16,768]{1,0:T(8,128)S(1)}, u32[]{:S(2)}, u32[]{:S(2)}) collective-permute-start(f32[16,768]{1,0:T(8,128)S(1)} %bitcast_subtract_fusion), channel_id=1, source_target_pairs={{0,16},{8,24},{16,0},{24,8},{32,48},{40,56},{48,32},{56,40},{64,80... | collective-permute-start | bytes 147464 | tf_op jit(solution)/shard_map/ppermute | solution.py:252
  86.7 12.1 %collective-permute-start.18 = (f32[2,16,768]{2,1,0:T(8,128)S(1)}, f32[2,16,768]{2,1,0:T(8,128)S(1)}, u32[]{:S(2)}, u32[]{:S(2)}) collective-permute-start(f32[2,16,768]{2,1,0:T(8,128)S(1)} %slice_bitcast_fusion), channel_id=1, source_target_pairs={{0,8},{8,0},{16,24},{24,16},{32,40},{40,32},{48,56},{56,48},{64,72... | collective-permute-start | bytes 294920 | tf_op jit(solution)/shard_map/ppermute | solution.py:247
  90.2 8.7 %copy-start.2 = (f32[16,2048]{1,0:T(8,128)}, f32[16,2048]{1,0:T(8,128)S(1)}, u32[]{:S(2)}) copy-start(f32[16,2048]{1,0:T(8,128)S(1)} %shard_map.73.first_ref) | copy-start | bytes 393220
  90.2 4.9 %collective-permute-start.23 = (f32[16,768]{1,0:T(8,128)S(1)}, f32[16,768]{1,0:T(8,128)S(1)}, u32[]{:S(2)}, u32[]{:S(2)}) collective-permute-start(f32[16,768]{1,0:T(8,128)S(1)} %add.116), channel_id=1, source_target_pairs={{0,64},{8,72},{16,80},{24,88},{32,96},{40,104},{48,112},{56,120},{... | collective-permute-start | bytes 147464 | tf_op jit(solution)/shard_map/ppermute | solution.py:255
  92.8 2.9 %collective-permute-start.24 = (f32[16,768]{1,0:T(8,128)S(1)}, f32[16,768]{1,0:T(8,128)S(1)}, u32[]{:S(2)}, u32[]{:S(2)}) collective-permute-start(f32[16,768]{1,0:T(8,128)S(1)} %add.116), channel_id=1, source_target_pairs={{0,96},{8,104},{16,112},{24,120},{32,0},{40,8},{48,16},{56,24},{64... | collective-permute-start | bytes 147464 | tf_op jit(solution)/shard_map/ppermute | solution.py:255
  92.8 4.2 %collective-permute-start.22 = (f32[16,768]{1,0:T(8,128)S(1)}, f32[16,768]{1,0:T(8,128)S(1)}, u32[]{:S(2)}, u32[]{:S(2)}) collective-permute-start(f32[16,768]{1,0:T(8,128)S(1)} %add.116), channel_id=1, source_target_pairs={{0,32},{8,40},{16,48},{24,56},{32,64},{40,72},{48,80},{56,88},{64,... | collective-permute-start | bytes 147464 | tf_op jit(solution)/shard_map/ppermute | solution.py:255
  97.2 2.4 %collective-permute-start.25 = (f32[16,192]{1,0:T(8,128)S(1)}, f32[16,192]{1,0:T(8,128)S(1)}, u32[]{:S(2)}, u32[]{:S(2)}) collective-permute-start(f32[16,192]{1,0:T(8,128)S(1)} %fusion.33), channel_id=1, source_target_pairs={{0,8},{8,0},{16,24},{24,16},{32,40},{40,32},{48,56},{56,48},{64,72... | collective-permute-start | bytes 36872 | tf_op jit(solution)/shard_map/ppermute | solution.py:247
  99.9 3.5 %collective-permute-start.26 = (f32[16,768]{1,0:T(8,128)S(1)}, f32[16,768]{1,0:T(8,128)S(1)}, u32[]{:S(2)}, u32[]{:S(2)}) collective-permute-start(f32[16,768]{1,0:T(8,128)S(1)} %fusion.59), channel_id=1, source_target_pairs={{0,16},{8,24},{16,0},{24,8},{32,48},{40,56},{48,32},{56,40},{64,80... | collective-permute-start | bytes 147464 | tf_op jit(solution)/shard_map/ppermute | solution.py:252
  100.7 5.7 %copy-start.5 = (f32[6,192,768]{2,1,0:T(8,128)S(1)}, f32[6,192,768]{2,1,0:T(8,128)}, u32[]{:S(2)}) copy-start(f32[6,192,768]{2,1,0:T(8,128)} %shard_map.69) | copy-start | bytes 10616836
  103.4 12.3 %copy-start.3 = (f32[2,1,16,768]{3,2,1,0:T(8,128)}, f32[2,1,16,768]{3,2,1,0:T(8,128)S(1)}, u32[]{:S(2)}) copy-start(f32[2,1,16,768]{3,2,1,0:T(8,128)S(1)} %shard_map.74.refs_2_) | copy-start | bytes 294916
  103.4 4.5 %collective-permute-start.28 = (f32[16,768]{1,0:T(8,128)S(1)}, f32[16,768]{1,0:T(8,128)S(1)}, u32[]{:S(2)}, u32[]{:S(2)}) collective-permute-start(f32[16,768]{1,0:T(8,128)S(1)} %add.121), channel_id=1, source_target_pairs={{0,64},{8,72},{16,80},{24,88},{32,96},{40,104},{48,112},{56,120},{... | collective-permute-start | bytes 147464 | tf_op jit(solution)/shard_map/ppermute | solution.py:255
  104.3 3.7 %collective-permute-start.29 = (f32[16,768]{1,0:T(8,128)S(1)}, f32[16,768]{1,0:T(8,128)S(1)}, u32[]{:S(2)}, u32[]{:S(2)}) collective-permute-start(f32[16,768]{1,0:T(8,128)S(1)} %add.121), channel_id=1, source_target_pairs={{0,96},{8,104},{16,112},{24,120},{32,0},{40,8},{48,16},{56,24},{64... | collective-permute-start | bytes 147464 | tf_op jit(solution)/shard_map/ppermute | solution.py:255
  106.4 4.2 %collective-permute-start.27 = (f32[16,768]{1,0:T(8,128)S(1)}, f32[16,768]{1,0:T(8,128)S(1)}, u32[]{:S(2)}, u32[]{:S(2)}) collective-permute-start(f32[16,768]{1,0:T(8,128)S(1)} %add.121), channel_id=1, source_target_pairs={{0,32},{8,40},{16,48},{24,56},{32,64},{40,72},{48,80},{56,88},{64,... | collective-permute-start | bytes 147464 | tf_op jit(solution)/shard_map/ppermute | solution.py:255
  110.9 3.6 %collective-permute-start.30 = (f32[16,192]{1,0:T(8,128)S(1)}, f32[16,192]{1,0:T(8,128)S(1)}, u32[]{:S(2)}, u32[]{:S(2)}) collective-permute-start(f32[16,192]{1,0:T(8,128)S(1)} %fusion.25), channel_id=1, source_target_pairs={{0,8},{8,0},{16,24},{24,16},{32,40},{40,32},{48,56},{56,48},{64,72... | collective-permute-start | bytes 36872 | tf_op jit(solution)/shard_map/ppermute | solution.py:247
  114.8 3.0 %collective-permute-start.31 = (f32[16,768]{1,0:T(8,128)S(1)}, f32[16,768]{1,0:T(8,128)S(1)}, u32[]{:S(2)}, u32[]{:S(2)}) collective-permute-start(f32[16,768]{1,0:T(8,128)S(1)} %fusion.63), channel_id=1, source_target_pairs={{0,16},{8,24},{16,0},{24,8},{32,48},{40,56},{48,32},{56,40},{64,80... | collective-permute-start | bytes 147464 | tf_op jit(solution)/shard_map/ppermute | solution.py:252
  117.8 4.5 %collective-permute-start.33 = (f32[16,768]{1,0:T(8,128)S(1)}, f32[16,768]{1,0:T(8,128)S(1)}, u32[]{:S(2)}, u32[]{:S(2)}) collective-permute-start(f32[16,768]{1,0:T(8,128)S(1)} %add.126), channel_id=1, source_target_pairs={{0,64},{8,72},{16,80},{24,88},{32,96},{40,104},{48,112},{56,120},{... | collective-permute-start | bytes 147464 | tf_op jit(solution)/shard_map/ppermute | solution.py:255
  117.9 4.4 %collective-permute-start.34 = (f32[16,768]{1,0:T(8,128)S(1)}, f32[16,768]{1,0:T(8,128)S(1)}, u32[]{:S(2)}, u32[]{:S(2)}) collective-permute-start(f32[16,768]{1,0:T(8,128)S(1)} %add.126), channel_id=1, source_target_pairs={{0,96},{8,104},{16,112},{24,120},{32,0},{40,8},{48,16},{56,24},{64... | collective-permute-start | bytes 147464 | tf_op jit(solution)/shard_map/ppermute | solution.py:255
  118.8 4.2 %collective-permute-start.32 = (f32[16,768]{1,0:T(8,128)S(1)}, f32[16,768]{1,0:T(8,128)S(1)}, u32[]{:S(2)}, u32[]{:S(2)}) collective-permute-start(f32[16,768]{1,0:T(8,128)S(1)} %add.126), channel_id=1, source_target_pairs={{0,32},{8,40},{16,48},{24,56},{32,64},{40,72},{48,80},{56,88},{64,... | collective-permute-start | bytes 147464 | tf_op jit(solution)/shard_map/ppermute | solution.py:255
  123.2 4.1 %collective-permute-start.35 = (f32[16,192]{1,0:T(8,128)S(1)}, f32[16,192]{1,0:T(8,128)S(1)}, u32[]{:S(2)}, u32[]{:S(2)}) collective-permute-start(f32[16,192]{1,0:T(8,128)S(1)} %fusion.21), channel_id=1, source_target_pairs={{0,8},{8,0},{16,24},{24,16},{32,40},{40,32},{48,56},{56,48},{64,72... | collective-permute-start | bytes 36872 | tf_op jit(solution)/shard_map/ppermute | solution.py:247

commit v4 on v3

--- a/solution.py
+++ b/solution.py
@@ -253,7 +253,7 @@
     array, beside = lax.optimization_barrier((array, beside))
     others = [
         lax.ppermute(array, "wide", [(i, (i + by) % size) for i in range(size)])
-        for by in (4, 8, 12)
+        for by in (12, 8, 4)
     ]
     return (array + others[0]) + (others[1] + others[2]), beside
 

time: 129 us -> 127 us (0.984)
  waiting for transfers between devices: 22.5 us -> 15.9 us
  starting transfers between devices: 55.5 us -> 60.9 us
    ppermute x15, starting transfers between devices: 13.8 us -> 21.1 us  [from_chips(): lax.ppermute(array, 'wide', [(i, (i + by) % size) for i in range(size)])]
    ppermute x15, waiting for transfers between devices: 14.8 us -> 8.25 us  [from_chips(): lax.ppermute(array, 'wide', [(i, (i + by) % size) for i in range(size)])]
    ppermute x12, starting transfers between devices: 21.1 us -> 19.3 us  [swapped(): return lax.ppermute(array, 'wide', [(i, i ^ 1) for i in range(size)])]
  transfers between devices with their start and end apart: 38 -> 38, of which waited for: 19 -> 18; matrix products, arithmetic and copies ran while one was open for 16% -> 16% of each run, Pallas kernels for 20% -> 21%
where the time goes in v4:
time: 127 us
  starting transfers between devices  60.9 us (48%)
  Pallas kernels  26.2 us (21%)
  matrix products  18.1 us (14%)
  waiting for transfers between devices  15.9 us (13%)
  other arithmetic  2.53 us (2%)
  local copies, waits for them, and re-layouts  2.2 us (2%)
    ppermute x15, starting transfers between devices, from_chips(): lax.ppermute(array, 'wide', [(i, (i + by) % size) for i in range(size)])  21.1 us
    ppermute x12, starting transfers between devices, swapped(): return lax.ppermute(array, 'wide', [(i, i ^ 1) for i in range(size)])  19.3 us
    dot_general x2, matrix products, gram_of(): lax.dot_general(reflectors[1, lo:hi], reflectors[0, lo:hi], (((0,), (0,))...  13.8 us
    pallas_call x4, Pallas kernels, updated(): pl.pallas_call(functools.partial(update_kernel, z_first, first, which), o...  11.7 us
    ppermute x15, waiting for transfers between devices, from_chips(): lax.ppermute(array, 'wide', [(i, (i + by) % size) for i in range(size)])  8.25 us
    pallas_call x1, Pallas kernels, products_of(): pl.pallas_call(products_kernel, out_shape=[jax.ShapeDtypeStruct((rows, le...  6.57 us
    all_to_all x1, starting transfers between devices, body(): received = lax.all_to_all(received, 'wide', 0, 0, tiled=True)  6.54 us
    all_to_all x1, starting transfers between devices, body(): received = lax.all_to_all(received, 'narrow', 0, 0, tiled=True)  6.36 us
  transfers between devices with their start and end apart: 38, of which 18 were waited for; matrix products, arithmetic and copies ran while one was open for 16% of the time, Pallas kernels for 21%

profile of v4, /device:TPU:1, one launch (start us, length us, event | category | flops | bytes accessed | tf_op | source)
XLA Modules:
  0.0 127.0 jit_solution(5629300900190389218)
XLA Ops:
  0.6 1.5 %collective-permute-start.2 = (f32[6,96,1536]{2,1,0:T(8,128)}, f32[6,96,1536]{2,1,0:T(8,128)}, u32[]{:S(2)}, u32[]{:S(2)}) collective-permute-start(f32[6,96,1536]{2,1,0:T(8,128)} %own_ref), channel_id=1, source_target_pairs={{0,8},{8,0},{16,24},{24,16},{32,40},{40,32},{48,56},{56,48},{64,72... | collective-permute-start | bytes 10616840 | tf_op jit(solution)/shard_map/ppermute | solution.py:247
  2.1 6.5 %all-to-all-start = ((f32[16,64,128]{2,1,0:T(8,128)}), f32[16,64,128]{2,1,0:T(8,128)}, u32[]{:S(2)}, u32[]{:S(2)}) async-start(f32[16,64,128]{2,1,0:T(8,128)} %bitcast.121), calls=%async_computation | async-start | bytes 1048576 | tf_op jit(solution)/shard_map/all_to_all | solution.py:328
  8.9 6.9 %fusion.3 = f32[256,256]{1,0:T(8,128)S(1)} fusion(f32[2,8192,256]{2,1,0:T(8,128)} %v_ref.9), kind=kOutput, calls=%fused_computation.3 | convolution fusion | flops 1610612736 | bytes 8650752 | tf_op jit(solution)/shard_map/dot_general | solution.py:307
  15.8 1.5 %slice.104 = f32[2,768,256]{2,1,0:T(8,128)S(1)} slice(f32[2,8192,256]{2,1,0:T(8,128)} %v_ref.9), slice={[0:2], [6656:7424], [0:256]} | slice | bytes 3145728 | tf_op jit(solution)/shard_map/slice | solution.py:331
  17.3 1.3 all-to-all-done
  18.6 1.2 collective-permute-start
  19.7 6.4 %all-to-all-start.1 = ((f32[16,64,128]{2,1,0:T(8,128)}), f32[16,64,128]{2,1,0:T(8,128)S(1)}, u32[]{:S(2)}, u32[]{:S(2)}) async-start(f32[16,64,128]{2,1,0:T(8,128)} %all-to-all-done), calls=%async_computation.1 | async-start | bytes 1048576 | tf_op jit(solution)/shard_map/all_to_all | solution.py:335
  26.1 6.9 %fusion.10 = f32[256,256]{1,0:T(8,128)S(1)} fusion(f32[256,256]{1,0:T(8,128)S(1)} %fusion.3, f32[2,8192,256]{2,1,0:T(8,128)} %v_ref.9), kind=kOutput, calls=%fused_computation.11 | convolution fusion | flops 1610678272 | bytes 8912896 | tf_op jit(solution)/shard_map/dot_general | solution.py:307
  33.0 2.1 %slice_select_fusion = f32[2,768,256]{2,1,0:T(8,128)S(1)} fusion(f32[2,768,256]{2,1,0:T(8,128)} %collective-permute-done, f32[2,8192,256]{2,1,0:T(8,128)} %v_ref.9, pred[]{:T(512)S(6)} %eq.12), kind=kLoop, calls=%fused_computation.10 | loop fusion | flops 393216 | bytes 4718593 | tf_op jit(solution)/shard_map/jit(_where)/select_n | solution.py:337
  35.1 1.5 %all-to-all-done.1 = f32[16,64,128]{2,1,0:T(8,128)S(1)} async-done(((f32[16,64,128]{2,1,0:T(8,128)}), f32[16,64,128]{2,1,0:T(8,128)S(1)}, u32[]{:S(2)}, u32[]{:S(2)}) %all-to-all-start.1) | async-done | bytes 524320 | tf_op jit(solution)/shard_map/all_to_all | solution.py:335
  36.6 6.6 %shard_map.68 = (f32[16,8192]{1,0:T(8,128)S(1)}, f32[16,256]{1,0:T(8,128)S(1)}, f32[16,256]{1,0:T(8,128)S(1)}) custom-call(f32[8,2,64,128]{3,2,1,0:T(8,128)S(1)} %bitcast.118, f32[2,8192,256]{2,1,0:T(8,128)} %v_ref.9), custom_call_target="tpu_custom_call" | custom-call | flops 402653184 | bytes 17334272 | tf_op jit(solution)/shard_map/pallas_call | solution.py:158
  43.2 1.1 collective-permute-start.3
  44.3 0.8 collective-permute-done.3
  45.2 3.3 %shard_map.69 = f32[6,192,768]{2,1,0:T(8,128)} custom-call(s32[1]{0:T(128)} %bitcast.7.core_ref, f32[6,96,1536]{2,1,0:T(8,128)} %own_ref, f32[6,96,1536]{2,1,0:T(8,128)} %collective-permute-done.2.other_ref), custom_call_target="tpu_custom_call" | custom-call | bytes 884736 | tf_op jit(solution)/shard_map/pallas_call | solution.py:86
  48.6 1.9 %collective-permute-start.6 = (f32[16,256]{1,0:T(8,128)S(1)}, f32[16,256]{1,0:T(8,128)S(1)}, u32[]{:S(2)}, u32[]{:S(2)}) collective-permute-start(f32[16,256]{1,0:T(8,128)S(1)} %add.101), channel_id=1, source_target_pairs={{0,64},{8,72},{16,80},{24,88},{32,96},{40,104},{48,112},{56,120},{... | collective-permute-start | bytes 49160 | tf_op jit(solution)/shard_map/ppermute | solution.py:255
  50.8 2.4 %collective-permute-start.5 = (f32[16,256]{1,0:T(8,128)S(1)}, f32[16,256]{1,0:T(8,128)S(1)}, u32[]{:S(2)}, u32[]{:S(2)}) collective-permute-start(f32[16,256]{1,0:T(8,128)S(1)} %add.101), channel_id=1, source_target_pairs={{0,96},{8,104},{16,112},{24,120},{32,0},{40,8},{48,16},{56,24},{64... | collective-permute-start | bytes 49160 | tf_op jit(solution)/shard_map/ppermute | solution.py:255
  53.2 1.5 %collective-permute-start.13 = (f32[16,768]{1,0:T(8,128)S(1)}, f32[16,768]{1,0:T(8,128)S(1)}, u32[]{:S(2)}, u32[]{:S(2)}) collective-permute-start(f32[16,768]{1,0:T(8,128)S(1)} %slice.110), channel_id=1, source_target_pairs={{0,8},{8,0},{16,24},{24,16},{32,40},{40,32},{48,56},{56,48},{64,72... | collective-permute-start | bytes 147464 | tf_op jit(solution)/shard_map/ppermute | solution.py:247
  55.1 1.8 %collective-permute-start.8 = (f32[16,256]{1,0:T(8,128)S(1)}, f32[16,256]{1,0:T(8,128)S(1)}, u32[]{:S(2)}, u32[]{:S(2)}) collective-permute-start(f32[16,256]{1,0:T(8,128)S(1)} %convolution_subtract_fusion), channel_id=1, source_target_pairs={{0,8},{8,0},{16,24},{24,16},{32,40},{40,32},{48,56},{56,48},{64,72... | collective-permute-start | bytes 49160 | tf_op jit(solution)/shard_map/ppermute | solution.py:247
  56.8 0.8 collective-permute-done.8
  57.7 0.9 collective-permute-start.9
  58.6 2.7 %shard_map.70 = f32[4,192,768]{2,1,0:T(8,128)} custom-call(s32[1]{0:T(128)} %bitcast.7.core_ref, f32[4,96,1536]{2,1,0:T(8,128)} %bitcast.120, f32[4,96,1536]{2,1,0:T(8,128)} %collective-permute-done.1.other_ref), custom_call_target="tpu_custom_call" | custom-call | bytes 589824 | tf_op jit(solution)/shard_map/pallas_call | solution.py:86
  61.3 1.3 collective-permute-start.11
  62.6 2.3 %collective-permute-start.12 = (f32[16,256]{1,0:T(8,128)S(1)}, f32[16,256]{1,0:T(8,128)S(1)}, u32[]{:S(2)}, u32[]{:S(2)}) collective-permute-start(f32[16,256]{1,0:T(8,128)S(1)} %add.107), channel_id=1, source_target_pairs={{0,32},{8,40},{16,48},{24,56},{32,64},{40,72},{48,80},{56,88},{64,... | collective-permute-start | bytes 49160 | tf_op jit(solution)/shard_map/ppermute | solution.py:255
  65.0 0.3 collective-permute-start.10
  65.3 0.5 select_subtract_fusion
  65.7 1.0 collective-permute-done.12
  66.7 1.1 collective-permute-done.10
  68.0 0.5 fusion.15
  68.6 0.7 collective-permute-start.16
  69.3 0.7 collective-permute-start.15
  69.9 0.7 collective-permute-start.14
  70.6 2.5 %shard_map.71.refs_1_ = f32[2,1,16,768]{3,2,1,0:T(8,128)S(1)} custom-call(f32[16,8192]{1,0:T(8,128)S(1)} %get-tuple-element.74.z_ref, f32[2,8192,256]{2,1,0:T(8,128)} %v_ref.9, f32[16,256]{1,0:T(8,128)S(1)} %fusion.53.refs_0_, f32[16,256]{1,0:T(8,128)S(1)} %fusion.51.refs_1_), custom_call_target="tpu_custom_call" | custom-call | flops 75497472 | bytes 3276800 | tf_op jit(solution)/shard_map/pallas_call | solution.py:208
  73.2 1.3 %collective-permute-start.17 = (f32[16,768]{1,0:T(8,128)S(1)}, f32[16,768]{1,0:T(8,128)S(1)}, u32[]{:S(2)}, u32[]{:S(2)}) collective-permute-start(f32[16,768]{1,0:T(8,128)S(1)} %add_add_fusion), channel_id=1, source_target_pairs={{16,0},{24,8},{48,32},{56,40},{80,64},{88,72},{112,96},{120,104},{... | collective-permute-start | bytes 147464 | tf_op jit(solution)/shard_map/ppermute | solution.py:275
  74.5 2.1 %collective-permute-start.20 = (f32[1,16,768]{2,1,0:T(8,128)S(1)}, f32[1,16,768]{2,1,0:T(8,128)S(1)}, u32[]{:S(2)}, u32[]{:S(2)}) collective-permute-start(f32[1,16,768]{2,1,0:T(8,128)S(1)} %slice_bitcast_fusion.1), channel_id=1, source_target_pairs={{0,8},{8,0},{16,24},{24,16},{32,40},{40,32},{48,56},{56,48},{64,72... | collective-permute-start | bytes 147464 | tf_op jit(solution)/shard_map/ppermute | solution.py:247
  76.6 3.6 %shard_map.72.refs_0_ = f32[2,2,16,768]{3,2,1,0:T(8,128)S(1)} custom-call(f32[16,8192]{1,0:T(8,128)S(1)} %get-tuple-element.74.z_ref, f32[2,8192,256]{2,1,0:T(8,128)} %v_ref.9, f32[16,256]{1,0:T(8,128)S(1)} %fusion.53.refs_0_, f32[16,256]{1,0:T(8,128)S(1)} %fusion.51.refs_1_), custom_call_target="tpu_custom_call" | custom-call | flops 150994944 | bytes 6520832 | tf_op jit(solution)/shard_map/pallas_call | solution.py:208
  80.6 2.7 %collective-permute-start.19 = (f32[16,192]{1,0:T(8,128)S(1)}, f32[16,192]{1,0:T(8,128)S(1)}, u32[]{:S(2)}, u32[]{:S(2)}) collective-permute-start(f32[16,192]{1,0:T(8,128)S(1)} %fusion.39), channel_id=1, source_target_pairs={{0,8},{8,0},{16,24},{24,16},{32,40},{40,32},{48,56},{56,48},{64,72... | collective-permute-start | bytes 36872 | tf_op jit(solution)/shard_map/ppermute | solution.py:247
  83.2 0.8 collective-permute-done.19
  84.4 1.8 %collective-permute-start.21 = (f32[16,768]{1,0:T(8,128)S(1)}, f32[16,768]{1,0:T(8,128)S(1)}, u32[]{:S(2)}, u32[]{:S(2)}) collective-permute-start(f32[16,768]{1,0:T(8,128)S(1)} %bitcast_subtract_fusion), channel_id=1, source_target_pairs={{0,16},{8,24},{16,0},{24,8},{32,48},{40,56},{48,32},{56,40},{64,80... | collective-permute-start | bytes 147464 | tf_op jit(solution)/shard_map/ppermute | solution.py:252
  86.2 0.5 collective-permute-start.18
  86.7 2.9 %shard_map.73.first_ref = f32[16,2048]{1,0:T(8,128)S(1)} custom-call(f32[16,8192]{1,0:T(8,128)S(1)} %get-tuple-element.74.z_ref, f32[2,8192,256]{2,1,0:T(8,128)} %v_ref.9, f32[16,256]{1,0:T(8,128)S(1)} %fusion.53.refs_0_, f32[16,256]{1,0:T(8,128)S(1)} %fusion.51.refs_1_), custom_call_target="tpu_custom_call" | custom-call | flops 100663296 | bytes 4358144 | tf_op jit(solution)/shard_map/pallas_call | solution.py:208
  89.7 2.6 %collective-permute-start.23 = (f32[16,768]{1,0:T(8,128)S(1)}, f32[16,768]{1,0:T(8,128)S(1)}, u32[]{:S(2)}, u32[]{:S(2)}) collective-permute-start(f32[16,768]{1,0:T(8,128)S(1)} %add.116), channel_id=1, source_target_pairs={{0,64},{8,72},{16,80},{24,88},{32,96},{40,104},{48,112},{56,120},{... | collective-permute-start | bytes 147464 | tf_op jit(solution)/shard_map/ppermute | solution.py:255
  92.3 2.7 %collective-permute-start.22 = (f32[16,768]{1,0:T(8,128)S(1)}, f32[16,768]{1,0:T(8,128)S(1)}, u32[]{:S(2)}, u32[]{:S(2)}) collective-permute-start(f32[16,768]{1,0:T(8,128)S(1)} %add.116), channel_id=1, source_target_pairs={{0,96},{8,104},{16,112},{24,120},{32,0},{40,8},{48,16},{56,24},{64... | collective-permute-start | bytes 147464 | tf_op jit(solution)/shard_map/ppermute | solution.py:255
  95.2 1.2 collective-permute-done.24
  96.7 1.6 %collective-permute-start.25 = (f32[16,192]{1,0:T(8,128)S(1)}, f32[16,192]{1,0:T(8,128)S(1)}, u32[]{:S(2)}, u32[]{:S(2)}) collective-permute-start(f32[16,192]{1,0:T(8,128)S(1)} %fusion.33), channel_id=1, source_target_pairs={{0,8},{8,0},{16,24},{24,16},{32,40},{40,32},{48,56},{56,48},{64,72... | collective-permute-start | bytes 36872 | tf_op jit(solution)/shard_map/ppermute | solution.py:247
  98.3 0.8 collective-permute-done.25
  99.4 0.8 collective-permute-start.26
  100.2 2.7 %shard_map.74.refs_2_ = f32[2,1,16,768]{3,2,1,0:T(8,128)S(1)} custom-call(f32[16,8192]{1,0:T(8,128)S(1)} %get-tuple-element.74.z_ref, f32[2,8192,256]{2,1,0:T(8,128)} %v_ref.9, f32[16,256]{1,0:T(8,128)S(1)} %fusion.53.refs_0_, f32[16,256]{1,0:T(8,128)S(1)} %fusion.51.refs_1_), custom_call_target="tpu_custom_call" | custom-call | flops 75497472 | bytes 3276800 | tf_op jit(solution)/shard_map/pallas_call | solution.py:208
  102.9 1.3 collective-permute-start.28
  104.2 2.3 %collective-permute-start.29 = (f32[16,768]{1,0:T(8,128)S(1)}, f32[16,768]{1,0:T(8,128)S(1)}, u32[]{:S(2)}, u32[]{:S(2)}) collective-permute-start(f32[16,768]{1,0:T(8,128)S(1)} %add.121), channel_id=1, source_target_pairs={{0,32},{8,40},{16,48},{24,56},{32,64},{40,72},{48,80},{56,88},{64,... | collective-permute-start | bytes 147464 | tf_op jit(solution)/shard_map/ppermute | solution.py:255
  106.5 0.3 collective-permute-start.27
  107.4 0.9 collective-permute-done.29
  108.3 2.0 %collective-permute-done.27 = f32[16,768]{1,0:T(8,128)S(1)} collective-permute-done((f32[16,768]{1,0:T(8,128)S(1)}, f32[16,768]{1,0:T(8,128)S(1)}, u32[]{:S(2)}, u32[]{:S(2)}) %collective-permute-start.27) | collective-permute-done | bytes 49184 | tf_op jit(solution)/shard_map/ppermute | solution.py:255
  110.6 2.0 %collective-permute-start.30 = (f32[16,192]{1,0:T(8,128)S(1)}, f32[16,192]{1,0:T(8,128)S(1)}, u32[]{:S(2)}, u32[]{:S(2)}) collective-permute-start(f32[16,192]{1,0:T(8,128)S(1)} %fusion.25), channel_id=1, source_target_pairs={{0,8},{8,0},{16,24},{24,16},{32,40},{40,32},{48,56},{56,48},{64,72... | collective-permute-start | bytes 36872 | tf_op jit(solution)/shard_map/ppermute | solution.py:247
  112.8 0.6 collective-permute-done.30
  113.7 0.8 collective-permute-start.31
  114.5 1.9 %shard_map.75 = f32[16,8192]{1,0:T(8,128)} custom-call(f32[16,2048]{1,0:T(8,128)} %copy-done.2, f32[2,2,16,768]{3,2,1,0:T(8,128)} %copy-done, f32[2,1,16,768]{3,2,1,0:T(8,128)} %copy-done.1, f32[2,1,16,768]{3,2,1,0:T(8,128)} %copy-done.3), custom_call_target="tpu_custom_call" | custom-call | bytes 1048576 | tf_op jit(solution)/shard_map/pallas_call | solution.py:234
  116.7 0.7 collective-permute-start.33
  117.4 1.5 %collective-permute-start.34 = (f32[16,768]{1,0:T(8,128)S(1)}, f32[16,768]{1,0:T(8,128)S(1)}, u32[]{:S(2)}, u32[]{:S(2)}) collective-permute-start(f32[16,768]{1,0:T(8,128)S(1)} %add.126), channel_id=1, source_target_pairs={{0,32},{8,40},{16,48},{24,56},{32,64},{40,72},{48,80},{56,88},{64,... | collective-permute-start | bytes 147464 | tf_op jit(solution)/shard_map/ppermute | solution.py:255
  118.9 1.2 collective-permute-start.32
  120.1 1.1 collective-permute-done.33
  121.2 0.5 collective-permute-done.34
  122.2 3.2 %collective-permute-start.35 = (f32[16,192]{1,0:T(8,128)S(1)}, f32[16,192]{1,0:T(8,128)S(1)}, u32[]{:S(2)}, u32[]{:S(2)}) collective-permute-start(f32[16,192]{1,0:T(8,128)S(1)} %fusion.21), channel_id=1, source_target_pairs={{0,8},{8,0},{16,24},{24,16},{32,40},{40,32},{48,56},{56,48},{64,72... | collective-permute-start | bytes 36872 | tf_op jit(solution)/shard_map/ppermute | solution.py:247
  125.5 0.8 collective-permute-done.35
  126.3 0.6 copy.7
  (81 shorter events, 5.3 us)
Async XLA Ops:
  0.6 42.5 %collective-permute-start.2 = (f32[6,96,1536]{2,1,0:T(8,128)}, f32[6,96,1536]{2,1,0:T(8,128)}, u32[]{:S(2)}, u32[]{:S(2)}) collective-permute-start(f32[6,96,1536]{2,1,0:T(8,128)} %own_ref), channel_id=1, source_target_pairs={{0,8},{8,0},{16,24},{24,16},{32,40},{40,32},{48,56},{56,48},{64,72... | collective-permute-start | bytes 10616840 | tf_op jit(solution)/shard_map/ppermute | solution.py:247
  2.1 16.4 %all-to-all-start = ((f32[16,64,128]{2,1,0:T(8,128)}), f32[16,64,128]{2,1,0:T(8,128)}, u32[]{:S(2)}, u32[]{:S(2)}) async-start(f32[16,64,128]{2,1,0:T(8,128)} %bitcast.121), calls=%async_computation | async-start | bytes 1048576 | tf_op jit(solution)/shard_map/all_to_all | solution.py:328
  8.7 34.5 %collective-permute-start.1 = (f32[4,96,1536]{2,1,0:T(8,128)}, f32[4,96,1536]{2,1,0:T(8,128)}, u32[]{:S(2)}, u32[]{:S(2)}) collective-permute-start(f32[4,96,1536]{2,1,0:T(8,128)} %bitcast.119), channel_id=1, source_target_pairs={{0,8},{8,0},{16,24},{24,16},{32,40},{40,32},{48,56},{56,48},{64,72... | collective-permute-start | bytes 7077896 | tf_op jit(solution)/shard_map/ppermute | solution.py:247
  18.6 14.4 %collective-permute-start = (f32[2,768,256]{2,1,0:T(8,128)S(1)}, f32[2,768,256]{2,1,0:T(8,128)}, u32[]{:S(2)}, u32[]{:S(2)}) collective-permute-start(f32[2,768,256]{2,1,0:T(8,128)S(1)} %slice.104), channel_id=1, source_target_pairs={{0,8},{8,0},{16,24},{24,16},{32,40},{40,32},{48,56},{56,48},{64,72... | collective-permute-start | bytes 4718600 | tf_op jit(solution)/shard_map/ppermute | solution.py:247
  19.7 16.8 %all-to-all-start.1 = ((f32[16,64,128]{2,1,0:T(8,128)}), f32[16,64,128]{2,1,0:T(8,128)S(1)}, u32[]{:S(2)}, u32[]{:S(2)}) async-start(f32[16,64,128]{2,1,0:T(8,128)} %all-to-all-done), calls=%async_computation.1 | async-start | bytes 1048576 | tf_op jit(solution)/shard_map/all_to_all | solution.py:335
  43.2 2.0 %collective-permute-start.3 = (f32[16,256]{1,0:T(8,128)S(1)}, f32[16,256]{1,0:T(8,128)S(1)}, u32[]{:S(2)}, u32[]{:S(2)}) collective-permute-start(f32[16,256]{1,0:T(8,128)S(1)} %get-tuple-element.63), channel_id=1, source_target_pairs={{0,8},{8,0},{16,24},{24,16},{32,40},{40,32},{48,56},{56,48},{64,72... | collective-permute-start | bytes 49160 | tf_op jit(solution)/shard_map/ppermute | solution.py:247
  45.2 3.4 %collective-permute-start.4 = (f32[16,256]{1,0:T(8,128)S(1)}, f32[16,256]{1,0:T(8,128)S(1)}, u32[]{:S(2)}, u32[]{:S(2)}) collective-permute-start(f32[16,256]{1,0:T(8,128)S(1)} %add.100), channel_id=1, source_target_pairs={{0,16},{8,24},{16,0},{24,8},{32,48},{40,56},{48,32},{56,40},{64,80... | collective-permute-start | bytes 49160 | tf_op jit(solution)/shard_map/ppermute | solution.py:252
  45.2 9.4 %copy-start.7 = (f32[2,256,256]{2,1,0:T(8,128)S(1)}, f32[2,256,256]{2,1,0:T(8,128)}, u32[]{:S(2)}) copy-start(f32[2,256,256]{2,1,0:T(8,128)} %param.7) | copy-start | bytes 1572868
  48.6 6.1 %collective-permute-start.6 = (f32[16,256]{1,0:T(8,128)S(1)}, f32[16,256]{1,0:T(8,128)S(1)}, u32[]{:S(2)}, u32[]{:S(2)}) collective-permute-start(f32[16,256]{1,0:T(8,128)S(1)} %add.101), channel_id=1, source_target_pairs={{0,64},{8,72},{16,80},{24,88},{32,96},{40,104},{48,112},{56,120},{... | collective-permute-start | bytes 49160 | tf_op jit(solution)/shard_map/ppermute | solution.py:255
  50.5 4.2 %collective-permute-start.7 = (f32[16,256]{1,0:T(8,128)S(1)}, f32[16,256]{1,0:T(8,128)S(1)}, u32[]{:S(2)}, u32[]{:S(2)}) collective-permute-start(f32[16,256]{1,0:T(8,128)S(1)} %add.101), channel_id=1, source_target_pairs={{0,32},{8,40},{16,48},{24,56},{32,64},{40,72},{48,80},{56,88},{64,... | collective-permute-start | bytes 49160 | tf_op jit(solution)/shard_map/ppermute | solution.py:255
  50.8 3.9 %collective-permute-start.5 = (f32[16,256]{1,0:T(8,128)S(1)}, f32[16,256]{1,0:T(8,128)S(1)}, u32[]{:S(2)}, u32[]{:S(2)}) collective-permute-start(f32[16,256]{1,0:T(8,128)S(1)} %add.101), channel_id=1, source_target_pairs={{0,96},{8,104},{16,112},{24,120},{32,0},{40,8},{48,16},{56,24},{64... | collective-permute-start | bytes 49160 | tf_op jit(solution)/shard_map/ppermute | solution.py:255
  53.2 12.1 %collective-permute-start.13 = (f32[16,768]{1,0:T(8,128)S(1)}, f32[16,768]{1,0:T(8,128)S(1)}, u32[]{:S(2)}, u32[]{:S(2)}) collective-permute-start(f32[16,768]{1,0:T(8,128)S(1)} %slice.110), channel_id=1, source_target_pairs={{0,8},{8,0},{16,24},{24,16},{32,40},{40,32},{48,56},{56,48},{64,72... | collective-permute-start | bytes 147464 | tf_op jit(solution)/shard_map/ppermute | solution.py:247
  55.1 2.6 %collective-permute-start.8 = (f32[16,256]{1,0:T(8,128)S(1)}, f32[16,256]{1,0:T(8,128)S(1)}, u32[]{:S(2)}, u32[]{:S(2)}) collective-permute-start(f32[16,256]{1,0:T(8,128)S(1)} %convolution_subtract_fusion), channel_id=1, source_target_pairs={{0,8},{8,0},{16,24},{24,16},{32,40},{40,32},{48,56},{56,48},{64,72... | collective-permute-start | bytes 49160 | tf_op jit(solution)/shard_map/ppermute | solution.py:247
  57.7 3.6 %collective-permute-start.9 = (f32[16,256]{1,0:T(8,128)S(1)}, f32[16,256]{1,0:T(8,128)S(1)}, u32[]{:S(2)}, u32[]{:S(2)}) collective-permute-start(f32[16,256]{1,0:T(8,128)S(1)} %add.106), channel_id=1, source_target_pairs={{0,16},{8,24},{16,0},{24,8},{32,48},{40,56},{48,32},{56,40},{64,80... | collective-permute-start | bytes 49160 | tf_op jit(solution)/shard_map/ppermute | solution.py:252
  61.3 4.4 %collective-permute-start.11 = (f32[16,256]{1,0:T(8,128)S(1)}, f32[16,256]{1,0:T(8,128)S(1)}, u32[]{:S(2)}, u32[]{:S(2)}) collective-permute-start(f32[16,256]{1,0:T(8,128)S(1)} %add.107), channel_id=1, source_target_pairs={{0,64},{8,72},{16,80},{24,88},{32,96},{40,104},{48,112},{56,120},{... | collective-permute-start | bytes 49160 | tf_op jit(solution)/shard_map/ppermute | solution.py:255
  62.6 4.1 %collective-permute-start.12 = (f32[16,256]{1,0:T(8,128)S(1)}, f32[16,256]{1,0:T(8,128)S(1)}, u32[]{:S(2)}, u32[]{:S(2)}) collective-permute-start(f32[16,256]{1,0:T(8,128)S(1)} %add.107), channel_id=1, source_target_pairs={{0,32},{8,40},{16,48},{24,56},{32,64},{40,72},{48,80},{56,88},{64,... | collective-permute-start | bytes 49160 | tf_op jit(solution)/shard_map/ppermute | solution.py:255
  65.0 2.9 %collective-permute-start.10 = (f32[16,256]{1,0:T(8,128)S(1)}, f32[16,256]{1,0:T(8,128)S(1)}, u32[]{:S(2)}, u32[]{:S(2)}) collective-permute-start(f32[16,256]{1,0:T(8,128)S(1)} %add.107), channel_id=1, source_target_pairs={{0,96},{8,104},{16,112},{24,120},{32,0},{40,8},{48,16},{56,24},{64... | collective-permute-start | bytes 49160 | tf_op jit(solution)/shard_map/ppermute | solution.py:255
  68.6 4.6 %collective-permute-start.16 = (f32[16,768]{1,0:T(8,128)S(1)}, f32[16,768]{1,0:T(8,128)S(1)}, u32[]{:S(2)}, u32[]{:S(2)}) collective-permute-start(f32[16,768]{1,0:T(8,128)S(1)} %broadcast_select_fusion), channel_id=1, source_target_pairs={{112,48},{120,56},{113,49},{121,57},{114,50},{122,58},{115,51},{12... | collective-permute-start | bytes 147464 | tf_op jit(solution)/shard_map/ppermute | solution.py:272
  69.3 3.9 %collective-permute-start.15 = (f32[16,768]{1,0:T(8,128)S(1)}, f32[16,768]{1,0:T(8,128)S(1)}, u32[]{:S(2)}, u32[]{:S(2)}) collective-permute-start(f32[16,768]{1,0:T(8,128)S(1)} %broadcast_select_fusion), channel_id=1, source_target_pairs={{112,16},{120,24},{113,17},{121,25},{114,18},{122,26},{115,19},{12... | collective-permute-start | bytes 147464 | tf_op jit(solution)/shard_map/ppermute | solution.py:272
  69.9 3.2 %collective-permute-start.14 = (f32[16,768]{1,0:T(8,128)S(1)}, f32[16,768]{1,0:T(8,128)S(1)}, u32[]{:S(2)}, u32[]{:S(2)}) collective-permute-start(f32[16,768]{1,0:T(8,128)S(1)} %broadcast_select_fusion), channel_id=1, source_target_pairs={{112,80},{120,88},{113,81},{121,89},{114,82},{122,90},{115,83},{12... | collective-permute-start | bytes 147464 | tf_op jit(solution)/shard_map/ppermute | solution.py:272
  73.1 11.0 %copy-start.1 = (f32[2,1,16,768]{3,2,1,0:T(8,128)}, f32[2,1,16,768]{3,2,1,0:T(8,128)S(1)}, u32[]{:S(2)}) copy-start(f32[2,1,16,768]{3,2,1,0:T(8,128)S(1)} %shard_map.71.refs_1_) | copy-start | bytes 294916
  73.2 7.0 %collective-permute-start.17 = (f32[16,768]{1,0:T(8,128)S(1)}, f32[16,768]{1,0:T(8,128)S(1)}, u32[]{:S(2)}, u32[]{:S(2)}) collective-permute-start(f32[16,768]{1,0:T(8,128)S(1)} %add_add_fusion), channel_id=1, source_target_pairs={{16,0},{24,8},{48,32},{56,40},{80,64},{88,72},{112,96},{120,104},{... | collective-permute-start | bytes 147464 | tf_op jit(solution)/shard_map/ppermute | solution.py:275
  74.5 5.7 %copy-start.6 = (f32[4,192,768]{2,1,0:T(8,128)S(1)}, f32[4,192,768]{2,1,0:T(8,128)}, u32[]{:S(2)}) copy-start(f32[4,192,768]{2,1,0:T(8,128)} %shard_map.70) | copy-start | bytes 7077892
  74.5 9.6 %copy-start.4 = (f32[6,192,768]{2,1,0:T(8,128)S(1)}, f32[6,192,768]{2,1,0:T(8,128)}, u32[]{:S(2)}) copy-start(f32[6,192,768]{2,1,0:T(8,128)} %shard_map.69) | copy-start | bytes 10616836
  74.5 9.6 %collective-permute-start.20 = (f32[1,16,768]{2,1,0:T(8,128)S(1)}, f32[1,16,768]{2,1,0:T(8,128)S(1)}, u32[]{:S(2)}, u32[]{:S(2)}) collective-permute-start(f32[1,16,768]{2,1,0:T(8,128)S(1)} %slice_bitcast_fusion.1), channel_id=1, source_target_pairs={{0,8},{8,0},{16,24},{24,16},{32,40},{40,32},{48,56},{56,48},{64,72... | collective-permute-start | bytes 147464 | tf_op jit(solution)/shard_map/ppermute | solution.py:247
  80.2 18.1 %copy-start = (f32[2,2,16,768]{3,2,1,0:T(8,128)}, f32[2,2,16,768]{3,2,1,0:T(8,128)S(1)}, u32[]{:S(2)}) copy-start(f32[2,2,16,768]{3,2,1,0:T(8,128)S(1)} %shard_map.72.refs_0_) | copy-start | bytes 589828
  80.6 3.5 %collective-permute-start.19 = (f32[16,192]{1,0:T(8,128)S(1)}, f32[16,192]{1,0:T(8,128)S(1)}, u32[]{:S(2)}, u32[]{:S(2)}) collective-permute-start(f32[16,192]{1,0:T(8,128)S(1)} %fusion.39), channel_id=1, source_target_pairs={{0,8},{8,0},{16,24},{24,16},{32,40},{40,32},{48,56},{56,48},{64,72... | collective-permute-start | bytes 36872 | tf_op jit(solution)/shard_map/ppermute | solution.py:247
  84.4 5.3 %collective-permute-start.21 = (f32[16,768]{1,0:T(8,128)S(1)}, f32[16,768]{1,0:T(8,128)S(1)}, u32[]{:S(2)}, u32[]{:S(2)}) collective-permute-start(f32[16,768]{1,0:T(8,128)S(1)} %bitcast_subtract_fusion), channel_id=1, source_target_pairs={{0,16},{8,24},{16,0},{24,8},{32,48},{40,56},{48,32},{56,40},{64,80... | collective-permute-start | bytes 147464 | tf_op jit(solution)/shard_map/ppermute | solution.py:252
  86.2 12.1 %collective-permute-start.18 = (f32[2,16,768]{2,1,0:T(8,128)S(1)}, f32[2,16,768]{2,1,0:T(8,128)S(1)}, u32[]{:S(2)}, u32[]{:S(2)}) collective-permute-start(f32[2,16,768]{2,1,0:T(8,128)S(1)} %slice_bitcast_fusion), channel_id=1, source_target_pairs={{0,8},{8,0},{16,24},{24,16},{32,40},{40,32},{48,56},{56,48},{64,72... | collective-permute-start | bytes 294920 | tf_op jit(solution)/shard_map/ppermute | solution.py:247
  89.6 8.7 %copy-start.2 = (f32[16,2048]{1,0:T(8,128)}, f32[16,2048]{1,0:T(8,128)S(1)}, u32[]{:S(2)}) copy-start(f32[16,2048]{1,0:T(8,128)S(1)} %shard_map.73.first_ref) | copy-start | bytes 393220
  89.7 5.5 %collective-permute-start.23 = (f32[16,768]{1,0:T(8,128)S(1)}, f32[16,768]{1,0:T(8,128)S(1)}, u32[]{:S(2)}, u32[]{:S(2)}) collective-permute-start(f32[16,768]{1,0:T(8,128)S(1)} %add.116), channel_id=1, source_target_pairs={{0,64},{8,72},{16,80},{24,88},{32,96},{40,104},{48,112},{56,120},{... | collective-permute-start | bytes 147464 | tf_op jit(solution)/shard_map/ppermute | solution.py:255
  92.2 4.2 %collective-permute-start.24 = (f32[16,768]{1,0:T(8,128)S(1)}, f32[16,768]{1,0:T(8,128)S(1)}, u32[]{:S(2)}, u32[]{:S(2)}) collective-permute-start(f32[16,768]{1,0:T(8,128)S(1)} %add.116), channel_id=1, source_target_pairs={{0,32},{8,40},{16,48},{24,56},{32,64},{40,72},{48,80},{56,88},{64,... | collective-permute-start | bytes 147464 | tf_op jit(solution)/shard_map/ppermute | solution.py:255
  92.3 4.2 %collective-permute-start.22 = (f32[16,768]{1,0:T(8,128)S(1)}, f32[16,768]{1,0:T(8,128)S(1)}, u32[]{:S(2)}, u32[]{:S(2)}) collective-permute-start(f32[16,768]{1,0:T(8,128)S(1)} %add.116), channel_id=1, source_target_pairs={{0,96},{8,104},{16,112},{24,120},{32,0},{40,8},{48,16},{56,24},{64... | collective-permute-start | bytes 147464 | tf_op jit(solution)/shard_map/ppermute | solution.py:255
  96.7 2.4 %collective-permute-start.25 = (f32[16,192]{1,0:T(8,128)S(1)}, f32[16,192]{1,0:T(8,128)S(1)}, u32[]{:S(2)}, u32[]{:S(2)}) collective-permute-start(f32[16,192]{1,0:T(8,128)S(1)} %fusion.33), channel_id=1, source_target_pairs={{0,8},{8,0},{16,24},{24,16},{32,40},{40,32},{48,56},{56,48},{64,72... | collective-permute-start | bytes 36872 | tf_op jit(solution)/shard_map/ppermute | solution.py:247
  99.4 3.5 %collective-permute-start.26 = (f32[16,768]{1,0:T(8,128)S(1)}, f32[16,768]{1,0:T(8,128)S(1)}, u32[]{:S(2)}, u32[]{:S(2)}) collective-permute-start(f32[16,768]{1,0:T(8,128)S(1)} %fusion.59), channel_id=1, source_target_pairs={{0,16},{8,24},{16,0},{24,8},{32,48},{40,56},{48,32},{56,40},{64,80... | collective-permute-start | bytes 147464 | tf_op jit(solution)/shard_map/ppermute | solution.py:252
  100.2 6.7 %copy-start.5 = (f32[6,192,768]{2,1,0:T(8,128)S(1)}, f32[6,192,768]{2,1,0:T(8,128)}, u32[]{:S(2)}) copy-start(f32[6,192,768]{2,1,0:T(8,128)} %shard_map.69) | copy-start | bytes 10616836
  102.9 11.7 %copy-start.3 = (f32[2,1,16,768]{3,2,1,0:T(8,128)}, f32[2,1,16,768]{3,2,1,0:T(8,128)S(1)}, u32[]{:S(2)}) copy-start(f32[2,1,16,768]{3,2,1,0:T(8,128)S(1)} %shard_map.74.refs_2_) | copy-start | bytes 294916
  102.9 4.5 %collective-permute-start.28 = (f32[16,768]{1,0:T(8,128)S(1)}, f32[16,768]{1,0:T(8,128)S(1)}, u32[]{:S(2)}, u32[]{:S(2)}) collective-permute-start(f32[16,768]{1,0:T(8,128)S(1)} %add.121), channel_id=1, source_target_pairs={{0,64},{8,72},{16,80},{24,88},{32,96},{40,104},{48,112},{56,120},{... | collective-permute-start | bytes 147464 | tf_op jit(solution)/shard_map/ppermute | solution.py:255
  104.2 4.2 %collective-permute-start.29 = (f32[16,768]{1,0:T(8,128)S(1)}, f32[16,768]{1,0:T(8,128)S(1)}, u32[]{:S(2)}, u32[]{:S(2)}) collective-permute-start(f32[16,768]{1,0:T(8,128)S(1)} %add.121), channel_id=1, source_target_pairs={{0,32},{8,40},{16,48},{24,56},{32,64},{40,72},{48,80},{56,88},{64,... | collective-permute-start | bytes 147464 | tf_op jit(solution)/shard_map/ppermute | solution.py:255
  106.5 3.8 %collective-permute-start.27 = (f32[16,768]{1,0:T(8,128)S(1)}, f32[16,768]{1,0:T(8,128)S(1)}, u32[]{:S(2)}, u32[]{:S(2)}) collective-permute-start(f32[16,768]{1,0:T(8,128)S(1)} %add.121), channel_id=1, source_target_pairs={{0,96},{8,104},{16,112},{24,120},{32,0},{40,8},{48,16},{56,24},{64... | collective-permute-start | bytes 147464 | tf_op jit(solution)/shard_map/ppermute | solution.py:255
  110.6 2.8 %collective-permute-start.30 = (f32[16,192]{1,0:T(8,128)S(1)}, f32[16,192]{1,0:T(8,128)S(1)}, u32[]{:S(2)}, u32[]{:S(2)}) collective-permute-start(f32[16,192]{1,0:T(8,128)S(1)} %fusion.25), channel_id=1, source_target_pairs={{0,8},{8,0},{16,24},{24,16},{32,40},{40,32},{48,56},{56,48},{64,72... | collective-permute-start | bytes 36872 | tf_op jit(solution)/shard_map/ppermute | solution.py:247
  113.7 3.0 %collective-permute-start.31 = (f32[16,768]{1,0:T(8,128)S(1)}, f32[16,768]{1,0:T(8,128)S(1)}, u32[]{:S(2)}, u32[]{:S(2)}) collective-permute-start(f32[16,768]{1,0:T(8,128)S(1)} %fusion.63), channel_id=1, source_target_pairs={{0,16},{8,24},{16,0},{24,8},{32,48},{40,56},{48,32},{56,40},{64,80... | collective-permute-start | bytes 147464 | tf_op jit(solution)/shard_map/ppermute | solution.py:252
  116.7 4.5 %collective-permute-start.33 = (f32[16,768]{1,0:T(8,128)S(1)}, f32[16,768]{1,0:T(8,128)S(1)}, u32[]{:S(2)}, u32[]{:S(2)}) collective-permute-start(f32[16,768]{1,0:T(8,128)S(1)} %add.126), channel_id=1, source_target_pairs={{0,64},{8,72},{16,80},{24,88},{32,96},{40,104},{48,112},{56,120},{... | collective-permute-start | bytes 147464 | tf_op jit(solution)/shard_map/ppermute | solution.py:255
  117.4 4.3 %collective-permute-start.34 = (f32[16,768]{1,0:T(8,128)S(1)}, f32[16,768]{1,0:T(8,128)S(1)}, u32[]{:S(2)}, u32[]{:S(2)}) collective-permute-start(f32[16,768]{1,0:T(8,128)S(1)} %add.126), channel_id=1, source_target_pairs={{0,32},{8,40},{16,48},{24,56},{32,64},{40,72},{48,80},{56,88},{64,... | collective-permute-start | bytes 147464 | tf_op jit(solution)/shard_map/ppermute | solution.py:255
  118.9 3.1 %collective-permute-start.32 = (f32[16,768]{1,0:T(8,128)S(1)}, f32[16,768]{1,0:T(8,128)S(1)}, u32[]{:S(2)}, u32[]{:S(2)}) collective-permute-start(f32[16,768]{1,0:T(8,128)S(1)} %add.126), channel_id=1, source_target_pairs={{0,96},{8,104},{16,112},{24,120},{32,0},{40,8},{48,16},{56,24},{64... | collective-permute-start | bytes 147464 | tf_op jit(solution)/shard_map/ppermute | solution.py:255
  122.2 4.0 %collective-permute-start.35 = (f32[16,192]{1,0:T(8,128)S(1)}, f32[16,192]{1,0:T(8,128)S(1)}, u32[]{:S(2)}, u32[]{:S(2)}) collective-permute-start(f32[16,192]{1,0:T(8,128)S(1)} %fusion.21), channel_id=1, source_target_pairs={{0,8},{8,0},{16,24},{24,16},{32,40},{40,32},{48,56},{56,48},{64,72... | collective-permute-start | bytes 36872 | tf_op jit(solution)/shard_map/ppermute | solution.py:247

commit v5 on v4

--- a/solution.py
+++ b/solution.py
@@ -128,10 +128,10 @@
             start(i + slots)
 
 
-def products_kernel(z_ref, v_ref, flat_ref, p1_ref, p0_ref, held, sems):
+def first_products_kernel(z_ref, v_ref, flat_ref, p_ref, held, sems):
     unit = held.shape[2]
     _, per, subs, lanes = z_ref.shape
-    sums = [jnp.zeros(p1_ref.shape, jnp.float32) for _ in range(2)]
+    sums = [jnp.zeros(p_ref.shape, jnp.float32)]
 
     def use(i, v_ref):
         columns = []
@@ -140,30 +140,52 @@
             columns.append(jnp.concatenate(rows, axis=0))
         z = jnp.concatenate(columns, axis=1)
         flat_ref[:, i * unit : (i + 1) * unit] = z
-        z = split(z)
-        for which in range(2):
-            sums[which] = sums[which] + dot_split(z, split(v_ref[which]), NN)
-
-    streamed(v_ref, held, sems, (0, 1), 0, subs * lanes // unit, use)
-    p1_ref[...] = sums[1]
-    p0_ref[...] = sums[0]
-
-
-def products_of(received, reflectors):
+        sums[0] = sums[0] + dot_split(split(z), split(v_ref[0]), NN)
+
+    streamed(v_ref, held, sems, (1,), 0, subs * lanes // unit, use)
+    p_ref[...] = sums[0]
+
+
+def second_products_kernel(z_ref, v_ref, p_ref, held, sems):
+    unit = held.shape[2]
+    sums = [jnp.zeros(p_ref.shape, jnp.float32)]
+
+    def use(i, v_ref):
+        z = split(z_ref[:, i * unit : (i + 1) * unit])
+        sums[0] = sums[0] + dot_split(z, split(v_ref[0]), NN)
+
+    streamed(v_ref, held, sems, (0,), 0, z_ref.shape[1] // unit, use)
+    p_ref[...] = sums[0]
+
+
+def products_call(kernel, z, reflectors, outs):
+    rows, block = outs[-1].shape
+    return pl.pallas_call(
+        kernel,
+        out_shape=outs,
+        in_specs=in_vmem(1) + [pl.BlockSpec(memory_space=pl.ANY)],
+        out_specs=in_vmem(len(outs)),
+        scratch_shapes=held_pieces(block, 1, 1024, 6),
+        compiler_params=BIG,
+        cost_estimate=pl.CostEstimate(
+            flops=6 * z.size * block,
+            bytes_accessed=z.size,
+            transcendentals=0,
+        ),
+    )(z, reflectors)
+
+
+def first_products(received, reflectors):
     parts, per, subs, lanes = received.shape
     rows = parts * per
-    length = subs * lanes
-    block = reflectors.shape[2]
-    sums = jax.ShapeDtypeStruct((rows, block), jnp.float32)
-    return pl.pallas_call(
-        products_kernel,
-        out_shape=[jax.ShapeDtypeStruct((rows, length), jnp.float32), sums, sums],
-        in_specs=in_vmem(1) + [pl.BlockSpec(memory_space=pl.ANY)],
-        out_specs=in_vmem(3),
-        scratch_shapes=held_pieces(block, 2, 1024, 4),
-        compiler_params=BIG,
-        cost_estimate=dot_cost(rows, length, 2 * block),
-    )(received, reflectors)
+    flat = jax.ShapeDtypeStruct((rows, subs * lanes), jnp.float32)
+    sums = jax.ShapeDtypeStruct((rows, reflectors.shape[2]), jnp.float32)
+    return products_call(first_products_kernel, received, reflectors, [flat, sums])
+
+
+def second_products(flat, reflectors):
+    sums = jax.ShapeDtypeStruct((flat.shape[0], reflectors.shape[2]), jnp.float32)
+    return products_call(second_products_kernel, flat, reflectors, [sums])[0]
 
 
 def pieces_of(z_ref, z_first, coeffs, v_ref, held, sems, which, first, count, write):
@@ -334,14 +356,16 @@
     received, later = lax.optimization_barrier((received, reflectors))
     received = lax.all_to_all(received, "narrow", 0, 0, tiled=True)
     gram = gram + gram_of(later, length // 2, length)
-    v_mine = jnp.where(is_owner, reflectors[:, last + half :], v_low)
-    received, gram, v_mine = lax.optimization_barrier((received, gram, v_mine))
+    l_pair = half_pair(weights[1], traded[1], half)
+    received, gram, l_pair = lax.optimization_barrier((received, gram, l_pair))
     per = wide_size // narrow_size
     received = received.reshape(narrow_size, per, subs, 128)
-    flat, first, second = products_of(received, reflectors)
+    flat, first = first_products(received, reflectors)
     z_mine = jnp.where(is_owner, flat[:, last + half :], swapped(flat[:, last : last + half]))
-    first, weights, traded = lax.optimization_barrier((first, weights, traded))
-    first, l_pair = summed_over_wide(first, half_pair(weights[1], traded[1], half))
+    first, later, v_low = lax.optimization_barrier((first, reflectors, v_low))
+    first, second = summed_over_wide(first, second_products(flat, later))
+    v_mine = jnp.where(is_owner, later[:, last + half :], v_low)
+    first, v_mine = lax.optimization_barrier((first, v_mine))
     coeffs1 = dot(first, triangles[1].T)
     second = second - dot(coeffs1, gram)
     second, weights, traded = lax.optimization_barrier((second, weights, traded))

time: 127 us -> 127 us (level)
  waiting for transfers between devices: 15.9 us -> 14 us
  starting transfers between devices: 60.9 us -> 59.3 us
  Pallas kernels: 26.2 us -> 27.7 us
    ppermute x12, starting transfers between devices: 19.3 us -> 17.8 us  [swapped(): return lax.ppermute(array, 'wide', [(i, i ^ 1) for i in range(size)])]
    pallas_call x1 -> x2, Pallas kernels: 6.57 us -> 8.13 us  [products_call(): pl.pallas_call(kernel, out_shape=outs, in_specs=in_vmem(1) + [pl.BlockSpe...]
  transfers between devices with their start and end apart: 38 -> 38, of which waited for: 18 -> 19; matrix products, arithmetic and copies ran while one was open for 16% -> 17% of each run, Pallas kernels for 21% -> 22%
where the time goes in v5:
time: 127 us; the launch traced here: 126 us
  starting transfers between devices  59.3 us (47%)
  Pallas kernels  27.7 us (22%)
  matrix products  18.1 us (14%)
  waiting for transfers between devices  14 us (11%)
  local copies, waits for them, and re-layouts  3.37 us (3%)
  other arithmetic  2.57 us (2%)
    ppermute x15, starting transfers between devices, from_chips(): lax.ppermute(array, 'wide', [(i, (i + by) % size) for i in range(size)])  21.1 us
    ppermute x12, starting transfers between devices, swapped(): return lax.ppermute(array, 'wide', [(i, i ^ 1) for i in range(size)])  17.8 us
    dot_general x2, matrix products, gram_of(): lax.dot_general(reflectors[1, lo:hi], reflectors[0, lo:hi], (((0,), (0,))...  13.8 us
    pallas_call x4, Pallas kernels, updated(): pl.pallas_call(functools.partial(update_kernel, z_first, first, which), o...  11.7 us
    ppermute x15, waiting for transfers between devices, from_chips(): lax.ppermute(array, 'wide', [(i, (i + by) % size) for i in range(size)])  8.48 us
    pallas_call x2, Pallas kernels, products_call(): pl.pallas_call(kernel, out_shape=outs, in_specs=in_vmem(1) + [pl.BlockSpe...  8.13 us
    all_to_all x1, starting transfers between devices, body(): received = lax.all_to_all(received, 'wide', 0, 0, tiled=True)  6.54 us
    all_to_all x1, starting transfers between devices, body(): received = lax.all_to_all(received, 'narrow', 0, 0, tiled=True)  6.36 us
  transfers between devices with their start and end apart: 38, of which 19 were waited for; matrix products, arithmetic and copies ran while one was open for 17% of the time, Pallas kernels for 22%

profile of v5, /device:TPU:1, one launch (start us, length us, event | category | flops | bytes accessed | tf_op | source)
XLA Modules:
  0.0 126.2 jit_solution(11012957479090963862)
XLA Ops:
  0.6 1.5 %collective-permute-start = (f32[6,96,1536]{2,1,0:T(8,128)}, f32[6,96,1536]{2,1,0:T(8,128)}, u32[]{:S(2)}, u32[]{:S(2)}) collective-permute-start(f32[6,96,1536]{2,1,0:T(8,128)} %own_ref.1), channel_id=1, source_target_pairs={{0,8},{8,0},{16,24},{24,16},{32,40},{40,32},{48,56},{56,48},{64,72... | collective-permute-start | bytes 10616840 | tf_op jit(solution)/shard_map/ppermute | solution.py:269
  2.1 6.5 %all-to-all-start = ((f32[16,64,128]{2,1,0:T(8,128)}), f32[16,64,128]{2,1,0:T(8,128)}, u32[]{:S(2)}, u32[]{:S(2)}) async-start(f32[16,64,128]{2,1,0:T(8,128)} %bitcast.120), calls=%async_computation | async-start | bytes 1048576 | tf_op jit(solution)/shard_map/all_to_all | solution.py:350
  8.7 6.9 %fusion.3 = f32[256,256]{1,0:T(8,128)S(1)} fusion(f32[2,8192,256]{2,1,0:T(8,128)} %v_ref.10), kind=kOutput, calls=%fused_computation.3 | convolution fusion | flops 1610612736 | bytes 8650752 | tf_op jit(solution)/shard_map/dot_general | solution.py:329
  15.6 2.7 %slice.104 = f32[2,768,256]{2,1,0:T(8,128)} slice(f32[2,8192,256]{2,1,0:T(8,128)} %v_ref.10), slice={[0:2], [6656:7424], [0:256]} | slice | bytes 3145728 | tf_op jit(solution)/shard_map/slice | solution.py:353
  18.2 0.3 all-to-all-done
  18.6 1.2 collective-permute-start.1
  19.7 6.4 %all-to-all-start.1 = ((f32[16,64,128]{2,1,0:T(8,128)}), f32[16,64,128]{2,1,0:T(8,128)S(1)}, u32[]{:S(2)}, u32[]{:S(2)}) async-start(f32[16,64,128]{2,1,0:T(8,128)} %all-to-all-done), calls=%async_computation.1 | async-start | bytes 1048576 | tf_op jit(solution)/shard_map/all_to_all | solution.py:357
  26.1 6.9 %fusion.10 = f32[256,256]{1,0:T(8,128)S(1)} fusion(f32[256,256]{1,0:T(8,128)S(1)} %fusion.3, f32[2,8192,256]{2,1,0:T(8,128)} %v_ref.10), kind=kOutput, calls=%fused_computation.11 | convolution fusion | flops 1610678272 | bytes 8912896 | tf_op jit(solution)/shard_map/dot_general | solution.py:329
  33.0 3.3 %shard_map.68 = f32[6,192,768]{2,1,0:T(8,128)} custom-call(s32[1]{0:T(128)} %bitcast.5.core_ref, f32[6,96,1536]{2,1,0:T(8,128)} %own_ref.1, f32[6,96,1536]{2,1,0:T(8,128)} %collective-permute-done.other_ref), custom_call_target="tpu_custom_call" | custom-call | bytes 884736 | tf_op jit(solution)/shard_map/pallas_call | solution.py:86
  36.3 0.4 all-to-all-done.1
  36.7 4.1 %shard_map.69 = (f32[16,8192]{1,0:T(8,128)S(1)}, f32[16,256]{1,0:T(8,128)S(1)}) custom-call(f32[8,2,64,128]{3,2,1,0:T(8,128)S(1)} %bitcast.119, f32[2,8192,256]{2,1,0:T(8,128)} %v_ref.10), custom_call_target="tpu_custom_call" | custom-call | flops 201326592 | bytes 131072 | tf_op jit(solution)/shard_map/pallas_call | solution.py:163
  40.8 1.4 %collective-permute-start.2 = (f32[16,256]{1,0:T(8,128)S(1)}, f32[16,256]{1,0:T(8,128)S(1)}, u32[]{:S(2)}, u32[]{:S(2)}) collective-permute-start(f32[16,256]{1,0:T(8,128)S(1)} %get-tuple-element.61), channel_id=1, source_target_pairs={{0,8},{8,0},{16,24},{24,16},{32,40},{40,32},{48,56},{56,48},{64,72... | collective-permute-start | bytes 49160 | tf_op jit(solution)/shard_map/ppermute | solution.py:269
  42.2 0.7 collective-permute-done.2
  43.0 4.1 %shard_map.70 = f32[16,256]{1,0:T(8,128)S(1)} custom-call(f32[16,8192]{1,0:T(8,128)S(1)} %get-tuple-element.62.z_ref, f32[2,8192,256]{2,1,0:T(8,128)} %v_ref.10), custom_call_target="tpu_custom_call" | custom-call | flops 201326592 | bytes 131072 | tf_op jit(solution)/shard_map/pallas_call | solution.py:163
  47.1 2.5 %collective-permute-start.5 = (f32[16,256]{1,0:T(8,128)S(1)}, f32[16,256]{1,0:T(8,128)S(1)}, u32[]{:S(2)}, u32[]{:S(2)}) collective-permute-start(f32[16,256]{1,0:T(8,128)S(1)} %add.102), channel_id=1, source_target_pairs={{0,64},{8,72},{16,80},{24,88},{32,96},{40,104},{48,112},{56,120},{... | collective-permute-start | bytes 49160 | tf_op jit(solution)/shard_map/ppermute | solution.py:277
  49.9 2.4 %collective-permute-start.4 = (f32[16,256]{1,0:T(8,128)S(1)}, f32[16,256]{1,0:T(8,128)S(1)}, u32[]{:S(2)}, u32[]{:S(2)}) collective-permute-start(f32[16,256]{1,0:T(8,128)S(1)} %add.102), channel_id=1, source_target_pairs={{0,96},{8,104},{16,112},{24,120},{32,0},{40,8},{48,16},{56,24},{64... | collective-permute-start | bytes 49160 | tf_op jit(solution)/shard_map/ppermute | solution.py:277
  52.3 2.1 %slice_select_fusion = f32[2,768,256]{2,1,0:T(8,128)S(1)} fusion(f32[2,768,256]{2,1,0:T(8,128)} %copy-done.7, f32[2,8192,256]{2,1,0:T(8,128)} %v_ref.10, pred[]{:T(512)S(6)} %eq.12), kind=kLoop, calls=%fused_computation.10 | loop fusion | flops 393216 | bytes 4718593 | tf_op jit(solution)/shard_map/jit(_where)/select_n | solution.py:367
  54.9 1.5 %collective-permute-start.8 = (f32[16,256]{1,0:T(8,128)S(1)}, f32[16,256]{1,0:T(8,128)S(1)}, u32[]{:S(2)}, u32[]{:S(2)}) collective-permute-start(f32[16,256]{1,0:T(8,128)S(1)} %sub.27), channel_id=1, source_target_pairs={{0,8},{8,0},{16,24},{24,16},{32,40},{40,32},{48,56},{56,48},{64,72... | collective-permute-start | bytes 49160 | tf_op jit(solution)/shard_map/ppermute | solution.py:269
  56.5 0.8 collective-permute-done.8
  57.3 0.9 collective-permute-start.9
  58.2 2.7 %shard_map.71 = f32[4,192,768]{2,1,0:T(8,128)} custom-call(s32[1]{0:T(128)} %bitcast.5.core_ref, f32[4,96,1536]{2,1,0:T(8,128)} %bitcast.8.own_ref, f32[4,96,1536]{2,1,0:T(8,128)} %collective-permute-done.7.other_ref), custom_call_target="tpu_custom_call" | custom-call | bytes 589824 | tf_op jit(solution)/shard_map/pallas_call | solution.py:86
  60.9 0.8 collective-permute-start.11
  61.8 2.3 %collective-permute-start.12 = (f32[16,256]{1,0:T(8,128)S(1)}, f32[16,256]{1,0:T(8,128)S(1)}, u32[]{:S(2)}, u32[]{:S(2)}) collective-permute-start(f32[16,256]{1,0:T(8,128)S(1)} %add.107), channel_id=1, source_target_pairs={{0,32},{8,40},{16,48},{24,56},{32,64},{40,72},{48,80},{56,88},{64,... | collective-permute-start | bytes 49160 | tf_op jit(solution)/shard_map/ppermute | solution.py:277
  64.1 0.3 collective-permute-start.10
  64.5 0.5 select_subtract_fusion
  65.1 0.5 collective-permute-done.12
  65.6 1.4 %collective-permute-done.10 = f32[16,256]{1,0:T(8,128)S(1)} collective-permute-done((f32[16,256]{1,0:T(8,128)S(1)}, f32[16,256]{1,0:T(8,128)S(1)}, u32[]{:S(2)}, u32[]{:S(2)}) %collective-permute-start.10) | collective-permute-done | bytes 16416 | tf_op jit(solution)/shard_map/ppermute | solution.py:277
  67.2 0.5 fusion.15
  67.8 0.7 collective-permute-start.16
  68.5 0.7 collective-permute-start.15
  69.1 0.7 collective-permute-start.14
  69.8 2.5 %shard_map.72.refs_1_ = f32[2,1,16,768]{3,2,1,0:T(8,128)S(1)} custom-call(f32[16,8192]{1,0:T(8,128)S(1)} %get-tuple-element.62.z_ref, f32[2,8192,256]{2,1,0:T(8,128)} %v_ref.10, f32[16,256]{1,0:T(8,128)S(1)} %fusion.53.refs_0_, f32[16,256]{1,0:T(8,128)S(1)} %fusion.51.refs_1_), custom_call_target="tpu_custom_call" | custom-call | flops 75497472 | bytes 3276800 | tf_op jit(solution)/shard_map/pallas_call | solution.py:230
  72.4 1.3 %collective-permute-start.17 = (f32[16,768]{1,0:T(8,128)S(1)}, f32[16,768]{1,0:T(8,128)S(1)}, u32[]{:S(2)}, u32[]{:S(2)}) collective-permute-start(f32[16,768]{1,0:T(8,128)S(1)} %add_add_fusion), channel_id=1, source_target_pairs={{16,0},{24,8},{48,32},{56,40},{80,64},{88,72},{112,96},{120,104},{... | collective-permute-start | bytes 147464 | tf_op jit(solution)/shard_map/ppermute | solution.py:297
  73.7 2.1 %collective-permute-start.20 = (f32[1,16,768]{2,1,0:T(8,128)S(1)}, f32[1,16,768]{2,1,0:T(8,128)S(1)}, u32[]{:S(2)}, u32[]{:S(2)}) collective-permute-start(f32[1,16,768]{2,1,0:T(8,128)S(1)} %slice_bitcast_fusion.1), channel_id=1, source_target_pairs={{0,8},{8,0},{16,24},{24,16},{32,40},{40,32},{48,56},{56,48},{64,72... | collective-permute-start | bytes 147464 | tf_op jit(solution)/shard_map/ppermute | solution.py:269
  75.8 3.6 %shard_map.73.refs_0_ = f32[2,2,16,768]{3,2,1,0:T(8,128)S(1)} custom-call(f32[16,8192]{1,0:T(8,128)S(1)} %get-tuple-element.62.z_ref, f32[2,8192,256]{2,1,0:T(8,128)} %v_ref.10, f32[16,256]{1,0:T(8,128)S(1)} %fusion.53.refs_0_, f32[16,256]{1,0:T(8,128)S(1)} %fusion.51.refs_1_), custom_call_target="tpu_custom_call" | custom-call | flops 150994944 | bytes 6520832 | tf_op jit(solution)/shard_map/pallas_call | solution.py:230
  79.8 2.7 %collective-permute-start.19 = (f32[16,192]{1,0:T(8,128)S(1)}, f32[16,192]{1,0:T(8,128)S(1)}, u32[]{:S(2)}, u32[]{:S(2)}) collective-permute-start(f32[16,192]{1,0:T(8,128)S(1)} %fusion.39), channel_id=1, source_target_pairs={{0,8},{8,0},{16,24},{24,16},{32,40},{40,32},{48,56},{56,48},{64,72... | collective-permute-start | bytes 36872 | tf_op jit(solution)/shard_map/ppermute | solution.py:269
  82.5 0.8 collective-permute-done.19
  83.6 1.8 %collective-permute-start.21 = (f32[16,768]{1,0:T(8,128)S(1)}, f32[16,768]{1,0:T(8,128)S(1)}, u32[]{:S(2)}, u32[]{:S(2)}) collective-permute-start(f32[16,768]{1,0:T(8,128)S(1)} %bitcast_subtract_fusion), channel_id=1, source_target_pairs={{0,16},{8,24},{16,0},{24,8},{32,48},{40,56},{48,32},{56,40},{64,80... | collective-permute-start | bytes 147464 | tf_op jit(solution)/shard_map/ppermute | solution.py:274
  85.4 0.5 collective-permute-start.18
  86.0 2.9 %shard_map.74.first_ref = f32[16,2048]{1,0:T(8,128)S(1)} custom-call(f32[16,8192]{1,0:T(8,128)S(1)} %get-tuple-element.62.z_ref, f32[2,8192,256]{2,1,0:T(8,128)} %v_ref.10, f32[16,256]{1,0:T(8,128)S(1)} %fusion.53.refs_0_, f32[16,256]{1,0:T(8,128)S(1)} %fusion.51.refs_1_), custom_call_target="tpu_custom_call" | custom-call | flops 100663296 | bytes 4358144 | tf_op jit(solution)/shard_map/pallas_call | solution.py:230
  88.9 2.6 %collective-permute-start.23 = (f32[16,768]{1,0:T(8,128)S(1)}, f32[16,768]{1,0:T(8,128)S(1)}, u32[]{:S(2)}, u32[]{:S(2)}) collective-permute-start(f32[16,768]{1,0:T(8,128)S(1)} %add.116), channel_id=1, source_target_pairs={{0,64},{8,72},{16,80},{24,88},{32,96},{40,104},{48,112},{56,120},{... | collective-permute-start | bytes 147464 | tf_op jit(solution)/shard_map/ppermute | solution.py:277
  91.5 2.7 %collective-permute-start.22 = (f32[16,768]{1,0:T(8,128)S(1)}, f32[16,768]{1,0:T(8,128)S(1)}, u32[]{:S(2)}, u32[]{:S(2)}) collective-permute-start(f32[16,768]{1,0:T(8,128)S(1)} %add.116), channel_id=1, source_target_pairs={{0,96},{8,104},{16,112},{24,120},{32,0},{40,8},{48,16},{56,24},{64... | collective-permute-start | bytes 147464 | tf_op jit(solution)/shard_map/ppermute | solution.py:277
  94.4 1.2 collective-permute-done.24
  95.9 1.6 %collective-permute-start.25 = (f32[16,192]{1,0:T(8,128)S(1)}, f32[16,192]{1,0:T(8,128)S(1)}, u32[]{:S(2)}, u32[]{:S(2)}) collective-permute-start(f32[16,192]{1,0:T(8,128)S(1)} %fusion.33), channel_id=1, source_target_pairs={{0,8},{8,0},{16,24},{24,16},{32,40},{40,32},{48,56},{56,48},{64,72... | collective-permute-start | bytes 36872 | tf_op jit(solution)/shard_map/ppermute | solution.py:269
  97.5 0.8 collective-permute-done.25
  98.6 0.8 collective-permute-start.26
  99.4 2.7 %shard_map.75.refs_2_ = f32[2,1,16,768]{3,2,1,0:T(8,128)S(1)} custom-call(f32[16,8192]{1,0:T(8,128)S(1)} %get-tuple-element.62.z_ref, f32[2,8192,256]{2,1,0:T(8,128)} %v_ref.10, f32[16,256]{1,0:T(8,128)S(1)} %fusion.53.refs_0_, f32[16,256]{1,0:T(8,128)S(1)} %fusion.51.refs_1_), custom_call_target="tpu_custom_call" | custom-call | flops 75497472 | bytes 3276800 | tf_op jit(solution)/shard_map/pallas_call | solution.py:230
  102.1 1.3 %collective-permute-start.28 = (f32[16,768]{1,0:T(8,128)S(1)}, f32[16,768]{1,0:T(8,128)S(1)}, u32[]{:S(2)}, u32[]{:S(2)}) collective-permute-start(f32[16,768]{1,0:T(8,128)S(1)} %add.121), channel_id=1, source_target_pairs={{0,64},{8,72},{16,80},{24,88},{32,96},{40,104},{48,112},{56,120},{... | collective-permute-start | bytes 147464 | tf_op jit(solution)/shard_map/ppermute | solution.py:277
  103.4 2.3 %collective-permute-start.29 = (f32[16,768]{1,0:T(8,128)S(1)}, f32[16,768]{1,0:T(8,128)S(1)}, u32[]{:S(2)}, u32[]{:S(2)}) collective-permute-start(f32[16,768]{1,0:T(8,128)S(1)} %add.121), channel_id=1, source_target_pairs={{0,32},{8,40},{16,48},{24,56},{32,64},{40,72},{48,80},{56,88},{64,... | collective-permute-start | bytes 147464 | tf_op jit(solution)/shard_map/ppermute | solution.py:277
  105.7 0.3 collective-permute-start.27
  106.6 0.9 collective-permute-done.29
  107.5 2.0 %collective-permute-done.27 = f32[16,768]{1,0:T(8,128)S(1)} collective-permute-done((f32[16,768]{1,0:T(8,128)S(1)}, f32[16,768]{1,0:T(8,128)S(1)}, u32[]{:S(2)}, u32[]{:S(2)}) %collective-permute-start.27) | collective-permute-done | bytes 49184 | tf_op jit(solution)/shard_map/ppermute | solution.py:277
  109.8 2.0 %collective-permute-start.30 = (f32[16,192]{1,0:T(8,128)S(1)}, f32[16,192]{1,0:T(8,128)S(1)}, u32[]{:S(2)}, u32[]{:S(2)}) collective-permute-start(f32[16,192]{1,0:T(8,128)S(1)} %fusion.25), channel_id=1, source_target_pairs={{0,8},{8,0},{16,24},{24,16},{32,40},{40,32},{48,56},{56,48},{64,72... | collective-permute-start | bytes 36872 | tf_op jit(solution)/shard_map/ppermute | solution.py:269
  112.0 0.6 collective-permute-done.30
  112.9 0.8 collective-permute-start.31
  113.7 1.9 %shard_map.76 = f32[16,8192]{1,0:T(8,128)} custom-call(f32[16,2048]{1,0:T(8,128)} %copy-done.2, f32[2,2,16,768]{3,2,1,0:T(8,128)} %copy-done, f32[2,1,16,768]{3,2,1,0:T(8,128)} %copy-done.1, f32[2,1,16,768]{3,2,1,0:T(8,128)} %copy-done.3), custom_call_target="tpu_custom_call" | custom-call | bytes 1048576 | tf_op jit(solution)/shard_map/pallas_call | solution.py:256
  115.9 0.5 collective-permute-start.33
  116.4 1.7 %collective-permute-start.34 = (f32[16,768]{1,0:T(8,128)S(1)}, f32[16,768]{1,0:T(8,128)S(1)}, u32[]{:S(2)}, u32[]{:S(2)}) collective-permute-start(f32[16,768]{1,0:T(8,128)S(1)} %add.126), channel_id=1, source_target_pairs={{0,32},{8,40},{16,48},{24,56},{32,64},{40,72},{48,80},{56,88},{64,... | collective-permute-start | bytes 147464 | tf_op jit(solution)/shard_map/ppermute | solution.py:277
  118.1 1.0 collective-permute-start.32
  119.1 1.3 %collective-permute-done.33 = f32[16,768]{1,0:T(8,128)S(1)} collective-permute-done((f32[16,768]{1,0:T(8,128)S(1)}, f32[16,768]{1,0:T(8,128)S(1)}, u32[]{:S(2)}, u32[]{:S(2)}) %collective-permute-start.33) | collective-permute-done | bytes 49184 | tf_op jit(solution)/shard_map/ppermute | solution.py:277
  120.5 0.5 collective-permute-done.34
  121.4 3.2 %collective-permute-start.35 = (f32[16,192]{1,0:T(8,128)S(1)}, f32[16,192]{1,0:T(8,128)S(1)}, u32[]{:S(2)}, u32[]{:S(2)}) collective-permute-start(f32[16,192]{1,0:T(8,128)S(1)} %fusion.21), channel_id=1, source_target_pairs={{0,8},{8,0},{16,24},{24,16},{32,40},{40,32},{48,56},{56,48},{64,72... | collective-permute-start | bytes 36872 | tf_op jit(solution)/shard_map/ppermute | solution.py:269
  124.7 0.8 collective-permute-done.35
  125.6 0.6 copy.7
  (86 shorter events, 5.3 us)
Async XLA Ops:
  0.6 32.4 %collective-permute-start = (f32[6,96,1536]{2,1,0:T(8,128)}, f32[6,96,1536]{2,1,0:T(8,128)}, u32[]{:S(2)}, u32[]{:S(2)}) collective-permute-start(f32[6,96,1536]{2,1,0:T(8,128)} %own_ref.1), channel_id=1, source_target_pairs={{0,8},{8,0},{16,24},{24,16},{32,40},{40,32},{48,56},{56,48},{64,72... | collective-permute-start | bytes 10616840 | tf_op jit(solution)/shard_map/ppermute | solution.py:269
  2.1 16.4 %all-to-all-start = ((f32[16,64,128]{2,1,0:T(8,128)}), f32[16,64,128]{2,1,0:T(8,128)}, u32[]{:S(2)}, u32[]{:S(2)}) async-start(f32[16,64,128]{2,1,0:T(8,128)} %bitcast.120), calls=%async_computation | async-start | bytes 1048576 | tf_op jit(solution)/shard_map/all_to_all | solution.py:350
  18.6 22.2 %collective-permute-start.1 = (f32[2,768,256]{2,1,0:T(8,128)}, f32[2,768,256]{2,1,0:T(8,128)S(1)}, u32[]{:S(2)}, u32[]{:S(2)}) collective-permute-start(f32[2,768,256]{2,1,0:T(8,128)} %slice.104), channel_id=1, source_target_pairs={{0,8},{8,0},{16,24},{24,16},{32,40},{40,32},{48,56},{56,48},{64,72... | collective-permute-start | bytes 4718600 | tf_op jit(solution)/shard_map/ppermute | solution.py:269
  19.7 35.2 %collective-permute-start.7 = (f32[4,96,1536]{2,1,0:T(8,128)}, f32[4,96,1536]{2,1,0:T(8,128)}, u32[]{:S(2)}, u32[]{:S(2)}) collective-permute-start(f32[4,96,1536]{2,1,0:T(8,128)} %bitcast.8.own_ref), channel_id=1, source_target_pairs={{0,8},{8,0},{16,24},{24,16},{32,40},{40,32},{48,56},{56,48},{64,72... | collective-permute-start | bytes 7077896 | tf_op jit(solution)/shard_map/ppermute | solution.py:269
  19.7 16.9 %all-to-all-start.1 = ((f32[16,64,128]{2,1,0:T(8,128)}), f32[16,64,128]{2,1,0:T(8,128)S(1)}, u32[]{:S(2)}, u32[]{:S(2)}) async-start(f32[16,64,128]{2,1,0:T(8,128)} %all-to-all-done), calls=%async_computation.1 | async-start | bytes 1048576 | tf_op jit(solution)/shard_map/all_to_all | solution.py:357
  40.7 6.3 %copy-start.7 = (f32[2,768,256]{2,1,0:T(8,128)}, f32[2,768,256]{2,1,0:T(8,128)S(1)}, u32[]{:S(2)}) copy-start(f32[2,768,256]{2,1,0:T(8,128)S(1)} %collective-permute-done.1) | copy-start | bytes 4718596
  40.8 2.2 %collective-permute-start.2 = (f32[16,256]{1,0:T(8,128)S(1)}, f32[16,256]{1,0:T(8,128)S(1)}, u32[]{:S(2)}, u32[]{:S(2)}) collective-permute-start(f32[16,256]{1,0:T(8,128)S(1)} %get-tuple-element.61), channel_id=1, source_target_pairs={{0,8},{8,0},{16,24},{24,16},{32,40},{40,32},{48,56},{56,48},{64,72... | collective-permute-start | bytes 49160 | tf_op jit(solution)/shard_map/ppermute | solution.py:269
  42.1 22.4 %collective-permute-start.13 = (f32[16,768]{1,0:T(8,128)S(1)}, f32[16,768]{1,0:T(8,128)S(1)}, u32[]{:S(2)}, u32[]{:S(2)}) collective-permute-start(f32[16,768]{1,0:T(8,128)S(1)} %slice.110), channel_id=1, source_target_pairs={{0,8},{8,0},{16,24},{24,16},{32,40},{40,32},{48,56},{56,48},{64,72... | collective-permute-start | bytes 147464 | tf_op jit(solution)/shard_map/ppermute | solution.py:269
  43.0 4.1 %collective-permute-start.3 = (f32[16,256]{1,0:T(8,128)S(1)}, f32[16,256]{1,0:T(8,128)S(1)}, u32[]{:S(2)}, u32[]{:S(2)}) collective-permute-start(f32[16,256]{1,0:T(8,128)S(1)} %add.101), channel_id=1, source_target_pairs={{0,16},{8,24},{16,0},{24,8},{32,48},{40,56},{48,32},{56,40},{64,80... | collective-permute-start | bytes 49160 | tf_op jit(solution)/shard_map/ppermute | solution.py:274
  47.1 7.4 %copy-start.8 = (f32[2,256,256]{2,1,0:T(8,128)S(1)}, f32[2,256,256]{2,1,0:T(8,128)}, u32[]{:S(2)}) copy-start(f32[2,256,256]{2,1,0:T(8,128)} %param.7) | copy-start | bytes 1572868
  47.1 7.3 %collective-permute-start.5 = (f32[16,256]{1,0:T(8,128)S(1)}, f32[16,256]{1,0:T(8,128)S(1)}, u32[]{:S(2)}, u32[]{:S(2)}) collective-permute-start(f32[16,256]{1,0:T(8,128)S(1)} %add.102), channel_id=1, source_target_pairs={{0,64},{8,72},{16,80},{24,88},{32,96},{40,104},{48,112},{56,120},{... | collective-permute-start | bytes 49160 | tf_op jit(solution)/shard_map/ppermute | solution.py:277
  49.6 4.8 %collective-permute-start.6 = (f32[16,256]{1,0:T(8,128)S(1)}, f32[16,256]{1,0:T(8,128)S(1)}, u32[]{:S(2)}, u32[]{:S(2)}) collective-permute-start(f32[16,256]{1,0:T(8,128)S(1)} %add.102), channel_id=1, source_target_pairs={{0,32},{8,40},{16,48},{24,56},{32,64},{40,72},{48,80},{56,88},{64,... | collective-permute-start | bytes 49160 | tf_op jit(solution)/shard_map/ppermute | solution.py:277
  49.9 4.5 %collective-permute-start.4 = (f32[16,256]{1,0:T(8,128)S(1)}, f32[16,256]{1,0:T(8,128)S(1)}, u32[]{:S(2)}, u32[]{:S(2)}) collective-permute-start(f32[16,256]{1,0:T(8,128)S(1)} %add.102), channel_id=1, source_target_pairs={{0,96},{8,104},{16,112},{24,120},{32,0},{40,8},{48,16},{56,24},{64... | collective-permute-start | bytes 49160 | tf_op jit(solution)/shard_map/ppermute | solution.py:277
  54.9 2.4 %collective-permute-start.8 = (f32[16,256]{1,0:T(8,128)S(1)}, f32[16,256]{1,0:T(8,128)S(1)}, u32[]{:S(2)}, u32[]{:S(2)}) collective-permute-start(f32[16,256]{1,0:T(8,128)S(1)} %sub.27), channel_id=1, source_target_pairs={{0,8},{8,0},{16,24},{24,16},{32,40},{40,32},{48,56},{56,48},{64,72... | collective-permute-start | bytes 49160 | tf_op jit(solution)/shard_map/ppermute | solution.py:269
  57.3 3.6 %collective-permute-start.9 = (f32[16,256]{1,0:T(8,128)S(1)}, f32[16,256]{1,0:T(8,128)S(1)}, u32[]{:S(2)}, u32[]{:S(2)}) collective-permute-start(f32[16,256]{1,0:T(8,128)S(1)} %add.106), channel_id=1, source_target_pairs={{0,16},{8,24},{16,0},{24,8},{32,48},{40,56},{48,32},{56,40},{64,80... | collective-permute-start | bytes 49160 | tf_op jit(solution)/shard_map/ppermute | solution.py:274
  60.9 4.2 %collective-permute-start.11 = (f32[16,256]{1,0:T(8,128)S(1)}, f32[16,256]{1,0:T(8,128)S(1)}, u32[]{:S(2)}, u32[]{:S(2)}) collective-permute-start(f32[16,256]{1,0:T(8,128)S(1)} %add.107), channel_id=1, source_target_pairs={{0,64},{8,72},{16,80},{24,88},{32,96},{40,104},{48,112},{56,120},{... | collective-permute-start | bytes 49160 | tf_op jit(solution)/shard_map/ppermute | solution.py:277
  61.8 3.8 %collective-permute-start.12 = (f32[16,256]{1,0:T(8,128)S(1)}, f32[16,256]{1,0:T(8,128)S(1)}, u32[]{:S(2)}, u32[]{:S(2)}) collective-permute-start(f32[16,256]{1,0:T(8,128)S(1)} %add.107), channel_id=1, source_target_pairs={{0,32},{8,40},{16,48},{24,56},{32,64},{40,72},{48,80},{56,88},{64,... | collective-permute-start | bytes 49160 | tf_op jit(solution)/shard_map/ppermute | solution.py:277
  64.1 2.9 %collective-permute-start.10 = (f32[16,256]{1,0:T(8,128)S(1)}, f32[16,256]{1,0:T(8,128)S(1)}, u32[]{:S(2)}, u32[]{:S(2)}) collective-permute-start(f32[16,256]{1,0:T(8,128)S(1)} %add.107), channel_id=1, source_target_pairs={{0,96},{8,104},{16,112},{24,120},{32,0},{40,8},{48,16},{56,24},{64... | collective-permute-start | bytes 49160 | tf_op jit(solution)/shard_map/ppermute | solution.py:277
  67.8 4.6 %collective-permute-start.16 = (f32[16,768]{1,0:T(8,128)S(1)}, f32[16,768]{1,0:T(8,128)S(1)}, u32[]{:S(2)}, u32[]{:S(2)}) collective-permute-start(f32[16,768]{1,0:T(8,128)S(1)} %broadcast_select_fusion), channel_id=1, source_target_pairs={{112,48},{120,56},{113,49},{121,57},{114,50},{122,58},{115,51},{12... | collective-permute-start | bytes 147464 | tf_op jit(solution)/shard_map/ppermute | solution.py:294
  68.5 3.9 %collective-permute-start.15 = (f32[16,768]{1,0:T(8,128)S(1)}, f32[16,768]{1,0:T(8,128)S(1)}, u32[]{:S(2)}, u32[]{:S(2)}) collective-permute-start(f32[16,768]{1,0:T(8,128)S(1)} %broadcast_select_fusion), channel_id=1, source_target_pairs={{112,16},{120,24},{113,17},{121,25},{114,18},{122,26},{115,19},{12... | collective-permute-start | bytes 147464 | tf_op jit(solution)/shard_map/ppermute | solution.py:294
  69.1 3.2 %collective-permute-start.14 = (f32[16,768]{1,0:T(8,128)S(1)}, f32[16,768]{1,0:T(8,128)S(1)}, u32[]{:S(2)}, u32[]{:S(2)}) collective-permute-start(f32[16,768]{1,0:T(8,128)S(1)} %broadcast_select_fusion), channel_id=1, source_target_pairs={{112,80},{120,88},{113,81},{121,89},{114,82},{122,90},{115,83},{12... | collective-permute-start | bytes 147464 | tf_op jit(solution)/shard_map/ppermute | solution.py:294
  72.3 11.0 %copy-start.1 = (f32[2,1,16,768]{3,2,1,0:T(8,128)}, f32[2,1,16,768]{3,2,1,0:T(8,128)S(1)}, u32[]{:S(2)}) copy-start(f32[2,1,16,768]{3,2,1,0:T(8,128)S(1)} %shard_map.72.refs_1_) | copy-start | bytes 294916
  72.4 7.1 %collective-permute-start.17 = (f32[16,768]{1,0:T(8,128)S(1)}, f32[16,768]{1,0:T(8,128)S(1)}, u32[]{:S(2)}, u32[]{:S(2)}) collective-permute-start(f32[16,768]{1,0:T(8,128)S(1)} %add_add_fusion), channel_id=1, source_target_pairs={{16,0},{24,8},{48,32},{56,40},{80,64},{88,72},{112,96},{120,104},{... | collective-permute-start | bytes 147464 | tf_op jit(solution)/shard_map/ppermute | solution.py:297
  73.7 5.8 %copy-start.6 = (f32[4,192,768]{2,1,0:T(8,128)S(1)}, f32[4,192,768]{2,1,0:T(8,128)}, u32[]{:S(2)}) copy-start(f32[4,192,768]{2,1,0:T(8,128)} %shard_map.71) | copy-start | bytes 7077892
  73.7 9.6 %copy-start.4 = (f32[6,192,768]{2,1,0:T(8,128)S(1)}, f32[6,192,768]{2,1,0:T(8,128)}, u32[]{:S(2)}) copy-start(f32[6,192,768]{2,1,0:T(8,128)} %shard_map.68) | copy-start | bytes 10616836
  73.7 9.6 %collective-permute-start.20 = (f32[1,16,768]{2,1,0:T(8,128)S(1)}, f32[1,16,768]{2,1,0:T(8,128)S(1)}, u32[]{:S(2)}, u32[]{:S(2)}) collective-permute-start(f32[1,16,768]{2,1,0:T(8,128)S(1)} %slice_bitcast_fusion.1), channel_id=1, source_target_pairs={{0,8},{8,0},{16,24},{24,16},{32,40},{40,32},{48,56},{56,48},{64,72... | collective-permute-start | bytes 147464 | tf_op jit(solution)/shard_map/ppermute | solution.py:269
  79.4 18.1 %copy-start = (f32[2,2,16,768]{3,2,1,0:T(8,128)}, f32[2,2,16,768]{3,2,1,0:T(8,128)S(1)}, u32[]{:S(2)}) copy-start(f32[2,2,16,768]{3,2,1,0:T(8,128)S(1)} %shard_map.73.refs_0_) | copy-start | bytes 589828
  79.8 3.5 %collective-permute-start.19 = (f32[16,192]{1,0:T(8,128)S(1)}, f32[16,192]{1,0:T(8,128)S(1)}, u32[]{:S(2)}, u32[]{:S(2)}) collective-permute-start(f32[16,192]{1,0:T(8,128)S(1)} %fusion.39), channel_id=1, source_target_pairs={{0,8},{8,0},{16,24},{24,16},{32,40},{40,32},{48,56},{56,48},{64,72... | collective-permute-start | bytes 36872 | tf_op jit(solution)/shard_map/ppermute | solution.py:269
  83.6 5.3 %collective-permute-start.21 = (f32[16,768]{1,0:T(8,128)S(1)}, f32[16,768]{1,0:T(8,128)S(1)}, u32[]{:S(2)}, u32[]{:S(2)}) collective-permute-start(f32[16,768]{1,0:T(8,128)S(1)} %bitcast_subtract_fusion), channel_id=1, source_target_pairs={{0,16},{8,24},{16,0},{24,8},{32,48},{40,56},{48,32},{56,40},{64,80... | collective-permute-start | bytes 147464 | tf_op jit(solution)/shard_map/ppermute | solution.py:274
  85.4 12.1 %collective-permute-start.18 = (f32[2,16,768]{2,1,0:T(8,128)S(1)}, f32[2,16,768]{2,1,0:T(8,128)S(1)}, u32[]{:S(2)}, u32[]{:S(2)}) collective-permute-start(f32[2,16,768]{2,1,0:T(8,128)S(1)} %slice_bitcast_fusion), channel_id=1, source_target_pairs={{0,8},{8,0},{16,24},{24,16},{32,40},{40,32},{48,56},{56,48},{64,72... | collective-permute-start | bytes 294920 | tf_op jit(solution)/shard_map/ppermute | solution.py:269
  88.9 8.7 %copy-start.2 = (f32[16,2048]{1,0:T(8,128)}, f32[16,2048]{1,0:T(8,128)S(1)}, u32[]{:S(2)}) copy-start(f32[16,2048]{1,0:T(8,128)S(1)} %shard_map.74.first_ref) | copy-start | bytes 393220
  88.9 5.5 %collective-permute-start.23 = (f32[16,768]{1,0:T(8,128)S(1)}, f32[16,768]{1,0:T(8,128)S(1)}, u32[]{:S(2)}, u32[]{:S(2)}) collective-permute-start(f32[16,768]{1,0:T(8,128)S(1)} %add.116), channel_id=1, source_target_pairs={{0,64},{8,72},{16,80},{24,88},{32,96},{40,104},{48,112},{56,120},{... | collective-permute-start | bytes 147464 | tf_op jit(solution)/shard_map/ppermute | solution.py:277
  91.5 4.2 %collective-permute-start.24 = (f32[16,768]{1,0:T(8,128)S(1)}, f32[16,768]{1,0:T(8,128)S(1)}, u32[]{:S(2)}, u32[]{:S(2)}) collective-permute-start(f32[16,768]{1,0:T(8,128)S(1)} %add.116), channel_id=1, source_target_pairs={{0,32},{8,40},{16,48},{24,56},{32,64},{40,72},{48,80},{56,88},{64,... | collective-permute-start | bytes 147464 | tf_op jit(solution)/shard_map/ppermute | solution.py:277
  91.5 4.2 %collective-permute-start.22 = (f32[16,768]{1,0:T(8,128)S(1)}, f32[16,768]{1,0:T(8,128)S(1)}, u32[]{:S(2)}, u32[]{:S(2)}) collective-permute-start(f32[16,768]{1,0:T(8,128)S(1)} %add.116), channel_id=1, source_target_pairs={{0,96},{8,104},{16,112},{24,120},{32,0},{40,8},{48,16},{56,24},{64... | collective-permute-start | bytes 147464 | tf_op jit(solution)/shard_map/ppermute | solution.py:277
  95.9 2.4 %collective-permute-start.25 = (f32[16,192]{1,0:T(8,128)S(1)}, f32[16,192]{1,0:T(8,128)S(1)}, u32[]{:S(2)}, u32[]{:S(2)}) collective-permute-start(f32[16,192]{1,0:T(8,128)S(1)} %fusion.33), channel_id=1, source_target_pairs={{0,8},{8,0},{16,24},{24,16},{32,40},{40,32},{48,56},{56,48},{64,72... | collective-permute-start | bytes 36872 | tf_op jit(solution)/shard_map/ppermute | solution.py:269
  98.6 3.5 %collective-permute-start.26 = (f32[16,768]{1,0:T(8,128)S(1)}, f32[16,768]{1,0:T(8,128)S(1)}, u32[]{:S(2)}, u32[]{:S(2)}) collective-permute-start(f32[16,768]{1,0:T(8,128)S(1)} %fusion.59), channel_id=1, source_target_pairs={{0,16},{8,24},{16,0},{24,8},{32,48},{40,56},{48,32},{56,40},{64,80... | collective-permute-start | bytes 147464 | tf_op jit(solution)/shard_map/ppermute | solution.py:274
  99.4 6.7 %copy-start.5 = (f32[6,192,768]{2,1,0:T(8,128)S(1)}, f32[6,192,768]{2,1,0:T(8,128)}, u32[]{:S(2)}) copy-start(f32[6,192,768]{2,1,0:T(8,128)} %shard_map.68) | copy-start | bytes 10616836
  102.1 11.7 %copy-start.3 = (f32[2,1,16,768]{3,2,1,0:T(8,128)}, f32[2,1,16,768]{3,2,1,0:T(8,128)S(1)}, u32[]{:S(2)}) copy-start(f32[2,1,16,768]{3,2,1,0:T(8,128)S(1)} %shard_map.75.refs_2_) | copy-start | bytes 294916
  102.1 4.5 %collective-permute-start.28 = (f32[16,768]{1,0:T(8,128)S(1)}, f32[16,768]{1,0:T(8,128)S(1)}, u32[]{:S(2)}, u32[]{:S(2)}) collective-permute-start(f32[16,768]{1,0:T(8,128)S(1)} %add.121), channel_id=1, source_target_pairs={{0,64},{8,72},{16,80},{24,88},{32,96},{40,104},{48,112},{56,120},{... | collective-permute-start | bytes 147464 | tf_op jit(solution)/shard_map/ppermute | solution.py:277
  103.4 4.2 %collective-permute-start.29 = (f32[16,768]{1,0:T(8,128)S(1)}, f32[16,768]{1,0:T(8,128)S(1)}, u32[]{:S(2)}, u32[]{:S(2)}) collective-permute-start(f32[16,768]{1,0:T(8,128)S(1)} %add.121), channel_id=1, source_target_pairs={{0,32},{8,40},{16,48},{24,56},{32,64},{40,72},{48,80},{56,88},{64,... | collective-permute-start | bytes 147464 | tf_op jit(solution)/shard_map/ppermute | solution.py:277
  105.7 3.8 %collective-permute-start.27 = (f32[16,768]{1,0:T(8,128)S(1)}, f32[16,768]{1,0:T(8,128)S(1)}, u32[]{:S(2)}, u32[]{:S(2)}) collective-permute-start(f32[16,768]{1,0:T(8,128)S(1)} %add.121), channel_id=1, source_target_pairs={{0,96},{8,104},{16,112},{24,120},{32,0},{40,8},{48,16},{56,24},{64... | collective-permute-start | bytes 147464 | tf_op jit(solution)/shard_map/ppermute | solution.py:277
  109.8 2.8 %collective-permute-start.30 = (f32[16,192]{1,0:T(8,128)S(1)}, f32[16,192]{1,0:T(8,128)S(1)}, u32[]{:S(2)}, u32[]{:S(2)}) collective-permute-start(f32[16,192]{1,0:T(8,128)S(1)} %fusion.25), channel_id=1, source_target_pairs={{0,8},{8,0},{16,24},{24,16},{32,40},{40,32},{48,56},{56,48},{64,72... | collective-permute-start | bytes 36872 | tf_op jit(solution)/shard_map/ppermute | solution.py:269
  112.9 3.0 %collective-permute-start.31 = (f32[16,768]{1,0:T(8,128)S(1)}, f32[16,768]{1,0:T(8,128)S(1)}, u32[]{:S(2)}, u32[]{:S(2)}) collective-permute-start(f32[16,768]{1,0:T(8,128)S(1)} %fusion.63), channel_id=1, source_target_pairs={{0,16},{8,24},{16,0},{24,8},{32,48},{40,56},{48,32},{56,40},{64,80... | collective-permute-start | bytes 147464 | tf_op jit(solution)/shard_map/ppermute | solution.py:274
  115.9 4.6 %collective-permute-start.33 = (f32[16,768]{1,0:T(8,128)S(1)}, f32[16,768]{1,0:T(8,128)S(1)}, u32[]{:S(2)}, u32[]{:S(2)}) collective-permute-start(f32[16,768]{1,0:T(8,128)S(1)} %add.126), channel_id=1, source_target_pairs={{0,64},{8,72},{16,80},{24,88},{32,96},{40,104},{48,112},{56,120},{... | collective-permute-start | bytes 147464 | tf_op jit(solution)/shard_map/ppermute | solution.py:277
  116.4 4.6 %collective-permute-start.34 = (f32[16,768]{1,0:T(8,128)S(1)}, f32[16,768]{1,0:T(8,128)S(1)}, u32[]{:S(2)}, u32[]{:S(2)}) collective-permute-start(f32[16,768]{1,0:T(8,128)S(1)} %add.126), channel_id=1, source_target_pairs={{0,32},{8,40},{16,48},{24,56},{32,64},{40,72},{48,80},{56,88},{64,... | collective-permute-start | bytes 147464 | tf_op jit(solution)/shard_map/ppermute | solution.py:277
  118.1 3.1 %collective-permute-start.32 = (f32[16,768]{1,0:T(8,128)S(1)}, f32[16,768]{1,0:T(8,128)S(1)}, u32[]{:S(2)}, u32[]{:S(2)}) collective-permute-start(f32[16,768]{1,0:T(8,128)S(1)} %add.126), channel_id=1, source_target_pairs={{0,96},{8,104},{16,112},{24,120},{32,0},{40,8},{48,16},{56,24},{64... | collective-permute-start | bytes 147464 | tf_op jit(solution)/shard_map/ppermute | solution.py:277
  121.4 4.0 %collective-permute-start.35 = (f32[16,192]{1,0:T(8,128)S(1)}, f32[16,192]{1,0:T(8,128)S(1)}, u32[]{:S(2)}, u32[]{:S(2)}) collective-permute-start(f32[16,192]{1,0:T(8,128)S(1)} %fusion.21), channel_id=1, source_target_pairs={{0,8},{8,0},{16,24},{24,16},{32,40},{40,32},{48,56},{56,48},{64,72... | collective-permute-start | bytes 36872 | tf_op jit(solution)/shard_map/ppermute | solution.py:269

commit v6 on v5

--- a/solution.py
+++ b/solution.py
@@ -361,19 +361,23 @@
     per = wide_size // narrow_size
     received = received.reshape(narrow_size, per, subs, 128)
     flat, first = first_products(received, reflectors)
-    z_mine = jnp.where(is_owner, flat[:, last + half :], swapped(flat[:, last : last + half]))
+    z_low = swapped(flat[:, last : last + half])
     first, later, v_low = lax.optimization_barrier((first, reflectors, v_low))
     first, second = summed_over_wide(first, second_products(flat, later))
-    v_mine = jnp.where(is_owner, later[:, last + half :], v_low)
+    v_mine = jnp.where(is_owner, later[0, last + half :], v_low[0])
     first, v_mine = lax.optimization_barrier((first, v_mine))
     coeffs1 = dot(first, triangles[1].T)
     second = second - dot(coeffs1, gram)
     second, weights, traded = lax.optimization_barrier((second, weights, traded))
     second, d_pair = summed_over_wide(second, half_pair(weights[0], traded[0], half))
-    z_mine = z_mine - dot_nt(coeffs1, v_mine[1])
+    z_mine = jnp.where(
+        is_owner,
+        flat[:, last + half :] - dot_nt(coeffs1, reflectors[1, last + half :]),
+        z_low - dot_nt(coeffs1, v_low[1]),
+    )
     second, z_mine = lax.optimization_barrier((second, z_mine))
     coeffs0 = dot(second, triangles[0].T)
-    corner = z_mine - dot_nt(coeffs0, v_mine[0])
+    corner = z_mine - dot_nt(coeffs0, v_mine)
 
     is_last = lax.axis_index("wide") >= wide_size - 2
     start = length - panels * panel_rows

time: 127 us -> 129 us (1.016)
  waiting for transfers between devices: 14 us -> 22 us
  starting transfers between devices: 59.3 us -> 52.9 us
  matrix products: 18.1 us -> 19.7 us
    ppermute x15, starting transfers between devices: 21.1 us -> 13.1 us  [from_chips(): lax.ppermute(array, 'wide', [(i, (i + by) % size) for i in range(size)])]
    ppermute x15, waiting for transfers between devices: 8.48 us -> 16.3 us  [from_chips(): lax.ppermute(array, 'wide', [(i, (i + by) % size) for i in range(size)])]
    ppermute x12, starting transfers between devices: 17.8 us -> 19.5 us  [swapped(): return lax.ppermute(array, 'wide', [(i, i ^ 1) for i in range(size)])]
    dot_general x6 -> x7, matrix products: 2.17 us -> 3.75 us  [dot_nt(): return lax.dot_general(a, b, NT, precision=HIGH)]
  transfers between devices with their start and end apart: 38 -> 38, of which waited for: 19 -> 22; matrix products, arithmetic and copies ran while one was open for 17% -> 17% of each run, Pallas kernels for 22% -> 22%
where the time goes in v6:
time: 129 us
  starting transfers between devices  52.9 us (41%)
  Pallas kernels  27.8 us (22%)
  waiting for transfers between devices  22 us (17%)
  matrix products  19.7 us (15%)
  local copies, waits for them, and re-layouts  3.36 us (3%)
  other arithmetic  1.72 us (1%)
    ppermute x12, starting transfers between devices, swapped(): return lax.ppermute(array, 'wide', [(i, i ^ 1) for i in range(size)])  19.5 us
    ppermute x15, waiting for transfers between devices, from_chips(): lax.ppermute(array, 'wide', [(i, (i + by) % size) for i in range(size)])  16.3 us
    dot_general x2, matrix products, gram_of(): lax.dot_general(reflectors[1, lo:hi], reflectors[0, lo:hi], (((0,), (0,))...  13.8 us
    ppermute x15, starting transfers between devices, from_chips(): lax.ppermute(array, 'wide', [(i, (i + by) % size) for i in range(size)])  13.1 us
    pallas_call x4, Pallas kernels, updated(): pl.pallas_call(functools.partial(update_kernel, z_first, first, which), o...  11.7 us
    pallas_call x2, Pallas kernels, products_call(): pl.pallas_call(kernel, out_shape=outs, in_specs=in_vmem(1) + [pl.BlockSpe...  8.19 us
    all_to_all x1, starting transfers between devices, body(): received = lax.all_to_all(received, 'wide', 0, 0, tiled=True)  6.54 us
    all_to_all x1, starting transfers between devices, body(): received = lax.all_to_all(received, 'narrow', 0, 0, tiled=True)  6.36 us
  transfers between devices with their start and end apart: 38, of which 22 were waited for; matrix products, arithmetic and copies ran while one was open for 17% of the time, Pallas kernels for 22%

profile of v6, /device:TPU:1, one launch (start us, length us, event | category | flops | bytes accessed | tf_op | source)
XLA Modules:
  0.0 128.6 jit_solution(2546206158443338303)
XLA Ops:
  0.6 1.5 %collective-permute-start = (f32[6,96,1536]{2,1,0:T(8,128)}, f32[6,96,1536]{2,1,0:T(8,128)}, u32[]{:S(2)}, u32[]{:S(2)}) collective-permute-start(f32[6,96,1536]{2,1,0:T(8,128)} %own_ref.1), channel_id=1, source_target_pairs={{0,8},{8,0},{16,24},{24,16},{32,40},{40,32},{48,56},{56,48},{64,72... | collective-permute-start | bytes 10616840 | tf_op jit(solution)/shard_map/ppermute | solution.py:269
  2.1 6.5 %all-to-all-start = ((f32[16,64,128]{2,1,0:T(8,128)}), f32[16,64,128]{2,1,0:T(8,128)}, u32[]{:S(2)}, u32[]{:S(2)}) async-start(f32[16,64,128]{2,1,0:T(8,128)} %bitcast.122), calls=%async_computation | async-start | bytes 1048576 | tf_op jit(solution)/shard_map/all_to_all | solution.py:350
  8.7 6.9 %fusion.3 = f32[256,256]{1,0:T(8,128)S(1)} fusion(f32[2,8192,256]{2,1,0:T(8,128)} %v_ref.10), kind=kOutput, calls=%fused_computation.3 | convolution fusion | flops 1610612736 | bytes 8650752 | tf_op jit(solution)/shard_map/dot_general | solution.py:329
  15.6 2.7 %slice.107 = f32[2,768,256]{2,1,0:T(8,128)} slice(f32[2,8192,256]{2,1,0:T(8,128)} %v_ref.10), slice={[0:2], [6656:7424], [0:256]} | slice | bytes 3145728 | tf_op jit(solution)/shard_map/slice | solution.py:353
  18.6 1.2 collective-permute-start.1
  19.7 6.4 %all-to-all-start.1 = ((f32[16,64,128]{2,1,0:T(8,128)}), f32[16,64,128]{2,1,0:T(8,128)S(1)}, u32[]{:S(2)}, u32[]{:S(2)}) async-start(f32[16,64,128]{2,1,0:T(8,128)} %all-to-all-done), calls=%async_computation.1 | async-start | bytes 1048576 | tf_op jit(solution)/shard_map/all_to_all | solution.py:357
  26.1 6.9 %fusion.10 = f32[256,256]{1,0:T(8,128)S(1)} fusion(f32[256,256]{1,0:T(8,128)S(1)} %fusion.3, f32[2,8192,256]{2,1,0:T(8,128)} %v_ref.10), kind=kOutput, calls=%fused_computation.10 | convolution fusion | flops 1610678272 | bytes 8912896 | tf_op jit(solution)/shard_map/dot_general | solution.py:329
  33.0 3.3 %shard_map.68 = f32[6,192,768]{2,1,0:T(8,128)} custom-call(s32[1]{0:T(128)} %bitcast.5.core_ref, f32[6,96,1536]{2,1,0:T(8,128)} %own_ref.1, f32[6,96,1536]{2,1,0:T(8,128)} %collective-permute-done.other_ref), custom_call_target="tpu_custom_call" | custom-call | bytes 884736 | tf_op jit(solution)/shard_map/pallas_call | solution.py:86
  36.7 4.1 %shard_map.69 = (f32[16,8192]{1,0:T(8,128)S(1)}, f32[16,256]{1,0:T(8,128)S(1)}) custom-call(f32[8,2,64,128]{3,2,1,0:T(8,128)S(1)} %bitcast.121, f32[2,8192,256]{2,1,0:T(8,128)} %v_ref.10), custom_call_target="tpu_custom_call" | custom-call | flops 201326592 | bytes 131072 | tf_op jit(solution)/shard_map/pallas_call | solution.py:163
  40.7 1.4 %collective-permute-start.2 = (f32[16,256]{1,0:T(8,128)S(1)}, f32[16,256]{1,0:T(8,128)S(1)}, u32[]{:S(2)}, u32[]{:S(2)}) collective-permute-start(f32[16,256]{1,0:T(8,128)S(1)} %get-tuple-element.61), channel_id=1, source_target_pairs={{0,8},{8,0},{16,24},{24,16},{32,40},{40,32},{48,56},{56,48},{64,72... | collective-permute-start | bytes 49160 | tf_op jit(solution)/shard_map/ppermute | solution.py:269
  42.1 0.8 collective-permute-done.2
  43.0 4.1 %shard_map.70 = f32[16,256]{1,0:T(8,128)S(1)} custom-call(f32[16,8192]{1,0:T(8,128)S(1)} %get-tuple-element.62.z_ref, f32[2,8192,256]{2,1,0:T(8,128)} %v_ref.10), custom_call_target="tpu_custom_call" | custom-call | flops 201326592 | bytes 131072 | tf_op jit(solution)/shard_map/pallas_call | solution.py:163
  47.1 2.2 %collective-permute-start.4 = (f32[16,256]{1,0:T(8,128)S(1)}, f32[16,256]{1,0:T(8,128)S(1)}, u32[]{:S(2)}, u32[]{:S(2)}) collective-permute-start(f32[16,256]{1,0:T(8,128)S(1)} %add.102), channel_id=1, source_target_pairs={{0,96},{8,104},{16,112},{24,120},{32,0},{40,8},{48,16},{56,24},{64... | collective-permute-start | bytes 49160 | tf_op jit(solution)/shard_map/ppermute | solution.py:277
  49.4 0.6 collective-permute-start.5
  49.9 0.6 collective-permute-start.6
  50.5 1.2 select_bitcast_fusion
  51.8 1.7 %collective-permute-done.5 = f32[16,256]{1,0:T(8,128)S(1)} collective-permute-done((f32[16,256]{1,0:T(8,128)S(1)}, f32[16,256]{1,0:T(8,128)S(1)}, u32[]{:S(2)}, u32[]{:S(2)}) %collective-permute-start.5) | collective-permute-done | bytes 16416 | tf_op jit(solution)/shard_map/ppermute | solution.py:277
  54.2 2.4 %collective-permute-start.8 = (f32[16,256]{1,0:T(8,128)S(1)}, f32[16,256]{1,0:T(8,128)S(1)}, u32[]{:S(2)}, u32[]{:S(2)}) collective-permute-start(f32[16,256]{1,0:T(8,128)S(1)} %sub.30), channel_id=1, source_target_pairs={{0,8},{8,0},{16,24},{24,16},{32,40},{40,32},{48,56},{56,48},{64,72... | collective-permute-start | bytes 49160 | tf_op jit(solution)/shard_map/ppermute | solution.py:269
  56.8 0.7 collective-permute-done.8
  57.5 0.9 collective-permute-start.9
  58.4 1.6 %convolution_subtract_fusion.1 = f32[16,768]{1,0:T(8,128)S(1)} fusion(f32[16,256]{1,0:T(8,128)S(1)} %fusion.52.refs_0_, f32[2,8192,256]{2,1,0:T(8,128)} %v_ref.10, f32[16,8192]{1,0:T(8,128)S(1)} %get-tuple-element.62.z_ref), kind=kOutput, calls=%fused_computation.13 | convolution fusion | flops 18886656 | bytes 901120 | tf_op jit(solution)/shard_map/dot_general | solution.py:20
  60.0 2.8 %shard_map.71 = f32[4,192,768]{2,1,0:T(8,128)} custom-call(s32[1]{0:T(128)} %bitcast.5.core_ref, f32[4,96,1536]{2,1,0:T(8,128)} %bitcast.9.own_ref, f32[4,96,1536]{2,1,0:T(8,128)} %collective-permute-done.7.other_ref), custom_call_target="tpu_custom_call" | custom-call | bytes 589824 | tf_op jit(solution)/shard_map/pallas_call | solution.py:86
  62.8 0.5 collective-permute-start.10
  63.3 0.8 collective-permute-start.11
  64.1 0.8 collective-permute-start.12
  65.4 2.0 %collective-permute-done.11 = f32[16,256]{1,0:T(8,128)S(1)} collective-permute-done((f32[16,256]{1,0:T(8,128)S(1)}, f32[16,256]{1,0:T(8,128)S(1)}, u32[]{:S(2)}, u32[]{:S(2)}) %collective-permute-start.11) | collective-permute-done | bytes 16416 | tf_op jit(solution)/shard_map/ppermute | solution.py:277
  67.4 0.5 collective-permute-done.12
  68.1 0.5 fusion.78
  68.7 0.7 collective-permute-start.14
  69.3 0.7 collective-permute-start.15
  70.0 0.7 collective-permute-start.16
  70.7 2.5 %shard_map.72.refs_1_ = f32[2,1,16,768]{3,2,1,0:T(8,128)S(1)} custom-call(f32[16,8192]{1,0:T(8,128)S(1)} %get-tuple-element.62.z_ref, f32[2,8192,256]{2,1,0:T(8,128)} %v_ref.10, f32[16,256]{1,0:T(8,128)S(1)} %fusion.52.refs_0_, f32[16,256]{1,0:T(8,128)S(1)} %fusion.50.refs_1_), custom_call_target="tpu_custom_call" | custom-call | flops 75497472 | bytes 3276800 | tf_op jit(solution)/shard_map/pallas_call | solution.py:230
  73.3 1.3 %collective-permute-start.17 = (f32[16,768]{1,0:T(8,128)S(1)}, f32[16,768]{1,0:T(8,128)S(1)}, u32[]{:S(2)}, u32[]{:S(2)}) collective-permute-start(f32[16,768]{1,0:T(8,128)S(1)} %add_add_fusion), channel_id=1, source_target_pairs={{16,0},{24,8},{48,32},{56,40},{80,64},{88,72},{112,96},{120,104},{... | collective-permute-start | bytes 147464 | tf_op jit(solution)/shard_map/ppermute | solution.py:297
  74.6 2.3 %collective-permute-start.20 = (f32[1,16,768]{2,1,0:T(8,128)S(1)}, f32[1,16,768]{2,1,0:T(8,128)S(1)}, u32[]{:S(2)}, u32[]{:S(2)}) collective-permute-start(f32[1,16,768]{2,1,0:T(8,128)S(1)} %slice_bitcast_fusion.1), channel_id=1, source_target_pairs={{0,8},{8,0},{16,24},{24,16},{32,40},{40,32},{48,56},{56,48},{64,72... | collective-permute-start | bytes 147464 | tf_op jit(solution)/shard_map/ppermute | solution.py:269
  76.9 3.6 %shard_map.73.refs_0_ = f32[2,2,16,768]{3,2,1,0:T(8,128)S(1)} custom-call(f32[16,8192]{1,0:T(8,128)S(1)} %get-tuple-element.62.z_ref, f32[2,8192,256]{2,1,0:T(8,128)} %v_ref.10, f32[16,256]{1,0:T(8,128)S(1)} %fusion.52.refs_0_, f32[16,256]{1,0:T(8,128)S(1)} %fusion.50.refs_1_), custom_call_target="tpu_custom_call" | custom-call | flops 150994944 | bytes 6520832 | tf_op jit(solution)/shard_map/pallas_call | solution.py:230
  80.8 2.5 %collective-permute-start.19 = (f32[16,192]{1,0:T(8,128)S(1)}, f32[16,192]{1,0:T(8,128)S(1)}, u32[]{:S(2)}, u32[]{:S(2)}) collective-permute-start(f32[16,192]{1,0:T(8,128)S(1)} %fusion.38), channel_id=1, source_target_pairs={{0,8},{8,0},{16,24},{24,16},{32,40},{40,32},{48,56},{56,48},{64,72... | collective-permute-start | bytes 36872 | tf_op jit(solution)/shard_map/ppermute | solution.py:269
  83.4 0.8 collective-permute-done.19
  84.5 1.8 %collective-permute-start.21 = (f32[16,768]{1,0:T(8,128)S(1)}, f32[16,768]{1,0:T(8,128)S(1)}, u32[]{:S(2)}, u32[]{:S(2)}) collective-permute-start(f32[16,768]{1,0:T(8,128)S(1)} %bitcast_subtract_fusion), channel_id=1, source_target_pairs={{0,16},{8,24},{16,0},{24,8},{32,48},{40,56},{48,32},{56,40},{64,80... | collective-permute-start | bytes 147464 | tf_op jit(solution)/shard_map/ppermute | solution.py:274
  86.4 0.5 collective-permute-start.18
  86.9 2.9 %shard_map.74.first_ref = f32[16,2048]{1,0:T(8,128)S(1)} custom-call(f32[16,8192]{1,0:T(8,128)S(1)} %get-tuple-element.62.z_ref, f32[2,8192,256]{2,1,0:T(8,128)} %v_ref.10, f32[16,256]{1,0:T(8,128)S(1)} %fusion.52.refs_0_, f32[16,256]{1,0:T(8,128)S(1)} %fusion.50.refs_1_), custom_call_target="tpu_custom_call" | custom-call | flops 100663296 | bytes 4358144 | tf_op jit(solution)/shard_map/pallas_call | solution.py:230
  89.8 1.6 %collective-permute-start.22 = (f32[16,768]{1,0:T(8,128)S(1)}, f32[16,768]{1,0:T(8,128)S(1)}, u32[]{:S(2)}, u32[]{:S(2)}) collective-permute-start(f32[16,768]{1,0:T(8,128)S(1)} %add.116), channel_id=1, source_target_pairs={{0,96},{8,104},{16,112},{24,120},{32,0},{40,8},{48,16},{56,24},{64... | collective-permute-start | bytes 147464 | tf_op jit(solution)/shard_map/ppermute | solution.py:277
  91.4 2.1 %collective-permute-start.23 = (f32[16,768]{1,0:T(8,128)S(1)}, f32[16,768]{1,0:T(8,128)S(1)}, u32[]{:S(2)}, u32[]{:S(2)}) collective-permute-start(f32[16,768]{1,0:T(8,128)S(1)} %add.116), channel_id=1, source_target_pairs={{0,64},{8,72},{16,80},{24,88},{32,96},{40,104},{48,112},{56,120},{... | collective-permute-start | bytes 147464 | tf_op jit(solution)/shard_map/ppermute | solution.py:277
  93.8 2.1 %collective-permute-done.23 = f32[16,768]{1,0:T(8,128)S(1)} collective-permute-done((f32[16,768]{1,0:T(8,128)S(1)}, f32[16,768]{1,0:T(8,128)S(1)}, u32[]{:S(2)}, u32[]{:S(2)}) %collective-permute-start.23) | collective-permute-done | bytes 49184 | tf_op jit(solution)/shard_map/ppermute | solution.py:277
  95.9 1.8 %collective-permute-done.24 = f32[16,768]{1,0:T(8,128)S(1)} collective-permute-done((f32[16,768]{1,0:T(8,128)S(1)}, f32[16,768]{1,0:T(8,128)S(1)}, u32[]{:S(2)}, u32[]{:S(2)}) %collective-permute-start.24) | collective-permute-done | bytes 49184 | tf_op jit(solution)/shard_map/ppermute | solution.py:277
  98.0 1.9 %collective-permute-start.25 = (f32[16,192]{1,0:T(8,128)S(1)}, f32[16,192]{1,0:T(8,128)S(1)}, u32[]{:S(2)}, u32[]{:S(2)}) collective-permute-start(f32[16,192]{1,0:T(8,128)S(1)} %fusion.32), channel_id=1, source_target_pairs={{0,8},{8,0},{16,24},{24,16},{32,40},{40,32},{48,56},{56,48},{64,72... | collective-permute-start | bytes 36872 | tf_op jit(solution)/shard_map/ppermute | solution.py:269
  99.9 0.8 collective-permute-done.25
  101.0 0.8 collective-permute-start.26
  101.8 2.7 %shard_map.75.refs_2_ = f32[2,1,16,768]{3,2,1,0:T(8,128)S(1)} custom-call(f32[16,8192]{1,0:T(8,128)S(1)} %get-tuple-element.62.z_ref, f32[2,8192,256]{2,1,0:T(8,128)} %v_ref.10, f32[16,256]{1,0:T(8,128)S(1)} %fusion.52.refs_0_, f32[16,256]{1,0:T(8,128)S(1)} %fusion.50.refs_1_), custom_call_target="tpu_custom_call" | custom-call | flops 75497472 | bytes 3276800 | tf_op jit(solution)/shard_map/pallas_call | solution.py:230
  104.6 0.8 collective-permute-start.28
  105.4 0.6 collective-permute-start.29
  106.3 1.2 collective-permute-done.27
  107.5 1.6 %collective-permute-done.28 = f32[16,768]{1,0:T(8,128)S(1)} collective-permute-done((f32[16,768]{1,0:T(8,128)S(1)}, f32[16,768]{1,0:T(8,128)S(1)}, u32[]{:S(2)}, u32[]{:S(2)}) %collective-permute-start.28) | collective-permute-done | bytes 49184 | tf_op jit(solution)/shard_map/ppermute | solution.py:277
  109.1 0.8 collective-permute-done.29
  110.2 2.7 %collective-permute-start.30 = (f32[16,192]{1,0:T(8,128)S(1)}, f32[16,192]{1,0:T(8,128)S(1)}, u32[]{:S(2)}, u32[]{:S(2)}) collective-permute-start(f32[16,192]{1,0:T(8,128)S(1)} %fusion.24), channel_id=1, source_target_pairs={{0,8},{8,0},{16,24},{24,16},{32,40},{40,32},{48,56},{56,48},{64,72... | collective-permute-start | bytes 36872 | tf_op jit(solution)/shard_map/ppermute | solution.py:269
  113.1 0.6 collective-permute-done.30
  114.0 0.6 collective-permute-start.31
  114.7 1.9 %shard_map.76 = f32[16,8192]{1,0:T(8,128)} custom-call(f32[16,2048]{1,0:T(8,128)} %copy-done.2, f32[2,2,16,768]{3,2,1,0:T(8,128)} %copy-done, f32[2,1,16,768]{3,2,1,0:T(8,128)} %copy-done.1, f32[2,1,16,768]{3,2,1,0:T(8,128)} %copy-done.3), custom_call_target="tpu_custom_call" | custom-call | bytes 1048576 | tf_op jit(solution)/shard_map/pallas_call | solution.py:256
  117.0 1.6 %collective-permute-start.32 = (f32[16,768]{1,0:T(8,128)S(1)}, f32[16,768]{1,0:T(8,128)S(1)}, u32[]{:S(2)}, u32[]{:S(2)}) collective-permute-start(f32[16,768]{1,0:T(8,128)S(1)} %add.126), channel_id=1, source_target_pairs={{0,96},{8,104},{16,112},{24,120},{32,0},{40,8},{48,16},{56,24},{64... | collective-permute-start | bytes 147464 | tf_op jit(solution)/shard_map/ppermute | solution.py:277
  118.6 0.6 collective-permute-start.33
  119.4 0.6 collective-permute-done.32
  120.0 3.1 %collective-permute-done.33 = f32[16,768]{1,0:T(8,128)S(1)} collective-permute-done((f32[16,768]{1,0:T(8,128)S(1)}, f32[16,768]{1,0:T(8,128)S(1)}, u32[]{:S(2)}, u32[]{:S(2)}) %collective-permute-start.33) | collective-permute-done | bytes 49184 | tf_op jit(solution)/shard_map/ppermute | solution.py:277
  123.9 3.1 %collective-permute-start.35 = (f32[16,192]{1,0:T(8,128)S(1)}, f32[16,192]{1,0:T(8,128)S(1)}, u32[]{:S(2)}, u32[]{:S(2)}) collective-permute-start(f32[16,192]{1,0:T(8,128)S(1)} %fusion.20), channel_id=1, source_target_pairs={{0,8},{8,0},{16,24},{24,16},{32,40},{40,32},{48,56},{56,48},{64,72... | collective-permute-start | bytes 36872 | tf_op jit(solution)/shard_map/ppermute | solution.py:269
  127.1 0.8 collective-permute-done.35
  127.9 0.6 copy.7
  (87 shorter events, 6.7 us)
Async XLA Ops:
  0.6 32.4 %collective-permute-start = (f32[6,96,1536]{2,1,0:T(8,128)}, f32[6,96,1536]{2,1,0:T(8,128)}, u32[]{:S(2)}, u32[]{:S(2)}) collective-permute-start(f32[6,96,1536]{2,1,0:T(8,128)} %own_ref.1), channel_id=1, source_target_pairs={{0,8},{8,0},{16,24},{24,16},{32,40},{40,32},{48,56},{56,48},{64,72... | collective-permute-start | bytes 10616840 | tf_op jit(solution)/shard_map/ppermute | solution.py:269
  2.1 16.4 %all-to-all-start = ((f32[16,64,128]{2,1,0:T(8,128)}), f32[16,64,128]{2,1,0:T(8,128)}, u32[]{:S(2)}, u32[]{:S(2)}) async-start(f32[16,64,128]{2,1,0:T(8,128)} %bitcast.122), calls=%async_computation | async-start | bytes 1048576 | tf_op jit(solution)/shard_map/all_to_all | solution.py:350
  18.6 22.2 %collective-permute-start.1 = (f32[2,768,256]{2,1,0:T(8,128)}, f32[2,768,256]{2,1,0:T(8,128)S(1)}, u32[]{:S(2)}, u32[]{:S(2)}) collective-permute-start(f32[2,768,256]{2,1,0:T(8,128)} %slice.107), channel_id=1, source_target_pairs={{0,8},{8,0},{16,24},{24,16},{32,40},{40,32},{48,56},{56,48},{64,72... | collective-permute-start | bytes 4718600 | tf_op jit(solution)/shard_map/ppermute | solution.py:269
  19.7 34.5 %collective-permute-start.7 = (f32[4,96,1536]{2,1,0:T(8,128)}, f32[4,96,1536]{2,1,0:T(8,128)}, u32[]{:S(2)}, u32[]{:S(2)}) collective-permute-start(f32[4,96,1536]{2,1,0:T(8,128)} %bitcast.9.own_ref), channel_id=1, source_target_pairs={{0,8},{8,0},{16,24},{24,16},{32,40},{40,32},{48,56},{56,48},{64,72... | collective-permute-start | bytes 7077896 | tf_op jit(solution)/shard_map/ppermute | solution.py:269
  19.7 16.9 %all-to-all-start.1 = ((f32[16,64,128]{2,1,0:T(8,128)}), f32[16,64,128]{2,1,0:T(8,128)S(1)}, u32[]{:S(2)}, u32[]{:S(2)}) async-start(f32[16,64,128]{2,1,0:T(8,128)} %all-to-all-done), calls=%async_computation.1 | async-start | bytes 1048576 | tf_op jit(solution)/shard_map/all_to_all | solution.py:357
  40.7 2.2 %collective-permute-start.2 = (f32[16,256]{1,0:T(8,128)S(1)}, f32[16,256]{1,0:T(8,128)S(1)}, u32[]{:S(2)}, u32[]{:S(2)}) collective-permute-start(f32[16,256]{1,0:T(8,128)S(1)} %get-tuple-element.61), channel_id=1, source_target_pairs={{0,8},{8,0},{16,24},{24,16},{32,40},{40,32},{48,56},{56,48},{64,72... | collective-permute-start | bytes 49160 | tf_op jit(solution)/shard_map/ppermute | solution.py:269
  42.9 4.2 %collective-permute-start.3 = (f32[16,256]{1,0:T(8,128)S(1)}, f32[16,256]{1,0:T(8,128)S(1)}, u32[]{:S(2)}, u32[]{:S(2)}) collective-permute-start(f32[16,256]{1,0:T(8,128)S(1)} %add.101), channel_id=1, source_target_pairs={{0,16},{8,24},{16,0},{24,8},{32,48},{40,56},{48,32},{56,40},{64,80... | collective-permute-start | bytes 49160 | tf_op jit(solution)/shard_map/ppermute | solution.py:274
  43.0 10.8 %copy-start.7 = (f32[2,256,256]{2,1,0:T(8,128)S(1)}, f32[2,256,256]{2,1,0:T(8,128)}, u32[]{:S(2)}) copy-start(f32[2,256,256]{2,1,0:T(8,128)} %param.7) | copy-start | bytes 1572868
  47.1 4.6 %collective-permute-start.4 = (f32[16,256]{1,0:T(8,128)S(1)}, f32[16,256]{1,0:T(8,128)S(1)}, u32[]{:S(2)}, u32[]{:S(2)}) collective-permute-start(f32[16,256]{1,0:T(8,128)S(1)} %add.102), channel_id=1, source_target_pairs={{0,96},{8,104},{16,112},{24,120},{32,0},{40,8},{48,16},{56,24},{64... | collective-permute-start | bytes 49160 | tf_op jit(solution)/shard_map/ppermute | solution.py:277
  49.4 4.1 %collective-permute-start.5 = (f32[16,256]{1,0:T(8,128)S(1)}, f32[16,256]{1,0:T(8,128)S(1)}, u32[]{:S(2)}, u32[]{:S(2)}) collective-permute-start(f32[16,256]{1,0:T(8,128)S(1)} %add.102), channel_id=1, source_target_pairs={{0,64},{8,72},{16,80},{24,88},{32,96},{40,104},{48,112},{56,120},{... | collective-permute-start | bytes 49160 | tf_op jit(solution)/shard_map/ppermute | solution.py:277
  49.9 3.8 %collective-permute-start.6 = (f32[16,256]{1,0:T(8,128)S(1)}, f32[16,256]{1,0:T(8,128)S(1)}, u32[]{:S(2)}, u32[]{:S(2)}) collective-permute-start(f32[16,256]{1,0:T(8,128)S(1)} %add.102), channel_id=1, source_target_pairs={{0,32},{8,40},{16,48},{24,56},{32,64},{40,72},{48,80},{56,88},{64,... | collective-permute-start | bytes 49160 | tf_op jit(solution)/shard_map/ppermute | solution.py:277
  54.2 3.3 %collective-permute-start.8 = (f32[16,256]{1,0:T(8,128)S(1)}, f32[16,256]{1,0:T(8,128)S(1)}, u32[]{:S(2)}, u32[]{:S(2)}) collective-permute-start(f32[16,256]{1,0:T(8,128)S(1)} %sub.30), channel_id=1, source_target_pairs={{0,8},{8,0},{16,24},{24,16},{32,40},{40,32},{48,56},{56,48},{64,72... | collective-permute-start | bytes 49160 | tf_op jit(solution)/shard_map/ppermute | solution.py:269
  56.6 8.2 %collective-permute-start.13 = (f32[16,768]{1,0:T(8,128)S(1)}, f32[16,768]{1,0:T(8,128)S(1)}, u32[]{:S(2)}, u32[]{:S(2)}) collective-permute-start(f32[16,768]{1,0:T(8,128)S(1)} %slice.115), channel_id=1, source_target_pairs={{0,8},{8,0},{16,24},{24,16},{32,40},{40,32},{48,56},{56,48},{64,72... | collective-permute-start | bytes 147464 | tf_op jit(solution)/shard_map/ppermute | solution.py:269
  57.5 5.3 %collective-permute-start.9 = (f32[16,256]{1,0:T(8,128)S(1)}, f32[16,256]{1,0:T(8,128)S(1)}, u32[]{:S(2)}, u32[]{:S(2)}) collective-permute-start(f32[16,256]{1,0:T(8,128)S(1)} %add.106), channel_id=1, source_target_pairs={{0,16},{8,24},{16,0},{24,8},{32,48},{40,56},{48,32},{56,40},{64,80... | collective-permute-start | bytes 49160 | tf_op jit(solution)/shard_map/ppermute | solution.py:274
  60.0 8.0 %copy-start.8 = (f32[2,256,256]{2,1,0:T(8,128)S(1)}, f32[2,256,256]{2,1,0:T(8,128)}, u32[]{:S(2)}) copy-start(f32[2,256,256]{2,1,0:T(8,128)} %param.7) | copy-start | bytes 1572868
  62.8 2.7 %collective-permute-start.10 = (f32[16,256]{1,0:T(8,128)S(1)}, f32[16,256]{1,0:T(8,128)S(1)}, u32[]{:S(2)}, u32[]{:S(2)}) collective-permute-start(f32[16,256]{1,0:T(8,128)S(1)} %add.107), channel_id=1, source_target_pairs={{0,96},{8,104},{16,112},{24,120},{32,0},{40,8},{48,16},{56,24},{64... | collective-permute-start | bytes 49160 | tf_op jit(solution)/shard_map/ppermute | solution.py:277
  63.3 4.1 %collective-permute-start.11 = (f32[16,256]{1,0:T(8,128)S(1)}, f32[16,256]{1,0:T(8,128)S(1)}, u32[]{:S(2)}, u32[]{:S(2)}) collective-permute-start(f32[16,256]{1,0:T(8,128)S(1)} %add.107), channel_id=1, source_target_pairs={{0,64},{8,72},{16,80},{24,88},{32,96},{40,104},{48,112},{56,120},{... | collective-permute-start | bytes 49160 | tf_op jit(solution)/shard_map/ppermute | solution.py:277
  64.1 3.8 %collective-permute-start.12 = (f32[16,256]{1,0:T(8,128)S(1)}, f32[16,256]{1,0:T(8,128)S(1)}, u32[]{:S(2)}, u32[]{:S(2)}) collective-permute-start(f32[16,256]{1,0:T(8,128)S(1)} %add.107), channel_id=1, source_target_pairs={{0,32},{8,40},{16,48},{24,56},{32,64},{40,72},{48,80},{56,88},{64,... | collective-permute-start | bytes 49160 | tf_op jit(solution)/shard_map/ppermute | solution.py:277
  68.7 4.6 %collective-permute-start.14 = (f32[16,768]{1,0:T(8,128)S(1)}, f32[16,768]{1,0:T(8,128)S(1)}, u32[]{:S(2)}, u32[]{:S(2)}) collective-permute-start(f32[16,768]{1,0:T(8,128)S(1)} %broadcast_select_fusion), channel_id=1, source_target_pairs={{112,80},{120,88},{113,81},{121,89},{114,82},{122,90},{115,83},{12... | collective-permute-start | bytes 147464 | tf_op jit(solution)/shard_map/ppermute | solution.py:294
  69.3 3.9 %collective-permute-start.15 = (f32[16,768]{1,0:T(8,128)S(1)}, f32[16,768]{1,0:T(8,128)S(1)}, u32[]{:S(2)}, u32[]{:S(2)}) collective-permute-start(f32[16,768]{1,0:T(8,128)S(1)} %broadcast_select_fusion), channel_id=1, source_target_pairs={{112,16},{120,24},{113,17},{121,25},{114,18},{122,26},{115,19},{12... | collective-permute-start | bytes 147464 | tf_op jit(solution)/shard_map/ppermute | solution.py:294
  70.0 3.2 %collective-permute-start.16 = (f32[16,768]{1,0:T(8,128)S(1)}, f32[16,768]{1,0:T(8,128)S(1)}, u32[]{:S(2)}, u32[]{:S(2)}) collective-permute-start(f32[16,768]{1,0:T(8,128)S(1)} %broadcast_select_fusion), channel_id=1, source_target_pairs={{112,48},{120,56},{113,49},{121,57},{114,50},{122,58},{115,51},{12... | collective-permute-start | bytes 147464 | tf_op jit(solution)/shard_map/ppermute | solution.py:294
  73.2 11.0 %copy-start.1 = (f32[2,1,16,768]{3,2,1,0:T(8,128)}, f32[2,1,16,768]{3,2,1,0:T(8,128)S(1)}, u32[]{:S(2)}) copy-start(f32[2,1,16,768]{3,2,1,0:T(8,128)S(1)} %shard_map.72.refs_1_) | copy-start | bytes 294916
  73.3 7.2 %collective-permute-start.17 = (f32[16,768]{1,0:T(8,128)S(1)}, f32[16,768]{1,0:T(8,128)S(1)}, u32[]{:S(2)}, u32[]{:S(2)}) collective-permute-start(f32[16,768]{1,0:T(8,128)S(1)} %add_add_fusion), channel_id=1, source_target_pairs={{16,0},{24,8},{48,32},{56,40},{80,64},{88,72},{112,96},{120,104},{... | collective-permute-start | bytes 147464 | tf_op jit(solution)/shard_map/ppermute | solution.py:297
  74.6 5.9 %copy-start.6 = (f32[4,192,768]{2,1,0:T(8,128)S(1)}, f32[4,192,768]{2,1,0:T(8,128)}, u32[]{:S(2)}) copy-start(f32[4,192,768]{2,1,0:T(8,128)} %shard_map.71) | copy-start | bytes 7077892
  74.6 9.6 %copy-start.4 = (f32[6,192,768]{2,1,0:T(8,128)S(1)}, f32[6,192,768]{2,1,0:T(8,128)}, u32[]{:S(2)}) copy-start(f32[6,192,768]{2,1,0:T(8,128)} %shard_map.68) | copy-start | bytes 10616836
  74.6 9.6 %collective-permute-start.20 = (f32[1,16,768]{2,1,0:T(8,128)S(1)}, f32[1,16,768]{2,1,0:T(8,128)S(1)}, u32[]{:S(2)}, u32[]{:S(2)}) collective-permute-start(f32[1,16,768]{2,1,0:T(8,128)S(1)} %slice_bitcast_fusion.1), channel_id=1, source_target_pairs={{0,8},{8,0},{16,24},{24,16},{32,40},{40,32},{48,56},{56,48},{64,72... | collective-permute-start | bytes 147464 | tf_op jit(solution)/shard_map/ppermute | solution.py:269
  80.5 19.4 %copy-start = (f32[2,2,16,768]{3,2,1,0:T(8,128)}, f32[2,2,16,768]{3,2,1,0:T(8,128)S(1)}, u32[]{:S(2)}) copy-start(f32[2,2,16,768]{3,2,1,0:T(8,128)S(1)} %shard_map.73.refs_0_) | copy-start | bytes 589828
  80.8 3.4 %collective-permute-start.19 = (f32[16,192]{1,0:T(8,128)S(1)}, f32[16,192]{1,0:T(8,128)S(1)}, u32[]{:S(2)}, u32[]{:S(2)}) collective-permute-start(f32[16,192]{1,0:T(8,128)S(1)} %fusion.38), channel_id=1, source_target_pairs={{0,8},{8,0},{16,24},{24,16},{32,40},{40,32},{48,56},{56,48},{64,72... | collective-permute-start | bytes 36872 | tf_op jit(solution)/shard_map/ppermute | solution.py:269
  84.5 5.3 %collective-permute-start.21 = (f32[16,768]{1,0:T(8,128)S(1)}, f32[16,768]{1,0:T(8,128)S(1)}, u32[]{:S(2)}, u32[]{:S(2)}) collective-permute-start(f32[16,768]{1,0:T(8,128)S(1)} %bitcast_subtract_fusion), channel_id=1, source_target_pairs={{0,16},{8,24},{16,0},{24,8},{32,48},{40,56},{48,32},{56,40},{64,80... | collective-permute-start | bytes 147464 | tf_op jit(solution)/shard_map/ppermute | solution.py:274
  86.4 13.5 %collective-permute-start.18 = (f32[2,16,768]{2,1,0:T(8,128)S(1)}, f32[2,16,768]{2,1,0:T(8,128)S(1)}, u32[]{:S(2)}, u32[]{:S(2)}) collective-permute-start(f32[2,16,768]{2,1,0:T(8,128)S(1)} %slice_bitcast_fusion), channel_id=1, source_target_pairs={{0,8},{8,0},{16,24},{24,16},{32,40},{40,32},{48,56},{56,48},{64,72... | collective-permute-start | bytes 294920 | tf_op jit(solution)/shard_map/ppermute | solution.py:269
  89.8 10.1 %copy-start.2 = (f32[16,2048]{1,0:T(8,128)}, f32[16,2048]{1,0:T(8,128)S(1)}, u32[]{:S(2)}) copy-start(f32[16,2048]{1,0:T(8,128)S(1)} %shard_map.74.first_ref) | copy-start | bytes 393220
  89.8 4.0 %collective-permute-start.22 = (f32[16,768]{1,0:T(8,128)S(1)}, f32[16,768]{1,0:T(8,128)S(1)}, u32[]{:S(2)}, u32[]{:S(2)}) collective-permute-start(f32[16,768]{1,0:T(8,128)S(1)} %add.116), channel_id=1, source_target_pairs={{0,96},{8,104},{16,112},{24,120},{32,0},{40,8},{48,16},{56,24},{64... | collective-permute-start | bytes 147464 | tf_op jit(solution)/shard_map/ppermute | solution.py:277
  91.4 4.4 %collective-permute-start.23 = (f32[16,768]{1,0:T(8,128)S(1)}, f32[16,768]{1,0:T(8,128)S(1)}, u32[]{:S(2)}, u32[]{:S(2)}) collective-permute-start(f32[16,768]{1,0:T(8,128)S(1)} %add.116), channel_id=1, source_target_pairs={{0,64},{8,72},{16,80},{24,88},{32,96},{40,104},{48,112},{56,120},{... | collective-permute-start | bytes 147464 | tf_op jit(solution)/shard_map/ppermute | solution.py:277
  93.6 4.2 %collective-permute-start.24 = (f32[16,768]{1,0:T(8,128)S(1)}, f32[16,768]{1,0:T(8,128)S(1)}, u32[]{:S(2)}, u32[]{:S(2)}) collective-permute-start(f32[16,768]{1,0:T(8,128)S(1)} %add.116), channel_id=1, source_target_pairs={{0,32},{8,40},{16,48},{24,56},{32,64},{40,72},{48,80},{56,88},{64,... | collective-permute-start | bytes 147464 | tf_op jit(solution)/shard_map/ppermute | solution.py:277
  98.0 2.7 %collective-permute-start.25 = (f32[16,192]{1,0:T(8,128)S(1)}, f32[16,192]{1,0:T(8,128)S(1)}, u32[]{:S(2)}, u32[]{:S(2)}) collective-permute-start(f32[16,192]{1,0:T(8,128)S(1)} %fusion.32), channel_id=1, source_target_pairs={{0,8},{8,0},{16,24},{24,16},{32,40},{40,32},{48,56},{56,48},{64,72... | collective-permute-start | bytes 36872 | tf_op jit(solution)/shard_map/ppermute | solution.py:269
  101.0 3.5 %collective-permute-start.26 = (f32[16,768]{1,0:T(8,128)S(1)}, f32[16,768]{1,0:T(8,128)S(1)}, u32[]{:S(2)}, u32[]{:S(2)}) collective-permute-start(f32[16,768]{1,0:T(8,128)S(1)} %fusion.58), channel_id=1, source_target_pairs={{0,16},{8,24},{16,0},{24,8},{32,48},{40,56},{48,32},{56,40},{64,80... | collective-permute-start | bytes 147464 | tf_op jit(solution)/shard_map/ppermute | solution.py:274
  101.8 4.3 %copy-start.5 = (f32[6,192,768]{2,1,0:T(8,128)S(1)}, f32[6,192,768]{2,1,0:T(8,128)}, u32[]{:S(2)}) copy-start(f32[6,192,768]{2,1,0:T(8,128)} %shard_map.68) | copy-start | bytes 10616836
  104.4 10.2 %copy-start.3 = (f32[2,1,16,768]{3,2,1,0:T(8,128)}, f32[2,1,16,768]{3,2,1,0:T(8,128)S(1)}, u32[]{:S(2)}) copy-start(f32[2,1,16,768]{3,2,1,0:T(8,128)S(1)} %shard_map.75.refs_2_) | copy-start | bytes 294916
  104.5 3.0 %collective-permute-start.27 = (f32[16,768]{1,0:T(8,128)S(1)}, f32[16,768]{1,0:T(8,128)S(1)}, u32[]{:S(2)}, u32[]{:S(2)}) collective-permute-start(f32[16,768]{1,0:T(8,128)S(1)} %add.121), channel_id=1, source_target_pairs={{0,96},{8,104},{16,112},{24,120},{32,0},{40,8},{48,16},{56,24},{64... | collective-permute-start | bytes 147464 | tf_op jit(solution)/shard_map/ppermute | solution.py:277
  104.6 4.5 %collective-permute-start.28 = (f32[16,768]{1,0:T(8,128)S(1)}, f32[16,768]{1,0:T(8,128)S(1)}, u32[]{:S(2)}, u32[]{:S(2)}) collective-permute-start(f32[16,768]{1,0:T(8,128)S(1)} %add.121), channel_id=1, source_target_pairs={{0,64},{8,72},{16,80},{24,88},{32,96},{40,104},{48,112},{56,120},{... | collective-permute-start | bytes 147464 | tf_op jit(solution)/shard_map/ppermute | solution.py:277
  105.4 4.5 %collective-permute-start.29 = (f32[16,768]{1,0:T(8,128)S(1)}, f32[16,768]{1,0:T(8,128)S(1)}, u32[]{:S(2)}, u32[]{:S(2)}) collective-permute-start(f32[16,768]{1,0:T(8,128)S(1)} %add.121), channel_id=1, source_target_pairs={{0,32},{8,40},{16,48},{24,56},{32,64},{40,72},{48,80},{56,88},{64,... | collective-permute-start | bytes 147464 | tf_op jit(solution)/shard_map/ppermute | solution.py:277
  110.2 3.5 %collective-permute-start.30 = (f32[16,192]{1,0:T(8,128)S(1)}, f32[16,192]{1,0:T(8,128)S(1)}, u32[]{:S(2)}, u32[]{:S(2)}) collective-permute-start(f32[16,192]{1,0:T(8,128)S(1)} %fusion.24), channel_id=1, source_target_pairs={{0,8},{8,0},{16,24},{24,16},{32,40},{40,32},{48,56},{56,48},{64,72... | collective-permute-start | bytes 36872 | tf_op jit(solution)/shard_map/ppermute | solution.py:269
  114.0 3.0 %collective-permute-start.31 = (f32[16,768]{1,0:T(8,128)S(1)}, f32[16,768]{1,0:T(8,128)S(1)}, u32[]{:S(2)}, u32[]{:S(2)}) collective-permute-start(f32[16,768]{1,0:T(8,128)S(1)} %fusion.62), channel_id=1, source_target_pairs={{0,16},{8,24},{16,0},{24,8},{32,48},{40,56},{48,32},{56,40},{64,80... | collective-permute-start | bytes 147464 | tf_op jit(solution)/shard_map/ppermute | solution.py:274
  117.0 3.0 %collective-permute-start.32 = (f32[16,768]{1,0:T(8,128)S(1)}, f32[16,768]{1,0:T(8,128)S(1)}, u32[]{:S(2)}, u32[]{:S(2)}) collective-permute-start(f32[16,768]{1,0:T(8,128)S(1)} %add.126), channel_id=1, source_target_pairs={{0,96},{8,104},{16,112},{24,120},{32,0},{40,8},{48,16},{56,24},{64... | collective-permute-start | bytes 147464 | tf_op jit(solution)/shard_map/ppermute | solution.py:277
  118.6 4.5 %collective-permute-start.33 = (f32[16,768]{1,0:T(8,128)S(1)}, f32[16,768]{1,0:T(8,128)S(1)}, u32[]{:S(2)}, u32[]{:S(2)}) collective-permute-start(f32[16,768]{1,0:T(8,128)S(1)} %add.126), channel_id=1, source_target_pairs={{0,64},{8,72},{16,80},{24,88},{32,96},{40,104},{48,112},{56,120},{... | collective-permute-start | bytes 147464 | tf_op jit(solution)/shard_map/ppermute | solution.py:277
  119.3 4.3 %collective-permute-start.34 = (f32[16,768]{1,0:T(8,128)S(1)}, f32[16,768]{1,0:T(8,128)S(1)}, u32[]{:S(2)}, u32[]{:S(2)}) collective-permute-start(f32[16,768]{1,0:T(8,128)S(1)} %add.126), channel_id=1, source_target_pairs={{0,32},{8,40},{16,48},{24,56},{32,64},{40,72},{48,80},{56,88},{64,... | collective-permute-start | bytes 147464 | tf_op jit(solution)/shard_map/ppermute | solution.py:277
  123.9 3.9 %collective-permute-start.35 = (f32[16,192]{1,0:T(8,128)S(1)}, f32[16,192]{1,0:T(8,128)S(1)}, u32[]{:S(2)}, u32[]{:S(2)}) collective-permute-start(f32[16,192]{1,0:T(8,128)S(1)} %fusion.20), channel_id=1, source_target_pairs={{0,8},{8,0},{16,24},{24,16},{32,40},{40,32},{48,56},{56,48},{64,72... | collective-permute-start | bytes 36872 | tf_op jit(solution)/shard_map/ppermute | solution.py:269

commit v7 on v5

--- a/solution.py
+++ b/solution.py
@@ -165,7 +165,7 @@
         out_shape=outs,
         in_specs=in_vmem(1) + [pl.BlockSpec(memory_space=pl.ANY)],
         out_specs=in_vmem(len(outs)),
-        scratch_shapes=held_pieces(block, 1, 1024, 6),
+        scratch_shapes=held_pieces(block, 1, 512, 8),
         compiler_params=BIG,
         cost_estimate=pl.CostEstimate(
             flops=6 * z.size * block,

time: 127 us -> 126 us (level)
  no operation moved by 1% of the time
where the time goes in v7:
time: 126 us
  starting transfers between devices  59.3 us (47%)
  Pallas kernels  27.4 us (22%)
  matrix products  18.1 us (14%)
  waiting for transfers between devices  14 us (11%)
  local copies, waits for them, and re-layouts  3.37 us (3%)
  other arithmetic  2.57 us (2%)
    ppermute x15, starting transfers between devices, from_chips(): lax.ppermute(array, 'wide', [(i, (i + by) % size) for i in range(size)])  21.1 us
    ppermute x12, starting transfers between devices, swapped(): return lax.ppermute(array, 'wide', [(i, i ^ 1) for i in range(size)])  17.8 us
    dot_general x2, matrix products, gram_of(): lax.dot_general(reflectors[1, lo:hi], reflectors[0, lo:hi], (((0,), (0,))...  13.8 us
    pallas_call x4, Pallas kernels, updated(): pl.pallas_call(functools.partial(update_kernel, z_first, first, which), o...  11.7 us
    ppermute x15, waiting for transfers between devices, from_chips(): lax.ppermute(array, 'wide', [(i, (i + by) % size) for i in range(size)])  8.48 us
    pallas_call x2, Pallas kernels, products_call(): pl.pallas_call(kernel, out_shape=outs, in_specs=in_vmem(1) + [pl.BlockSpe...  7.87 us
    all_to_all x1, starting transfers between devices, body(): received = lax.all_to_all(received, 'wide', 0, 0, tiled=True)  6.54 us
    all_to_all x1, starting transfers between devices, body(): received = lax.all_to_all(received, 'narrow', 0, 0, tiled=True)  6.36 us
  transfers between devices with their start and end apart: 38, of which 19 were waited for; matrix products, arithmetic and copies ran while one was open for 17% of the time, Pallas kernels for 22%

profile of v7, /device:TPU:1, one launch (start us, length us, event | category | flops | bytes accessed | tf_op | source)
XLA Modules:
  0.0 125.9 jit_solution(8937475528038123813)
XLA Ops:
  0.6 1.5 %collective-permute-start = (f32[6,96,1536]{2,1,0:T(8,128)}, f32[6,96,1536]{2,1,0:T(8,128)}, u32[]{:S(2)}, u32[]{:S(2)}) collective-permute-start(f32[6,96,1536]{2,1,0:T(8,128)} %own_ref.1), channel_id=1, source_target_pairs={{0,8},{8,0},{16,24},{24,16},{32,40},{40,32},{48,56},{56,48},{64,72... | collective-permute-start | bytes 10616840 | tf_op jit(solution)/shard_map/ppermute | solution.py:269
  2.1 6.5 %all-to-all-start = ((f32[16,64,128]{2,1,0:T(8,128)}), f32[16,64,128]{2,1,0:T(8,128)}, u32[]{:S(2)}, u32[]{:S(2)}) async-start(f32[16,64,128]{2,1,0:T(8,128)} %bitcast.120), calls=%async_computation | async-start | bytes 1048576 | tf_op jit(solution)/shard_map/all_to_all | solution.py:350
  8.7 6.9 %fusion.3 = f32[256,256]{1,0:T(8,128)S(1)} fusion(f32[2,8192,256]{2,1,0:T(8,128)} %v_ref.10), kind=kOutput, calls=%fused_computation.3 | convolution fusion | flops 1610612736 | bytes 8650752 | tf_op jit(solution)/shard_map/dot_general | solution.py:329
  15.6 2.7 %slice.104 = f32[2,768,256]{2,1,0:T(8,128)} slice(f32[2,8192,256]{2,1,0:T(8,128)} %v_ref.10), slice={[0:2], [6656:7424], [0:256]} | slice | bytes 3145728 | tf_op jit(solution)/shard_map/slice | solution.py:353
  18.2 0.3 all-to-all-done
  18.6 1.2 collective-permute-start.1
  19.7 6.4 %all-to-all-start.1 = ((f32[16,64,128]{2,1,0:T(8,128)}), f32[16,64,128]{2,1,0:T(8,128)S(1)}, u32[]{:S(2)}, u32[]{:S(2)}) async-start(f32[16,64,128]{2,1,0:T(8,128)} %all-to-all-done), calls=%async_computation.1 | async-start | bytes 1048576 | tf_op jit(solution)/shard_map/all_to_all | solution.py:357
  26.1 6.9 %fusion.10 = f32[256,256]{1,0:T(8,128)S(1)} fusion(f32[256,256]{1,0:T(8,128)S(1)} %fusion.3, f32[2,8192,256]{2,1,0:T(8,128)} %v_ref.10), kind=kOutput, calls=%fused_computation.11 | convolution fusion | flops 1610678272 | bytes 8912896 | tf_op jit(solution)/shard_map/dot_general | solution.py:329
  33.0 3.3 %shard_map.68 = f32[6,192,768]{2,1,0:T(8,128)} custom-call(s32[1]{0:T(128)} %bitcast.5.core_ref, f32[6,96,1536]{2,1,0:T(8,128)} %own_ref.1, f32[6,96,1536]{2,1,0:T(8,128)} %collective-permute-done.other_ref), custom_call_target="tpu_custom_call" | custom-call | bytes 884736 | tf_op jit(solution)/shard_map/pallas_call | solution.py:86
  36.3 0.4 all-to-all-done.1
  36.7 3.9 %shard_map.69 = (f32[16,8192]{1,0:T(8,128)S(1)}, f32[16,256]{1,0:T(8,128)S(1)}) custom-call(f32[8,2,64,128]{3,2,1,0:T(8,128)S(1)} %bitcast.119, f32[2,8192,256]{2,1,0:T(8,128)} %v_ref.10), custom_call_target="tpu_custom_call" | custom-call | flops 201326592 | bytes 131072 | tf_op jit(solution)/shard_map/pallas_call | solution.py:163
  40.6 1.4 %collective-permute-start.2 = (f32[16,256]{1,0:T(8,128)S(1)}, f32[16,256]{1,0:T(8,128)S(1)}, u32[]{:S(2)}, u32[]{:S(2)}) collective-permute-start(f32[16,256]{1,0:T(8,128)S(1)} %get-tuple-element.61), channel_id=1, source_target_pairs={{0,8},{8,0},{16,24},{24,16},{32,40},{40,32},{48,56},{56,48},{64,72... | collective-permute-start | bytes 49160 | tf_op jit(solution)/shard_map/ppermute | solution.py:269
  42.1 0.7 collective-permute-done.2
  42.9 3.9 %shard_map.70 = f32[16,256]{1,0:T(8,128)S(1)} custom-call(f32[16,8192]{1,0:T(8,128)S(1)} %get-tuple-element.62.z_ref, f32[2,8192,256]{2,1,0:T(8,128)} %v_ref.10), custom_call_target="tpu_custom_call" | custom-call | flops 201326592 | bytes 131072 | tf_op jit(solution)/shard_map/pallas_call | solution.py:163
  46.8 2.5 %collective-permute-start.5 = (f32[16,256]{1,0:T(8,128)S(1)}, f32[16,256]{1,0:T(8,128)S(1)}, u32[]{:S(2)}, u32[]{:S(2)}) collective-permute-start(f32[16,256]{1,0:T(8,128)S(1)} %add.102), channel_id=1, source_target_pairs={{0,64},{8,72},{16,80},{24,88},{32,96},{40,104},{48,112},{56,120},{... | collective-permute-start | bytes 49160 | tf_op jit(solution)/shard_map/ppermute | solution.py:277
  49.7 2.4 %collective-permute-start.4 = (f32[16,256]{1,0:T(8,128)S(1)}, f32[16,256]{1,0:T(8,128)S(1)}, u32[]{:S(2)}, u32[]{:S(2)}) collective-permute-start(f32[16,256]{1,0:T(8,128)S(1)} %add.102), channel_id=1, source_target_pairs={{0,96},{8,104},{16,112},{24,120},{32,0},{40,8},{48,16},{56,24},{64... | collective-permute-start | bytes 49160 | tf_op jit(solution)/shard_map/ppermute | solution.py:277
  52.1 2.1 %slice_select_fusion = f32[2,768,256]{2,1,0:T(8,128)S(1)} fusion(f32[2,768,256]{2,1,0:T(8,128)} %copy-done.7, f32[2,8192,256]{2,1,0:T(8,128)} %v_ref.10, pred[]{:T(512)S(6)} %eq.12), kind=kLoop, calls=%fused_computation.10 | loop fusion | flops 393216 | bytes 4718593 | tf_op jit(solution)/shard_map/jit(_where)/select_n | solution.py:367
  54.7 1.5 %collective-permute-start.8 = (f32[16,256]{1,0:T(8,128)S(1)}, f32[16,256]{1,0:T(8,128)S(1)}, u32[]{:S(2)}, u32[]{:S(2)}) collective-permute-start(f32[16,256]{1,0:T(8,128)S(1)} %sub.27), channel_id=1, source_target_pairs={{0,8},{8,0},{16,24},{24,16},{32,40},{40,32},{48,56},{56,48},{64,72... | collective-permute-start | bytes 49160 | tf_op jit(solution)/shard_map/ppermute | solution.py:269
  56.2 0.8 collective-permute-done.8
  57.1 0.9 collective-permute-start.9
  57.9 2.7 %shard_map.71 = f32[4,192,768]{2,1,0:T(8,128)} custom-call(s32[1]{0:T(128)} %bitcast.5.core_ref, f32[4,96,1536]{2,1,0:T(8,128)} %bitcast.8.own_ref, f32[4,96,1536]{2,1,0:T(8,128)} %collective-permute-done.7.other_ref), custom_call_target="tpu_custom_call" | custom-call | bytes 589824 | tf_op jit(solution)/shard_map/pallas_call | solution.py:86
  60.7 0.8 collective-permute-start.11
  61.5 2.3 %collective-permute-start.12 = (f32[16,256]{1,0:T(8,128)S(1)}, f32[16,256]{1,0:T(8,128)S(1)}, u32[]{:S(2)}, u32[]{:S(2)}) collective-permute-start(f32[16,256]{1,0:T(8,128)S(1)} %add.107), channel_id=1, source_target_pairs={{0,32},{8,40},{16,48},{24,56},{32,64},{40,72},{48,80},{56,88},{64,... | collective-permute-start | bytes 49160 | tf_op jit(solution)/shard_map/ppermute | solution.py:277
  63.9 0.3 collective-permute-start.10
  64.2 0.5 select_subtract_fusion
  64.9 0.5 collective-permute-done.12
  65.3 1.4 %collective-permute-done.10 = f32[16,256]{1,0:T(8,128)S(1)} collective-permute-done((f32[16,256]{1,0:T(8,128)S(1)}, f32[16,256]{1,0:T(8,128)S(1)}, u32[]{:S(2)}, u32[]{:S(2)}) %collective-permute-start.10) | collective-permute-done | bytes 16416 | tf_op jit(solution)/shard_map/ppermute | solution.py:277
  67.0 0.5 fusion.15
  67.5 0.7 collective-permute-start.16
  68.2 0.7 collective-permute-start.15
  68.9 0.7 collective-permute-start.14
  69.5 2.5 %shard_map.72.refs_1_ = f32[2,1,16,768]{3,2,1,0:T(8,128)S(1)} custom-call(f32[16,8192]{1,0:T(8,128)S(1)} %get-tuple-element.62.z_ref, f32[2,8192,256]{2,1,0:T(8,128)} %v_ref.10, f32[16,256]{1,0:T(8,128)S(1)} %fusion.53.refs_0_, f32[16,256]{1,0:T(8,128)S(1)} %fusion.51.refs_1_), custom_call_target="tpu_custom_call" | custom-call | flops 75497472 | bytes 3276800 | tf_op jit(solution)/shard_map/pallas_call | solution.py:230
  72.1 1.3 %collective-permute-start.17 = (f32[16,768]{1,0:T(8,128)S(1)}, f32[16,768]{1,0:T(8,128)S(1)}, u32[]{:S(2)}, u32[]{:S(2)}) collective-permute-start(f32[16,768]{1,0:T(8,128)S(1)} %add_add_fusion), channel_id=1, source_target_pairs={{16,0},{24,8},{48,32},{56,40},{80,64},{88,72},{112,96},{120,104},{... | collective-permute-start | bytes 147464 | tf_op jit(solution)/shard_map/ppermute | solution.py:297
  73.5 2.1 %collective-permute-start.20 = (f32[1,16,768]{2,1,0:T(8,128)S(1)}, f32[1,16,768]{2,1,0:T(8,128)S(1)}, u32[]{:S(2)}, u32[]{:S(2)}) collective-permute-start(f32[1,16,768]{2,1,0:T(8,128)S(1)} %slice_bitcast_fusion.1), channel_id=1, source_target_pairs={{0,8},{8,0},{16,24},{24,16},{32,40},{40,32},{48,56},{56,48},{64,72... | collective-permute-start | bytes 147464 | tf_op jit(solution)/shard_map/ppermute | solution.py:269
  75.6 3.6 %shard_map.73.refs_0_ = f32[2,2,16,768]{3,2,1,0:T(8,128)S(1)} custom-call(f32[16,8192]{1,0:T(8,128)S(1)} %get-tuple-element.62.z_ref, f32[2,8192,256]{2,1,0:T(8,128)} %v_ref.10, f32[16,256]{1,0:T(8,128)S(1)} %fusion.53.refs_0_, f32[16,256]{1,0:T(8,128)S(1)} %fusion.51.refs_1_), custom_call_target="tpu_custom_call" | custom-call | flops 150994944 | bytes 6520832 | tf_op jit(solution)/shard_map/pallas_call | solution.py:230
  79.5 2.7 %collective-permute-start.19 = (f32[16,192]{1,0:T(8,128)S(1)}, f32[16,192]{1,0:T(8,128)S(1)}, u32[]{:S(2)}, u32[]{:S(2)}) collective-permute-start(f32[16,192]{1,0:T(8,128)S(1)} %fusion.39), channel_id=1, source_target_pairs={{0,8},{8,0},{16,24},{24,16},{32,40},{40,32},{48,56},{56,48},{64,72... | collective-permute-start | bytes 36872 | tf_op jit(solution)/shard_map/ppermute | solution.py:269
  82.2 0.8 collective-permute-done.19
  83.3 1.8 %collective-permute-start.21 = (f32[16,768]{1,0:T(8,128)S(1)}, f32[16,768]{1,0:T(8,128)S(1)}, u32[]{:S(2)}, u32[]{:S(2)}) collective-permute-start(f32[16,768]{1,0:T(8,128)S(1)} %bitcast_subtract_fusion), channel_id=1, source_target_pairs={{0,16},{8,24},{16,0},{24,8},{32,48},{40,56},{48,32},{56,40},{64,80... | collective-permute-start | bytes 147464 | tf_op jit(solution)/shard_map/ppermute | solution.py:274
  85.2 0.5 collective-permute-start.18
  85.7 2.9 %shard_map.74.first_ref = f32[16,2048]{1,0:T(8,128)S(1)} custom-call(f32[16,8192]{1,0:T(8,128)S(1)} %get-tuple-element.62.z_ref, f32[2,8192,256]{2,1,0:T(8,128)} %v_ref.10, f32[16,256]{1,0:T(8,128)S(1)} %fusion.53.refs_0_, f32[16,256]{1,0:T(8,128)S(1)} %fusion.51.refs_1_), custom_call_target="tpu_custom_call" | custom-call | flops 100663296 | bytes 4358144 | tf_op jit(solution)/shard_map/pallas_call | solution.py:230
  88.6 2.6 %collective-permute-start.23 = (f32[16,768]{1,0:T(8,128)S(1)}, f32[16,768]{1,0:T(8,128)S(1)}, u32[]{:S(2)}, u32[]{:S(2)}) collective-permute-start(f32[16,768]{1,0:T(8,128)S(1)} %add.116), channel_id=1, source_target_pairs={{0,64},{8,72},{16,80},{24,88},{32,96},{40,104},{48,112},{56,120},{... | collective-permute-start | bytes 147464 | tf_op jit(solution)/shard_map/ppermute | solution.py:277
  91.2 2.7 %collective-permute-start.22 = (f32[16,768]{1,0:T(8,128)S(1)}, f32[16,768]{1,0:T(8,128)S(1)}, u32[]{:S(2)}, u32[]{:S(2)}) collective-permute-start(f32[16,768]{1,0:T(8,128)S(1)} %add.116), channel_id=1, source_target_pairs={{0,96},{8,104},{16,112},{24,120},{32,0},{40,8},{48,16},{56,24},{64... | collective-permute-start | bytes 147464 | tf_op jit(solution)/shard_map/ppermute | solution.py:277
  94.2 1.2 collective-permute-done.24
  95.7 1.6 %collective-permute-start.25 = (f32[16,192]{1,0:T(8,128)S(1)}, f32[16,192]{1,0:T(8,128)S(1)}, u32[]{:S(2)}, u32[]{:S(2)}) collective-permute-start(f32[16,192]{1,0:T(8,128)S(1)} %fusion.33), channel_id=1, source_target_pairs={{0,8},{8,0},{16,24},{24,16},{32,40},{40,32},{48,56},{56,48},{64,72... | collective-permute-start | bytes 36872 | tf_op jit(solution)/shard_map/ppermute | solution.py:269
  97.3 0.8 collective-permute-done.25
  98.4 0.8 collective-permute-start.26
  99.1 2.7 %shard_map.75.refs_2_ = f32[2,1,16,768]{3,2,1,0:T(8,128)S(1)} custom-call(f32[16,8192]{1,0:T(8,128)S(1)} %get-tuple-element.62.z_ref, f32[2,8192,256]{2,1,0:T(8,128)} %v_ref.10, f32[16,256]{1,0:T(8,128)S(1)} %fusion.53.refs_0_, f32[16,256]{1,0:T(8,128)S(1)} %fusion.51.refs_1_), custom_call_target="tpu_custom_call" | custom-call | flops 75497472 | bytes 3276800 | tf_op jit(solution)/shard_map/pallas_call | solution.py:230
  101.8 1.3 %collective-permute-start.28 = (f32[16,768]{1,0:T(8,128)S(1)}, f32[16,768]{1,0:T(8,128)S(1)}, u32[]{:S(2)}, u32[]{:S(2)}) collective-permute-start(f32[16,768]{1,0:T(8,128)S(1)} %add.121), channel_id=1, source_target_pairs={{0,64},{8,72},{16,80},{24,88},{32,96},{40,104},{48,112},{56,120},{... | collective-permute-start | bytes 147464 | tf_op jit(solution)/shard_map/ppermute | solution.py:277
  103.1 2.3 %collective-permute-start.29 = (f32[16,768]{1,0:T(8,128)S(1)}, f32[16,768]{1,0:T(8,128)S(1)}, u32[]{:S(2)}, u32[]{:S(2)}) collective-permute-start(f32[16,768]{1,0:T(8,128)S(1)} %add.121), channel_id=1, source_target_pairs={{0,32},{8,40},{16,48},{24,56},{32,64},{40,72},{48,80},{56,88},{64,... | collective-permute-start | bytes 147464 | tf_op jit(solution)/shard_map/ppermute | solution.py:277
  105.5 0.3 collective-permute-start.27
  106.4 0.9 collective-permute-done.29
  107.3 2.0 %collective-permute-done.27 = f32[16,768]{1,0:T(8,128)S(1)} collective-permute-done((f32[16,768]{1,0:T(8,128)S(1)}, f32[16,768]{1,0:T(8,128)S(1)}, u32[]{:S(2)}, u32[]{:S(2)}) %collective-permute-start.27) | collective-permute-done | bytes 49184 | tf_op jit(solution)/shard_map/ppermute | solution.py:277
  109.5 2.0 %collective-permute-start.30 = (f32[16,192]{1,0:T(8,128)S(1)}, f32[16,192]{1,0:T(8,128)S(1)}, u32[]{:S(2)}, u32[]{:S(2)}) collective-permute-start(f32[16,192]{1,0:T(8,128)S(1)} %fusion.25), channel_id=1, source_target_pairs={{0,8},{8,0},{16,24},{24,16},{32,40},{40,32},{48,56},{56,48},{64,72... | collective-permute-start | bytes 36872 | tf_op jit(solution)/shard_map/ppermute | solution.py:269
  111.8 0.6 collective-permute-done.30
  112.6 0.8 collective-permute-start.31
  113.5 1.9 %shard_map.76 = f32[16,8192]{1,0:T(8,128)} custom-call(f32[16,2048]{1,0:T(8,128)} %copy-done.2, f32[2,2,16,768]{3,2,1,0:T(8,128)} %copy-done, f32[2,1,16,768]{3,2,1,0:T(8,128)} %copy-done.1, f32[2,1,16,768]{3,2,1,0:T(8,128)} %copy-done.3), custom_call_target="tpu_custom_call" | custom-call | bytes 1048576 | tf_op jit(solution)/shard_map/pallas_call | solution.py:256
  115.6 0.5 collective-permute-start.33
  116.1 1.7 %collective-permute-start.34 = (f32[16,768]{1,0:T(8,128)S(1)}, f32[16,768]{1,0:T(8,128)S(1)}, u32[]{:S(2)}, u32[]{:S(2)}) collective-permute-start(f32[16,768]{1,0:T(8,128)S(1)} %add.126), channel_id=1, source_target_pairs={{0,32},{8,40},{16,48},{24,56},{32,64},{40,72},{48,80},{56,88},{64,... | collective-permute-start | bytes 147464 | tf_op jit(solution)/shard_map/ppermute | solution.py:277
  117.8 1.0 collective-permute-start.32
  118.9 1.3 %collective-permute-done.33 = f32[16,768]{1,0:T(8,128)S(1)} collective-permute-done((f32[16,768]{1,0:T(8,128)S(1)}, f32[16,768]{1,0:T(8,128)S(1)}, u32[]{:S(2)}, u32[]{:S(2)}) %collective-permute-start.33) | collective-permute-done | bytes 49184 | tf_op jit(solution)/shard_map/ppermute | solution.py:277
  120.2 0.5 collective-permute-done.34
  121.2 3.2 %collective-permute-start.35 = (f32[16,192]{1,0:T(8,128)S(1)}, f32[16,192]{1,0:T(8,128)S(1)}, u32[]{:S(2)}, u32[]{:S(2)}) collective-permute-start(f32[16,192]{1,0:T(8,128)S(1)} %fusion.21), channel_id=1, source_target_pairs={{0,8},{8,0},{16,24},{24,16},{32,40},{40,32},{48,56},{56,48},{64,72... | collective-permute-start | bytes 36872 | tf_op jit(solution)/shard_map/ppermute | solution.py:269
  124.4 0.8 collective-permute-done.35
  125.3 0.6 copy.7
  (86 shorter events, 5.3 us)
Async XLA Ops:
  0.6 32.4 %collective-permute-start = (f32[6,96,1536]{2,1,0:T(8,128)}, f32[6,96,1536]{2,1,0:T(8,128)}, u32[]{:S(2)}, u32[]{:S(2)}) collective-permute-start(f32[6,96,1536]{2,1,0:T(8,128)} %own_ref.1), channel_id=1, source_target_pairs={{0,8},{8,0},{16,24},{24,16},{32,40},{40,32},{48,56},{56,48},{64,72... | collective-permute-start | bytes 10616840 | tf_op jit(solution)/shard_map/ppermute | solution.py:269
  2.1 16.4 %all-to-all-start = ((f32[16,64,128]{2,1,0:T(8,128)}), f32[16,64,128]{2,1,0:T(8,128)}, u32[]{:S(2)}, u32[]{:S(2)}) async-start(f32[16,64,128]{2,1,0:T(8,128)} %bitcast.120), calls=%async_computation | async-start | bytes 1048576 | tf_op jit(solution)/shard_map/all_to_all | solution.py:350
  18.6 22.0 %collective-permute-start.1 = (f32[2,768,256]{2,1,0:T(8,128)}, f32[2,768,256]{2,1,0:T(8,128)S(1)}, u32[]{:S(2)}, u32[]{:S(2)}) collective-permute-start(f32[2,768,256]{2,1,0:T(8,128)} %slice.104), channel_id=1, source_target_pairs={{0,8},{8,0},{16,24},{24,16},{32,40},{40,32},{48,56},{56,48},{64,72... | collective-permute-start | bytes 4718600 | tf_op jit(solution)/shard_map/ppermute | solution.py:269
  19.7 34.9 %collective-permute-start.7 = (f32[4,96,1536]{2,1,0:T(8,128)}, f32[4,96,1536]{2,1,0:T(8,128)}, u32[]{:S(2)}, u32[]{:S(2)}) collective-permute-start(f32[4,96,1536]{2,1,0:T(8,128)} %bitcast.8.own_ref), channel_id=1, source_target_pairs={{0,8},{8,0},{16,24},{24,16},{32,40},{40,32},{48,56},{56,48},{64,72... | collective-permute-start | bytes 7077896 | tf_op jit(solution)/shard_map/ppermute | solution.py:269
  19.7 16.9 %all-to-all-start.1 = ((f32[16,64,128]{2,1,0:T(8,128)}), f32[16,64,128]{2,1,0:T(8,128)S(1)}, u32[]{:S(2)}, u32[]{:S(2)}) async-start(f32[16,64,128]{2,1,0:T(8,128)} %all-to-all-done), calls=%async_computation.1 | async-start | bytes 1048576 | tf_op jit(solution)/shard_map/all_to_all | solution.py:357
  40.6 6.2 %copy-start.7 = (f32[2,768,256]{2,1,0:T(8,128)}, f32[2,768,256]{2,1,0:T(8,128)S(1)}, u32[]{:S(2)}) copy-start(f32[2,768,256]{2,1,0:T(8,128)S(1)} %collective-permute-done.1) | copy-start | bytes 4718596
  40.6 2.2 %collective-permute-start.2 = (f32[16,256]{1,0:T(8,128)S(1)}, f32[16,256]{1,0:T(8,128)S(1)}, u32[]{:S(2)}, u32[]{:S(2)}) collective-permute-start(f32[16,256]{1,0:T(8,128)S(1)} %get-tuple-element.61), channel_id=1, source_target_pairs={{0,8},{8,0},{16,24},{24,16},{32,40},{40,32},{48,56},{56,48},{64,72... | collective-permute-start | bytes 49160 | tf_op jit(solution)/shard_map/ppermute | solution.py:269
  42.0 22.2 %collective-permute-start.13 = (f32[16,768]{1,0:T(8,128)S(1)}, f32[16,768]{1,0:T(8,128)S(1)}, u32[]{:S(2)}, u32[]{:S(2)}) collective-permute-start(f32[16,768]{1,0:T(8,128)S(1)} %slice.110), channel_id=1, source_target_pairs={{0,8},{8,0},{16,24},{24,16},{32,40},{40,32},{48,56},{56,48},{64,72... | collective-permute-start | bytes 147464 | tf_op jit(solution)/shard_map/ppermute | solution.py:269
  42.8 4.0 %collective-permute-start.3 = (f32[16,256]{1,0:T(8,128)S(1)}, f32[16,256]{1,0:T(8,128)S(1)}, u32[]{:S(2)}, u32[]{:S(2)}) collective-permute-start(f32[16,256]{1,0:T(8,128)S(1)} %add.101), channel_id=1, source_target_pairs={{0,16},{8,24},{16,0},{24,8},{32,48},{40,56},{48,32},{56,40},{64,80... | collective-permute-start | bytes 49160 | tf_op jit(solution)/shard_map/ppermute | solution.py:274
  46.8 7.4 %copy-start.8 = (f32[2,256,256]{2,1,0:T(8,128)S(1)}, f32[2,256,256]{2,1,0:T(8,128)}, u32[]{:S(2)}) copy-start(f32[2,256,256]{2,1,0:T(8,128)} %param.7) | copy-start | bytes 1572868
  46.8 7.3 %collective-permute-start.5 = (f32[16,256]{1,0:T(8,128)S(1)}, f32[16,256]{1,0:T(8,128)S(1)}, u32[]{:S(2)}, u32[]{:S(2)}) collective-permute-start(f32[16,256]{1,0:T(8,128)S(1)} %add.102), channel_id=1, source_target_pairs={{0,64},{8,72},{16,80},{24,88},{32,96},{40,104},{48,112},{56,120},{... | collective-permute-start | bytes 49160 | tf_op jit(solution)/shard_map/ppermute | solution.py:277
  49.4 4.8 %collective-permute-start.6 = (f32[16,256]{1,0:T(8,128)S(1)}, f32[16,256]{1,0:T(8,128)S(1)}, u32[]{:S(2)}, u32[]{:S(2)}) collective-permute-start(f32[16,256]{1,0:T(8,128)S(1)} %add.102), channel_id=1, source_target_pairs={{0,32},{8,40},{16,48},{24,56},{32,64},{40,72},{48,80},{56,88},{64,... | collective-permute-start | bytes 49160 | tf_op jit(solution)/shard_map/ppermute | solution.py:277
  49.7 4.5 %collective-permute-start.4 = (f32[16,256]{1,0:T(8,128)S(1)}, f32[16,256]{1,0:T(8,128)S(1)}, u32[]{:S(2)}, u32[]{:S(2)}) collective-permute-start(f32[16,256]{1,0:T(8,128)S(1)} %add.102), channel_id=1, source_target_pairs={{0,96},{8,104},{16,112},{24,120},{32,0},{40,8},{48,16},{56,24},{64... | collective-permute-start | bytes 49160 | tf_op jit(solution)/shard_map/ppermute | solution.py:277
  54.7 2.4 %collective-permute-start.8 = (f32[16,256]{1,0:T(8,128)S(1)}, f32[16,256]{1,0:T(8,128)S(1)}, u32[]{:S(2)}, u32[]{:S(2)}) collective-permute-start(f32[16,256]{1,0:T(8,128)S(1)} %sub.27), channel_id=1, source_target_pairs={{0,8},{8,0},{16,24},{24,16},{32,40},{40,32},{48,56},{56,48},{64,72... | collective-permute-start | bytes 49160 | tf_op jit(solution)/shard_map/ppermute | solution.py:269
  57.1 3.6 %collective-permute-start.9 = (f32[16,256]{1,0:T(8,128)S(1)}, f32[16,256]{1,0:T(8,128)S(1)}, u32[]{:S(2)}, u32[]{:S(2)}) collective-permute-start(f32[16,256]{1,0:T(8,128)S(1)} %add.106), channel_id=1, source_target_pairs={{0,16},{8,24},{16,0},{24,8},{32,48},{40,56},{48,32},{56,40},{64,80... | collective-permute-start | bytes 49160 | tf_op jit(solution)/shard_map/ppermute | solution.py:274
  60.7 4.2 %collective-permute-start.11 = (f32[16,256]{1,0:T(8,128)S(1)}, f32[16,256]{1,0:T(8,128)S(1)}, u32[]{:S(2)}, u32[]{:S(2)}) collective-permute-start(f32[16,256]{1,0:T(8,128)S(1)} %add.107), channel_id=1, source_target_pairs={{0,64},{8,72},{16,80},{24,88},{32,96},{40,104},{48,112},{56,120},{... | collective-permute-start | bytes 49160 | tf_op jit(solution)/shard_map/ppermute | solution.py:277
  61.5 3.8 %collective-permute-start.12 = (f32[16,256]{1,0:T(8,128)S(1)}, f32[16,256]{1,0:T(8,128)S(1)}, u32[]{:S(2)}, u32[]{:S(2)}) collective-permute-start(f32[16,256]{1,0:T(8,128)S(1)} %add.107), channel_id=1, source_target_pairs={{0,32},{8,40},{16,48},{24,56},{32,64},{40,72},{48,80},{56,88},{64,... | collective-permute-start | bytes 49160 | tf_op jit(solution)/shard_map/ppermute | solution.py:277
  63.9 2.9 %collective-permute-start.10 = (f32[16,256]{1,0:T(8,128)S(1)}, f32[16,256]{1,0:T(8,128)S(1)}, u32[]{:S(2)}, u32[]{:S(2)}) collective-permute-start(f32[16,256]{1,0:T(8,128)S(1)} %add.107), channel_id=1, source_target_pairs={{0,96},{8,104},{16,112},{24,120},{32,0},{40,8},{48,16},{56,24},{64... | collective-permute-start | bytes 49160 | tf_op jit(solution)/shard_map/ppermute | solution.py:277
  67.5 4.6 %collective-permute-start.16 = (f32[16,768]{1,0:T(8,128)S(1)}, f32[16,768]{1,0:T(8,128)S(1)}, u32[]{:S(2)}, u32[]{:S(2)}) collective-permute-start(f32[16,768]{1,0:T(8,128)S(1)} %broadcast_select_fusion), channel_id=1, source_target_pairs={{112,48},{120,56},{113,49},{121,57},{114,50},{122,58},{115,51},{12... | collective-permute-start | bytes 147464 | tf_op jit(solution)/shard_map/ppermute | solution.py:294
  68.2 3.9 %collective-permute-start.15 = (f32[16,768]{1,0:T(8,128)S(1)}, f32[16,768]{1,0:T(8,128)S(1)}, u32[]{:S(2)}, u32[]{:S(2)}) collective-permute-start(f32[16,768]{1,0:T(8,128)S(1)} %broadcast_select_fusion), channel_id=1, source_target_pairs={{112,16},{120,24},{113,17},{121,25},{114,18},{122,26},{115,19},{12... | collective-permute-start | bytes 147464 | tf_op jit(solution)/shard_map/ppermute | solution.py:294
  68.9 3.2 %collective-permute-start.14 = (f32[16,768]{1,0:T(8,128)S(1)}, f32[16,768]{1,0:T(8,128)S(1)}, u32[]{:S(2)}, u32[]{:S(2)}) collective-permute-start(f32[16,768]{1,0:T(8,128)S(1)} %broadcast_select_fusion), channel_id=1, source_target_pairs={{112,80},{120,88},{113,81},{121,89},{114,82},{122,90},{115,83},{12... | collective-permute-start | bytes 147464 | tf_op jit(solution)/shard_map/ppermute | solution.py:294
  72.1 11.0 %copy-start.1 = (f32[2,1,16,768]{3,2,1,0:T(8,128)}, f32[2,1,16,768]{3,2,1,0:T(8,128)S(1)}, u32[]{:S(2)}) copy-start(f32[2,1,16,768]{3,2,1,0:T(8,128)S(1)} %shard_map.72.refs_1_) | copy-start | bytes 294916
  72.1 7.1 %collective-permute-start.17 = (f32[16,768]{1,0:T(8,128)S(1)}, f32[16,768]{1,0:T(8,128)S(1)}, u32[]{:S(2)}, u32[]{:S(2)}) collective-permute-start(f32[16,768]{1,0:T(8,128)S(1)} %add_add_fusion), channel_id=1, source_target_pairs={{16,0},{24,8},{48,32},{56,40},{80,64},{88,72},{112,96},{120,104},{... | collective-permute-start | bytes 147464 | tf_op jit(solution)/shard_map/ppermute | solution.py:297
  73.4 5.8 %copy-start.6 = (f32[4,192,768]{2,1,0:T(8,128)S(1)}, f32[4,192,768]{2,1,0:T(8,128)}, u32[]{:S(2)}) copy-start(f32[4,192,768]{2,1,0:T(8,128)} %shard_map.71) | copy-start | bytes 7077892
  73.4 9.6 %copy-start.4 = (f32[6,192,768]{2,1,0:T(8,128)S(1)}, f32[6,192,768]{2,1,0:T(8,128)}, u32[]{:S(2)}) copy-start(f32[6,192,768]{2,1,0:T(8,128)} %shard_map.68) | copy-start | bytes 10616836
  73.5 9.6 %collective-permute-start.20 = (f32[1,16,768]{2,1,0:T(8,128)S(1)}, f32[1,16,768]{2,1,0:T(8,128)S(1)}, u32[]{:S(2)}, u32[]{:S(2)}) collective-permute-start(f32[1,16,768]{2,1,0:T(8,128)S(1)} %slice_bitcast_fusion.1), channel_id=1, source_target_pairs={{0,8},{8,0},{16,24},{24,16},{32,40},{40,32},{48,56},{56,48},{64,72... | collective-permute-start | bytes 147464 | tf_op jit(solution)/shard_map/ppermute | solution.py:269
  79.2 18.1 %copy-start = (f32[2,2,16,768]{3,2,1,0:T(8,128)}, f32[2,2,16,768]{3,2,1,0:T(8,128)S(1)}, u32[]{:S(2)}) copy-start(f32[2,2,16,768]{3,2,1,0:T(8,128)S(1)} %shard_map.73.refs_0_) | copy-start | bytes 589828
  79.5 3.5 %collective-permute-start.19 = (f32[16,192]{1,0:T(8,128)S(1)}, f32[16,192]{1,0:T(8,128)S(1)}, u32[]{:S(2)}, u32[]{:S(2)}) collective-permute-start(f32[16,192]{1,0:T(8,128)S(1)} %fusion.39), channel_id=1, source_target_pairs={{0,8},{8,0},{16,24},{24,16},{32,40},{40,32},{48,56},{56,48},{64,72... | collective-permute-start | bytes 36872 | tf_op jit(solution)/shard_map/ppermute | solution.py:269
  83.3 5.3 %collective-permute-start.21 = (f32[16,768]{1,0:T(8,128)S(1)}, f32[16,768]{1,0:T(8,128)S(1)}, u32[]{:S(2)}, u32[]{:S(2)}) collective-permute-start(f32[16,768]{1,0:T(8,128)S(1)} %bitcast_subtract_fusion), channel_id=1, source_target_pairs={{0,16},{8,24},{16,0},{24,8},{32,48},{40,56},{48,32},{56,40},{64,80... | collective-permute-start | bytes 147464 | tf_op jit(solution)/shard_map/ppermute | solution.py:274
  85.2 12.1 %collective-permute-start.18 = (f32[2,16,768]{2,1,0:T(8,128)S(1)}, f32[2,16,768]{2,1,0:T(8,128)S(1)}, u32[]{:S(2)}, u32[]{:S(2)}) collective-permute-start(f32[2,16,768]{2,1,0:T(8,128)S(1)} %slice_bitcast_fusion), channel_id=1, source_target_pairs={{0,8},{8,0},{16,24},{24,16},{32,40},{40,32},{48,56},{56,48},{64,72... | collective-permute-start | bytes 294920 | tf_op jit(solution)/shard_map/ppermute | solution.py:269
  88.6 8.7 %copy-start.2 = (f32[16,2048]{1,0:T(8,128)}, f32[16,2048]{1,0:T(8,128)S(1)}, u32[]{:S(2)}) copy-start(f32[16,2048]{1,0:T(8,128)S(1)} %shard_map.74.first_ref) | copy-start | bytes 393220
  88.6 5.5 %collective-permute-start.23 = (f32[16,768]{1,0:T(8,128)S(1)}, f32[16,768]{1,0:T(8,128)S(1)}, u32[]{:S(2)}, u32[]{:S(2)}) collective-permute-start(f32[16,768]{1,0:T(8,128)S(1)} %add.116), channel_id=1, source_target_pairs={{0,64},{8,72},{16,80},{24,88},{32,96},{40,104},{48,112},{56,120},{... | collective-permute-start | bytes 147464 | tf_op jit(solution)/shard_map/ppermute | solution.py:277
  91.2 4.2 %collective-permute-start.24 = (f32[16,768]{1,0:T(8,128)S(1)}, f32[16,768]{1,0:T(8,128)S(1)}, u32[]{:S(2)}, u32[]{:S(2)}) collective-permute-start(f32[16,768]{1,0:T(8,128)S(1)} %add.116), channel_id=1, source_target_pairs={{0,32},{8,40},{16,48},{24,56},{32,64},{40,72},{48,80},{56,88},{64,... | collective-permute-start | bytes 147464 | tf_op jit(solution)/shard_map/ppermute | solution.py:277
  91.2 4.2 %collective-permute-start.22 = (f32[16,768]{1,0:T(8,128)S(1)}, f32[16,768]{1,0:T(8,128)S(1)}, u32[]{:S(2)}, u32[]{:S(2)}) collective-permute-start(f32[16,768]{1,0:T(8,128)S(1)} %add.116), channel_id=1, source_target_pairs={{0,96},{8,104},{16,112},{24,120},{32,0},{40,8},{48,16},{56,24},{64... | collective-permute-start | bytes 147464 | tf_op jit(solution)/shard_map/ppermute | solution.py:277
  95.7 2.4 %collective-permute-start.25 = (f32[16,192]{1,0:T(8,128)S(1)}, f32[16,192]{1,0:T(8,128)S(1)}, u32[]{:S(2)}, u32[]{:S(2)}) collective-permute-start(f32[16,192]{1,0:T(8,128)S(1)} %fusion.33), channel_id=1, source_target_pairs={{0,8},{8,0},{16,24},{24,16},{32,40},{40,32},{48,56},{56,48},{64,72... | collective-permute-start | bytes 36872 | tf_op jit(solution)/shard_map/ppermute | solution.py:269
  98.4 3.5 %collective-permute-start.26 = (f32[16,768]{1,0:T(8,128)S(1)}, f32[16,768]{1,0:T(8,128)S(1)}, u32[]{:S(2)}, u32[]{:S(2)}) collective-permute-start(f32[16,768]{1,0:T(8,128)S(1)} %fusion.59), channel_id=1, source_target_pairs={{0,16},{8,24},{16,0},{24,8},{32,48},{40,56},{48,32},{56,40},{64,80... | collective-permute-start | bytes 147464 | tf_op jit(solution)/shard_map/ppermute | solution.py:274
  99.1 6.7 %copy-start.5 = (f32[6,192,768]{2,1,0:T(8,128)S(1)}, f32[6,192,768]{2,1,0:T(8,128)}, u32[]{:S(2)}) copy-start(f32[6,192,768]{2,1,0:T(8,128)} %shard_map.68) | copy-start | bytes 10616836
  101.8 11.7 %copy-start.3 = (f32[2,1,16,768]{3,2,1,0:T(8,128)}, f32[2,1,16,768]{3,2,1,0:T(8,128)S(1)}, u32[]{:S(2)}) copy-start(f32[2,1,16,768]{3,2,1,0:T(8,128)S(1)} %shard_map.75.refs_2_) | copy-start | bytes 294916
  101.8 4.5 %collective-permute-start.28 = (f32[16,768]{1,0:T(8,128)S(1)}, f32[16,768]{1,0:T(8,128)S(1)}, u32[]{:S(2)}, u32[]{:S(2)}) collective-permute-start(f32[16,768]{1,0:T(8,128)S(1)} %add.121), channel_id=1, source_target_pairs={{0,64},{8,72},{16,80},{24,88},{32,96},{40,104},{48,112},{56,120},{... | collective-permute-start | bytes 147464 | tf_op jit(solution)/shard_map/ppermute | solution.py:277
  103.1 4.2 %collective-permute-start.29 = (f32[16,768]{1,0:T(8,128)S(1)}, f32[16,768]{1,0:T(8,128)S(1)}, u32[]{:S(2)}, u32[]{:S(2)}) collective-permute-start(f32[16,768]{1,0:T(8,128)S(1)} %add.121), channel_id=1, source_target_pairs={{0,32},{8,40},{16,48},{24,56},{32,64},{40,72},{48,80},{56,88},{64,... | collective-permute-start | bytes 147464 | tf_op jit(solution)/shard_map/ppermute | solution.py:277
  105.5 3.8 %collective-permute-start.27 = (f32[16,768]{1,0:T(8,128)S(1)}, f32[16,768]{1,0:T(8,128)S(1)}, u32[]{:S(2)}, u32[]{:S(2)}) collective-permute-start(f32[16,768]{1,0:T(8,128)S(1)} %add.121), channel_id=1, source_target_pairs={{0,96},{8,104},{16,112},{24,120},{32,0},{40,8},{48,16},{56,24},{64... | collective-permute-start | bytes 147464 | tf_op jit(solution)/shard_map/ppermute | solution.py:277
  109.5 2.8 %collective-permute-start.30 = (f32[16,192]{1,0:T(8,128)S(1)}, f32[16,192]{1,0:T(8,128)S(1)}, u32[]{:S(2)}, u32[]{:S(2)}) collective-permute-start(f32[16,192]{1,0:T(8,128)S(1)} %fusion.25), channel_id=1, source_target_pairs={{0,8},{8,0},{16,24},{24,16},{32,40},{40,32},{48,56},{56,48},{64,72... | collective-permute-start | bytes 36872 | tf_op jit(solution)/shard_map/ppermute | solution.py:269
  112.6 3.0 %collective-permute-start.31 = (f32[16,768]{1,0:T(8,128)S(1)}, f32[16,768]{1,0:T(8,128)S(1)}, u32[]{:S(2)}, u32[]{:S(2)}) collective-permute-start(f32[16,768]{1,0:T(8,128)S(1)} %fusion.63), channel_id=1, source_target_pairs={{0,16},{8,24},{16,0},{24,8},{32,48},{40,56},{48,32},{56,40},{64,80... | collective-permute-start | bytes 147464 | tf_op jit(solution)/shard_map/ppermute | solution.py:274
  115.6 4.6 %collective-permute-start.33 = (f32[16,768]{1,0:T(8,128)S(1)}, f32[16,768]{1,0:T(8,128)S(1)}, u32[]{:S(2)}, u32[]{:S(2)}) collective-permute-start(f32[16,768]{1,0:T(8,128)S(1)} %add.126), channel_id=1, source_target_pairs={{0,64},{8,72},{16,80},{24,88},{32,96},{40,104},{48,112},{56,120},{... | collective-permute-start | bytes 147464 | tf_op jit(solution)/shard_map/ppermute | solution.py:277
  116.1 4.6 %collective-permute-start.34 = (f32[16,768]{1,0:T(8,128)S(1)}, f32[16,768]{1,0:T(8,128)S(1)}, u32[]{:S(2)}, u32[]{:S(2)}) collective-permute-start(f32[16,768]{1,0:T(8,128)S(1)} %add.126), channel_id=1, source_target_pairs={{0,32},{8,40},{16,48},{24,56},{32,64},{40,72},{48,80},{56,88},{64,... | collective-permute-start | bytes 147464 | tf_op jit(solution)/shard_map/ppermute | solution.py:277
  117.8 3.1 %collective-permute-start.32 = (f32[16,768]{1,0:T(8,128)S(1)}, f32[16,768]{1,0:T(8,128)S(1)}, u32[]{:S(2)}, u32[]{:S(2)}) collective-permute-start(f32[16,768]{1,0:T(8,128)S(1)} %add.126), channel_id=1, source_target_pairs={{0,96},{8,104},{16,112},{24,120},{32,0},{40,8},{48,16},{56,24},{64... | collective-permute-start | bytes 147464 | tf_op jit(solution)/shard_map/ppermute | solution.py:277
  121.2 4.0 %collective-permute-start.35 = (f32[16,192]{1,0:T(8,128)S(1)}, f32[16,192]{1,0:T(8,128)S(1)}, u32[]{:S(2)}, u32[]{:S(2)}) collective-permute-start(f32[16,192]{1,0:T(8,128)S(1)} %fusion.21), channel_id=1, source_target_pairs={{0,8},{8,0},{16,24},{24,16},{32,40},{40,32},{48,56},{56,48},{64,72... | collective-permute-start | bytes 36872 | tf_op jit(solution)/shard_map/ppermute | solution.py:269
